TPU v7x, 32 devices: a whole 2x2x4 slice. The times are simulated.
32 devices in a mesh: gx: 4 (over y, x), gy: 4 (over z), gz: 2 (over core).
Axes of the slice: x: 2, y: 2, z: 4, core: 2. Of those that a mesh axis runs over, the one named last changes fastest.
Arguments:
- velocity: float32 [3, 128, 128, 256], P(None, 'gx', 'gy', 'gz'), may hold values from -1100 to 1100
- view_sign: int32 [8], replicated, may hold values from 0 to 1
- transfer: float32 [8, 4, 128], replicated, may hold values from 0 to 1
Outputs:
- image: float32 [8, 4, 128, 256], P(None, None, 'gy', 'gz')
All inputs are finite; a program needn't handle non-finite values.
Results may differ from a plain program's by a relative error of at most 0.0003.
Values sent between devices are 32-bit elements; how exact they have to be, the bound alone decides.
No kernel may reach another device: no remote copies, remote signals or barrier semaphores. Data moves between devices by JAX's collectives and lax.ppermute only.
A program may use at most 64 MiB of HBM per device.

v0:
```python
import math

import jax
import jax.numpy as jnp
from jax import lax
from jax.sharding import PartitionSpec as P


def from_partner(shard, axis, bit):
    return lax.ppermute(shard, axis, [(i, i ^ 1 << bit) for i in range(lax.axis_size(axis))])


def extended(block, sides, width):
    for axis, dim in sides:
        count = lax.axis_size(axis)
        forward = [(i, i + 1) for i in range(count - 1)]
        backward = [(target, source) for source, target in forward]
        low = lax.ppermute(
            lax.slice_in_dim(block, block.shape[dim] - width, None, axis=dim), axis, forward
        )
        high = lax.ppermute(lax.slice_in_dim(block, 0, width, axis=dim), axis, backward)
        block = jnp.concatenate([low, block, high], axis=dim)
    return block


def q_criterion(padded):
    grad_x = (padded[:, 2:, 1:-1, 1:-1] - padded[:, :-2, 1:-1, 1:-1]) * 0.5
    grad_y = (padded[:, 1:-1, 2:, 1:-1] - padded[:, 1:-1, :-2, 1:-1]) * 0.5
    grad_z = (padded[:, 1:-1, 1:-1, 2:] - padded[:, 1:-1, 1:-1, :-2]) * 0.5
    gradients = (grad_x, grad_y, grad_z)
    summed = jnp.zeros(grad_x.shape[1:], jnp.float32)
    for outer in range(3):
        for inner in range(3):
            summed = summed + gradients[inner][outer] * gradients[outer][inner]
    return -0.5 * summed


def over(front_tile, back_tile):
    return front_tile + (1.0 - front_tile[:, 3:4]) * back_tile


def march(bin_coord, colour_table, ascending, depth_total):
    depth_cells, pixel_count = bin_coord.shape
    view_count = colour_table.shape[0] // 4
    bin_count = colour_table.shape[1]
    block_width = math.gcd(pixel_count, max(128, 16384 // depth_cells))
    block_count = pixel_count // block_width
    blocks = bin_coord.reshape(depth_cells, block_count, block_width).transpose(1, 0, 2)
    bin_levels = jnp.arange(bin_count, dtype=jnp.float32)[:, None]

    def render_block(pixel_block):
        hat_weights = jnp.maximum(0.0, 1.0 - jnp.abs(pixel_block.reshape(1, -1) - bin_levels))
        looked = jnp.dot(
            colour_table,
            hat_weights,
            precision=lax.Precision.HIGHEST,
            preferred_element_type=jnp.float32,
        )
        looked = looked.reshape(view_count, 4, depth_cells, block_width)
        optical = 3.0 * looked[:, 3] / depth_total
        colour = looked[:, 0:3]
        before = jnp.cumsum(optical, axis=1) - optical
        through = jnp.sum(optical, axis=1, keepdims=True)
        behind = through - before - optical
        absorbed = 1.0 - jnp.exp(-optical)
        weight = jnp.where(ascending[:, None, None], jnp.exp(-before), jnp.exp(-behind)) * absorbed
        tinted = jnp.sum(weight[:, None] * colour, axis=2)
        opacity = 1.0 - jnp.exp(-through)
        return jnp.concatenate([tinted, opacity], axis=1)

    rendered = lax.map(render_block, blocks)
    return rendered.transpose(1, 2, 0, 3).reshape(view_count, 4, pixel_count)


def binary_swap(image_tile, ascending):
    view_count, _, tile_rows, tile_cols = image_tile.shape
    depth_groups = lax.axis_size("gx")
    levels = depth_groups.bit_length() - 1
    my_index = lax.axis_index("gx")
    tile_piece = image_tile.reshape(
        (view_count, 4, tile_rows) + (2,) * levels + (tile_cols // depth_groups,)
    )
    for round_bit in range(levels):
        split_axis = 3 + levels - 1 - round_bit
        my_bit = jnp.right_shift(my_index, round_bit) & 1
        lower_half = lax.index_in_dim(tile_piece, 0, split_axis, keepdims=False)
        upper_half = lax.index_in_dim(tile_piece, 1, split_axis, keepdims=False)
        mine_lower = my_bit == 0
        kept_half = jnp.where(mine_lower, lower_half, upper_half)
        sent_half = jnp.where(mine_lower, upper_half, lower_half)
        partner_half = from_partner(sent_half, "gx", round_bit)
        front_mine = (ascending == mine_lower).reshape((view_count,) + (1,) * (kept_half.ndim - 1))
        tile_piece = jnp.where(
            front_mine, over(kept_half, partner_half), over(partner_half, kept_half)
        )
    return tile_piece


def on_device(velocity, view_sign, transfer):
    _, depth_cells, tile_rows, tile_cols = velocity.shape
    view_count, _, bin_count = transfer.shape
    depth_groups = lax.axis_size("gx")
    cell_count = (
        depth_cells
        * tile_rows
        * tile_cols
        * depth_groups
        * lax.axis_size("gy")
        * lax.axis_size("gz")
    )
    squares = jnp.sum(velocity * velocity)
    summed = lax.psum(squares, ("gx", "gy", "gz"))
    energy = summed / cell_count
    padded = extended(velocity, (("gx", 1), ("gy", 2), ("gz", 3)), 1)
    qcrit = q_criterion(padded)
    bin_coord = (bin_count - 1) * jax.nn.sigmoid(2.0 * qcrit / (energy + 1e-06))
    colour_table = transfer.reshape(view_count * 4, bin_count)
    ascending = view_sign == 0
    depth_total = depth_cells * depth_groups
    rendered = march(
        bin_coord.reshape(depth_cells, tile_rows * tile_cols), colour_table, ascending, depth_total
    )
    tile_piece = binary_swap(rendered.reshape(view_count, 4, tile_rows, tile_cols), ascending)
    return lax.all_gather(tile_piece, "gx", axis=3, tiled=True)


def solution(mesh):
    in_specs = (P(None, "gx", "gy", "gz"), P(), P())
    out_specs = P(None, None, "gy", "gz")
    return jax.shard_map(
        on_device, mesh=mesh, in_specs=in_specs, out_specs=out_specs, check_vma=False
    )
```

profile of v0, /device:TPU:0, one launch (start us, length us, event | category | flops | bytes accessed | tf_op | source)
XLA Modules:
  0.0 240.2 jit_solution(7340408007879587176)
XLA Ops:
  0.8 4.9 %collective-permute-start.1 = (f32[3,1,32,128]{3,2,1,0:T(8,128)S(1)}, f32[3,1,32,128]{3,2,1,0:T(8,128)S(1)}, u32[]{:S(2)}, u32[]{:S(2)}) collective-permute-start(f32[3,1,32,128]{3,2,1,0:T(8,128)S(1)} %get-tuple-element.149), channel_id=1, source_target_pairs={{0,8},{8,16},{16,24},{1,9},{9,17},{17,25},{2,10},{10,18},{18,26},{... | collective-permute-start | bytes 147464 | tf_op jit(solution)/shard_map/ppermute | solution.py:18
  7.4 4.2 %collective-permute-done = f32[3,1,32,128]{3,2,1,0:T(8,128)S(1)} collective-permute-done((f32[3,1,32,128]{3,2,1,0:T(8,128)S(1)}, f32[3,1,32,128]{3,2,1,0:T(8,128)S(1)}, u32[]{:S(2)}, u32[]{:S(2)}) %collective-permute-start) | collective-permute-done | bytes 49184 | tf_op jit(solution)/shard_map/ppermute | solution.py:21
  11.7 5.0 %multiply_reduce_fusion = (f32[]{:T(128)}, f32[3,32,32,128]{3,2,1,0:T(8,128)}, f32[3,34,32,128]{3,2,1,0:T(8,128)S(1)}) fusion(f32[3,32,32,128]{3,2,1,0:T(8,128)} %param.5, f32[3,1,32,128]{3,2,1,0:T(8,128)S(1)} %collective-permute-done.1, f32[3,1,32,128]{3,2,1,0:T(8,128)S(1)} %collective-permute-done, ...), kind=kLoop, calls=%fused_computation.41 | loop fusion | flops 2359295 | bytes 4816900 | tf_op jit(solution)/shard_map/reduce_sum | solution.py:111
  18.1 4.5 %collective-permute-start.3 = (f32[3,34,1,128]{3,1,2,0:T(8,128)S(1)}, f32[3,34,1,128]{3,1,2,0:T(8,128)S(1)}, u32[]{:S(2)}, u32[]{:S(2)}) collective-permute-start(f32[3,34,1,128]{3,1,2,0:T(8,128)S(1)} %copy.127), channel_id=1, source_target_pairs={{0,2},{2,4},{4,6},{1,3},{3,5},{5,7},{8,10},{10,12},{12,14},{9,11},... | collective-permute-start | bytes 156680 | tf_op jit(solution)/shard_map/ppermute | solution.py:18
  22.9 1.5 collective-permute-done.3
  24.9 2.0 fusion.28
  26.9 2.5 %copy.108 = f32[3,34,34,1]{2,1,3,0:T(8,128)S(1)} copy(f32[3,34,34,1]{3,2,1,0:T(8,128)} %get-tuple-element.133) | data formatting | bytes 27744 | tf_op jit(solution)/shard_map/slice | solution.py:21
  29.4 1.4 collective-permute-start.4
  31.8 3.0 %collective-permute-start.5 = (f32[3,34,34,1]{2,1,3,0:T(8,128)S(1)}, f32[3,34,34,1]{2,1,3,0:T(8,128)S(1)}, u32[]{:S(2)}, u32[]{:S(2)}) collective-permute-start(f32[3,34,34,1]{2,1,3,0:T(8,128)S(1)} %copy.110), channel_id=1, source_target_pairs={{0,1},{2,3},{4,5},{6,7},{8,9},{10,11},{12,13},{14,15},{16,17},{18,... | collective-permute-start | bytes 41624 | tf_op jit(solution)/shard_map/ppermute | solution.py:18
  34.9 40.9 %psum.7 = f32[]{:T(128)} all-reduce(f32[]{:T(128)} %get-tuple-element.139), channel_id=1, replica_groups=mesh['gx'=4,'gy'=4,'gz'=2] {'gx','gy','gz'}, use_global_device_ids=true, to_apply=%region_1.0 | all-reduce | flops 1 | bytes 8 | tf_op jit(solution)/shard_map/psum | solution.py:112
  77.2 2.2 copy.111
  79.4 5.7 %fusion.20 = (f32[3,32,32,128]{3,2,1,0:T(8,128)S(1)}, f32[3,32,32,128]{3,2,1,0:T(8,128)S(1)}) fusion(f32[3,34,32,128]{3,2,1,0:T(8,128)} %copy-done, f32[3,34,1,128]{3,2,1,0:T(1,128)S(1)} %copy.105, f32[3,34,1,128]{3,2,1,0:T(1,128)S(1)} %copy.103, f32[3,34,34,1]{3,2,1,0:T(8,128)} %copy.111, f32[3,34,34,1]{3,2,1,0:T(8,128)S(1)} %copy.109), kind=kLoop, calls=%fused_computation.35 | loop fusion | flops 4718592 | bytes 4949088 | tf_op jit(solution)/shard_map/mul | solution.py:28
  85.1 1.4 slice_multiply_fusion.6
  89.2 82.0 %while.13 = (s32[]{:T(128)}, f32[8,8,4,512]{3,2,1,0:T(4,128)}, pred[8]{0:T(512)(128)(4,1)S(1)}, f32[8,32,512]{2,0,1:T(8,128)}, f32[32,128]{1,0:T(8,128)S(1)}, /*index=5*/s32[]{:T(128)}) while((s32[]{:T(128)}, f32[8,8,4,512]{3,2,1,0:T(4,128)}, pred[8]{0:T(512)(128)(4,1)S(1)}, f32[8,32,512]{2,0,1:T(8,128)}, f32[32,128]{1,0:T(8,128)S(1)}, ...), condition=%wide.region_6.7_spmd.clone, body=%wide.region_2.6_spmd.clone.sunk | while | flops 820256768 | bytes 12550737 | solution.py:71
  90.3 5.8 %fusion.41 = f32[16384,32]{0,1:T(8,128)S(1)} fusion(f32[32,128]{1,0:T(8,128)S(1)} %get-tuple-element.203, f32[16384]{0:T(1024)S(1)} %bitcast.71), kind=kOutput, calls=%fused_computation.5.clone.1 | convolution fusion | flops 813694976 | bytes 2179072 | tf_op jit(solution)/shard_map/while/body/eval_jaxpr/dot_general | solution.py:53
  100.6 5.8 %fusion.41 = f32[16384,32]{0,1:T(8,128)S(1)} fusion(f32[32,128]{1,0:T(8,128)S(1)} %get-tuple-element.203, f32[16384]{0:T(1024)S(1)} %bitcast.71), kind=kOutput, calls=%fused_computation.5.clone.1 | convolution fusion | flops 813694976 | bytes 2179072 | tf_op jit(solution)/shard_map/while/body/eval_jaxpr/dot_general | solution.py:53
  110.8 5.8 %fusion.41 = f32[16384,32]{0,1:T(8,128)S(1)} fusion(f32[32,128]{1,0:T(8,128)S(1)} %get-tuple-element.203, f32[16384]{0:T(1024)S(1)} %bitcast.71), kind=kOutput, calls=%fused_computation.5.clone.1 | convolution fusion | flops 813694976 | bytes 2179072 | tf_op jit(solution)/shard_map/while/body/eval_jaxpr/dot_general | solution.py:53
  121.1 5.8 %fusion.41 = f32[16384,32]{0,1:T(8,128)S(1)} fusion(f32[32,128]{1,0:T(8,128)S(1)} %get-tuple-element.203, f32[16384]{0:T(1024)S(1)} %bitcast.71), kind=kOutput, calls=%fused_computation.5.clone.1 | convolution fusion | flops 813694976 | bytes 2179072 | tf_op jit(solution)/shard_map/while/body/eval_jaxpr/dot_general | solution.py:53
  131.3 5.8 %fusion.41 = f32[16384,32]{0,1:T(8,128)S(1)} fusion(f32[32,128]{1,0:T(8,128)S(1)} %get-tuple-element.203, f32[16384]{0:T(1024)S(1)} %bitcast.71), kind=kOutput, calls=%fused_computation.5.clone.1 | convolution fusion | flops 813694976 | bytes 2179072 | tf_op jit(solution)/shard_map/while/body/eval_jaxpr/dot_general | solution.py:53
  141.6 5.8 %fusion.41 = f32[16384,32]{0,1:T(8,128)S(1)} fusion(f32[32,128]{1,0:T(8,128)S(1)} %get-tuple-element.203, f32[16384]{0:T(1024)S(1)} %bitcast.71), kind=kOutput, calls=%fused_computation.5.clone.1 | convolution fusion | flops 813694976 | bytes 2179072 | tf_op jit(solution)/shard_map/while/body/eval_jaxpr/dot_general | solution.py:53
  151.8 5.8 %fusion.41 = f32[16384,32]{0,1:T(8,128)S(1)} fusion(f32[32,128]{1,0:T(8,128)S(1)} %get-tuple-element.203, f32[16384]{0:T(1024)S(1)} %bitcast.71), kind=kOutput, calls=%fused_computation.5.clone.1 | convolution fusion | flops 813694976 | bytes 2179072 | tf_op jit(solution)/shard_map/while/body/eval_jaxpr/dot_general | solution.py:53
  162.1 5.8 %fusion.41 = f32[16384,32]{0,1:T(8,128)S(1)} fusion(f32[32,128]{1,0:T(8,128)S(1)} %get-tuple-element.203, f32[16384]{0:T(1024)S(1)} %bitcast.71), kind=kOutput, calls=%fused_computation.5.clone.1 | convolution fusion | flops 813694976 | bytes 2179072 | tf_op jit(solution)/shard_map/while/body/eval_jaxpr/dot_general | solution.py:53
  171.3 1.3 copy.113
  172.6 1.7 reshape_reshape_reshape.3
  174.3 2.7 %fusion.27 = (f32[8,4,32,2,1,32]{5,4,3,2,1,0:T(1,128)S(1)}, f32[8,4,32,2,1,32]{5,4,3,2,1,0:T(1,128)S(1)}, f32[8,4,32,2,1,32]{5,4,3,2,1,0:T(1,128)S(1)}) fusion(f32[8,4,32,2,2,32]{5,4,3,2,1,0:T(2,128)S(1)} %reshape_reshape_reshape.3, pred[]{:T(512)S(6)} %eq.25), kind=kLoop, calls=%fused_computation.68 | loop fusion | flops 65536 | bytes 1310721 | tf_op jit(solution)/shard_map/slice | solution.py:87
  177.0 2.3 collective-permute-start.6
  180.2 22.2 %collective-permute-done.6 = f32[8,4,32,2,32]{4,3,2,1,0:T(2,128)S(1)} collective-permute-done((f32[8,4,32,2,32]{4,3,2,1,0:T(2,128)S(1)}, f32[8,4,32,2,32]{4,3,2,1,0:T(2,128)S(1)}, u32[]{:S(2)}, u32[]{:S(2)}) %collective-permute-start.6) | collective-permute-done | bytes 262176 | tf_op jit(solution)/shard_map/ppermute | solution.py:10
  202.6 1.4 add_select_fusion
  205.3 1.8 collective-permute-start.7
  207.2 11.1 %collective-permute-done.7 = f32[8,4,32,32]{3,2,1,0:T(8,128)S(1)} collective-permute-done((f32[8,4,32,32]{3,2,1,0:T(8,128)S(1)}, f32[8,4,32,32]{3,2,1,0:T(8,128)S(1)}, u32[]{:S(2)}, u32[]{:S(2)}) %collective-permute-start.7) | collective-permute-done | bytes 131104 | tf_op jit(solution)/shard_map/ppermute | solution.py:10
  219.0 19.1 %all_gather.3 = f32[8,4,32,128]{2,0,1,3:T(8,128)S(1)} all-gather(f32[8,4,32,32]{2,0,1,3:T(8,128)S(1)} %copy.122), channel_id=1, replica_groups=mesh['gx'=4,'gy'=4,'gz'=2] {'gx'}, dimensions={3}, use_global_device_ids=true | all-gather | bytes 655360 | tf_op jit(solution)/shard_map/all_gather | solution.py:124
  238.1 2.1 copy.123
  (123 shorter events, 47.7 us)
Async XLA Ops:
  0.8 6.6 %collective-permute-start.1 = (f32[3,1,32,128]{3,2,1,0:T(8,128)S(1)}, f32[3,1,32,128]{3,2,1,0:T(8,128)S(1)}, u32[]{:S(2)}, u32[]{:S(2)}) collective-permute-start(f32[3,1,32,128]{3,2,1,0:T(8,128)S(1)} %get-tuple-element.149), channel_id=1, source_target_pairs={{0,8},{8,16},{16,24},{1,9},{9,17},{17,25},{2,10},{10,18},{18,26},{... | collective-permute-start | bytes 147464 | tf_op jit(solution)/shard_map/ppermute | solution.py:18
  5.7 6.0 %collective-permute-start = (f32[3,1,32,128]{3,2,1,0:T(8,128)S(1)}, f32[3,1,32,128]{3,2,1,0:T(8,128)S(1)}, u32[]{:S(2)}, u32[]{:S(2)}) collective-permute-start(f32[3,1,32,128]{3,2,1,0:T(8,128)S(1)} %get-tuple-element.148), channel_id=1, source_target_pairs={{8,0},{16,8},{24,16},{9,1},{17,9},{25,17},{10,2},{18,10},{26,18},{... | collective-permute-start | bytes 147464 | tf_op jit(solution)/shard_map/ppermute | solution.py:21
  16.7 7.9 %copy-start = (f32[3,34,32,128]{3,2,1,0:T(8,128)}, f32[3,34,32,128]{3,2,1,0:T(8,128)S(1)}, u32[]{:S(2)}) copy-start(f32[3,34,32,128]{3,2,1,0:T(8,128)S(1)} %constant_dynamic-update-slice_fusion) | copy-start | bytes 5013508
  16.8 6.1 %collective-permute-start.2 = (f32[3,34,1,128]{3,1,2,0:T(8,128)S(1)}, f32[3,34,1,128]{3,1,2,0:T(8,128)S(1)}, u32[]{:S(2)}, u32[]{:S(2)}) collective-permute-start(f32[3,34,1,128]{3,1,2,0:T(8,128)S(1)} %copy.126), channel_id=1, source_target_pairs={{2,0},{4,2},{6,4},{3,1},{5,3},{7,5},{10,8},{12,10},{14,12},{11,9},... | collective-permute-start | bytes 156680 | tf_op jit(solution)/shard_map/ppermute | solution.py:21
  18.1 6.4 %collective-permute-start.3 = (f32[3,34,1,128]{3,1,2,0:T(8,128)S(1)}, f32[3,34,1,128]{3,1,2,0:T(8,128)S(1)}, u32[]{:S(2)}, u32[]{:S(2)}) collective-permute-start(f32[3,34,1,128]{3,1,2,0:T(8,128)S(1)} %copy.127), channel_id=1, source_target_pairs={{0,2},{2,4},{4,6},{1,3},{3,5},{5,7},{8,10},{10,12},{12,14},{9,11},... | collective-permute-start | bytes 156680 | tf_op jit(solution)/shard_map/ppermute | solution.py:18
  29.4 5.4 %copy-start.2 = (s32[8]{0:T(128)S(1)}, s32[8]{0:T(128)}, u32[]{:S(2)}) copy-start(s32[8]{0:T(128)} %param.6) | copy-start | bytes 100
  29.4 46.9 %collective-permute-start.4 = (f32[3,34,34,1]{2,1,3,0:T(8,128)S(1)}, f32[3,34,34,1]{2,1,3,0:T(8,128)S(1)}, u32[]{:S(2)}, u32[]{:S(2)}) collective-permute-start(f32[3,34,34,1]{2,1,3,0:T(8,128)S(1)} %copy.108), channel_id=1, source_target_pairs={{1,0},{3,2},{5,4},{7,6},{9,8},{11,10},{13,12},{15,14},{17,16},{19,... | collective-permute-start | bytes 41624 | tf_op jit(solution)/shard_map/ppermute | solution.py:21
  31.8 45.4 %collective-permute-start.5 = (f32[3,34,34,1]{2,1,3,0:T(8,128)S(1)}, f32[3,34,34,1]{2,1,3,0:T(8,128)S(1)}, u32[]{:S(2)}, u32[]{:S(2)}) collective-permute-start(f32[3,34,34,1]{2,1,3,0:T(8,128)S(1)} %copy.110), channel_id=1, source_target_pairs={{0,1},{2,3},{4,5},{6,7},{8,9},{10,11},{12,13},{14,15},{16,17},{18,... | collective-permute-start | bytes 41624 | tf_op jit(solution)/shard_map/ppermute | solution.py:18
  79.4 5.7 %copy-start.1 = (f32[3,32,32,128]{3,2,1,0:T(8,128)S(1)}, f32[3,32,32,128]{3,2,1,0:T(8,128)}, u32[]{:S(2)}) copy-start(f32[3,32,32,128]{3,2,1,0:T(8,128)} %get-tuple-element.140) | copy-start | bytes 4718596
  88.0 1.2 copy-start.3
  177.0 25.4 %collective-permute-start.6 = (f32[8,4,32,2,32]{4,3,2,1,0:T(2,128)S(1)}, f32[8,4,32,2,32]{4,3,2,1,0:T(2,128)S(1)}, u32[]{:S(2)}, u32[]{:S(2)}) collective-permute-start(f32[8,4,32,2,32]{4,3,2,1,0:T(2,128)S(1)} %bitcast.72), channel_id=1, source_target_pairs={{0,8},{8,0},{16,24},{24,16},{1,9},{9,1},{17,25},{25,17},{2,10},{10... | collective-permute-start | bytes 786440 | tf_op jit(solution)/shard_map/ppermute | solution.py:10
  205.3 13.1 %collective-permute-start.7 = (f32[8,4,32,32]{3,2,1,0:T(8,128)S(1)}, f32[8,4,32,32]{3,2,1,0:T(8,128)S(1)}, u32[]{:S(2)}, u32[]{:S(2)}) collective-permute-start(f32[8,4,32,32]{3,2,1,0:T(8,128)S(1)} %bitcast.74), channel_id=1, source_target_pairs={{0,16},{8,24},{16,0},{24,8},{1,17},{9,25},{17,1},{25,9},{2,18},{10... | collective-permute-start | bytes 393224 | tf_op jit(solution)/shard_map/ppermute | solution.py:10
where the time goes:
time: 241 us; the launch traced here: 240 us
  blocking collectives  60 us (25%)
  matrix products  46.1 us (19%)
  waiting for transfers between devices  39.8 us (17%)
  local copies, waits for them, and re-layouts  38 us (16%)
  other arithmetic  34.4 us (14%)
  starting transfers between devices  20.6 us (9%)
    dot_general x8, matrix products, render_block(): jnp.dot(colour_table, hat_weights, precision=lax.Precision.HIGHEST, prefe...  46.1 us
    psum x1, blocking collectives, on_device(): summed = lax.psum(squares, ('gx', 'gy', 'gz'))  40.9 us
    ppermute x2, waiting for transfers between devices, from_partner(): lax.ppermute(shard, axis, [(i, i ^ 1 << bit) for i in range(lax.axis_size...  33.3 us
    all_gather x1, blocking collectives, on_device(): return lax.all_gather(tile_piece, 'gx', axis=3, tiled=True)  19.1 us
    ppermute x3, starting transfers between devices, extended(): lax.ppermute(lax.slice_in_dim(block, block.shape[dim] - width, None, axis...  12.4 us
    while x8, local copies, waits for them, and re-layouts  9.74 us
    dynamic_slice x8, local copies, waits for them, and re-layouts, march(): rendered = lax.map(render_block, blocks)  8.74 us
    mul x1, other arithmetic, q_criterion(): grad_y = (padded[:, 1:-1, 2:, 1:-1] - padded[:, 1:-1, :-2, 1:-1]) * 0.5  5.65 us
  transfers between devices with their start and end apart: 8, of which 6 were waited for; matrix products, arithmetic and copies ran while one was open for 1% of the time, Pallas kernels for 0%

commit v1 on v0

v1 whole, which is shorter than its diff:
```python
import functools
import math

import jax
import jax.numpy as jnp
from jax import lax
from jax.experimental import pallas as pl
from jax.experimental.pallas import tpu as pltpu
from jax.sharding import PartitionSpec as P

SUB, LANES = 8, 128
AXES = ("gx", "gy", "gz")
ANY = pl.BlockSpec(memory_space=pl.ANY)
VMEM = pl.BlockSpec(memory_space=pltpu.VMEM)
SMEM = pl.BlockSpec(memory_space=pltpu.SMEM)
f32 = jnp.float32


def swap(x, axis, bit_mask):
    n = lax.axis_size(axis)
    return lax.ppermute(x, axis, [(i, i ^ bit_mask) for i in range(n)])


def swap_across(x, axis):
    n = lax.axis_size(axis)
    return lax.ppermute(x, axis, [(i, (i + 1) % n if i % 2 else (i - 1) % n) for i in range(n)])


def flags(sizes):
    out = []
    for axis, n in zip(AXES, sizes):
        i = lax.axis_index(axis)
        out.append((lax.rem(i, 2) == 0, i == 0, i == n - 1))
    return out


def faces_kernel(sizes, v_ref, *outs):
    comps, depth, rows, cols = v_ref.shape
    tiles = rows // SUB
    (ex, _, _), (ey, _, _), (ez, _, _) = flags(sizes)
    outs = list(outs)
    sq_ref = outs.pop()
    groups = depth * tiles // LANES
    lane = lax.broadcasted_iota(jnp.int32, (SUB, LANES), 1)
    zouts = []
    for axis, even, extent in (("x", ex, depth), ("y", ey, rows), ("z", ez, cols)):
        n = sizes["xyz".index(axis)]
        for far in range(0 if n == 1 else 1 if n == 2 else 2):
            out = outs.pop(0)
            at = jnp.where(even, extent - 1, 0)
            if far:
                at = extent - 1 - at
            if axis == "x":
                for c in range(comps):
                    out[c] = v_ref[c, at]
            elif axis == "y":
                for c in range(comps):
                    for x in range(depth):
                        out[c, pl.ds(x, 1), :] = v_ref[c, x, pl.ds(at, 1), :]
            else:
                zouts.append((out, at))
    per = LANES // tiles
    for g in range(groups):

        def body(i, carry):
            squares, picked = carry
            x = g * per + i
            picked = list(picked)
            for c in range(comps):
                for j in range(tiles):
                    tile = v_ref[c, x, pl.ds(j * SUB, SUB), :]
                    squares = squares + tile * tile
                    to = i * tiles + j
                    for o, (_, at) in enumerate(zouts):
                        moved = pltpu.roll(tile, lax.rem(to - at + cols, cols), 1)[:, :LANES]
                        picked[o * comps + c] = jnp.where(lane == to, moved, picked[o * comps + c])
            return squares, tuple(picked)

        zero = jnp.zeros((SUB, LANES), f32)
        squares = zero if g == 0 else sq_ref[...]
        squares, picked = lax.fori_loop(
            0, per, body, (squares, (zero,) * (comps * len(zouts))), unroll=4
        )
        sq_ref[...] = squares
        for o, (out, _) in enumerate(zouts):
            for c in range(comps):
                out[g, c] = picked[o * comps + c]


def q_kernel(sizes, v_hbm, *refs):
    comps, depth, rows, cols = v_hbm.shape
    tiles = rows // SUB
    nx = sizes[0]
    counts = [0 if n == 1 else 1 if n == 2 else 2 for n in sizes]
    halos = [[refs[sum(counts[:a]) + k] for k in range(counts[a])] for a in range(3)]
    refs = refs[sum(counts):]
    outs, (padded, zh, sem) = refs[:nx], refs[nx:]
    info = flags(sizes)
    copy = pltpu.make_async_copy(
        v_hbm, padded.at[:, pl.ds(1, depth), pl.ds(SUB, rows), :], sem.at[0]
    )
    copy.start()

    def both(axis, index):
        even, first, last = info[axis]
        if not halos[axis]:
            return None, None
        near = halos[axis][0][index]
        far = halos[axis][-1][index]
        low = jnp.where(first, 0.0, jnp.where(even, far, near))
        high = jnp.where(last, 0.0, jnp.where(even, near, far))
        return low, high

    for c in range(comps):
        low, high = both(0, c)
        shape = (rows, cols)
        padded[c, 0, pl.ds(SUB, rows), :] = jnp.zeros(shape, f32) if low is None else low
        padded[c, depth + 1, pl.ds(SUB, rows), :] = jnp.zeros(shape, f32) if high is None else high
        low, high = both(1, c)
        zero = jnp.zeros((1, cols), f32)
        for x in range(depth):
            padded[c, 1 + x, pl.ds(SUB - 1, 1), :] = zero if low is None else low[x:x + 1]
            padded[c, 1 + x, pl.ds(SUB + rows, 1), :] = zero if high is None else high[x:x + 1]
    groups = depth * tiles // LANES
    for g in range(groups):
        for c in range(comps):
            low, high = both(2, (g, c))
            zero = jnp.zeros((SUB, LANES), f32)
            zh[0, g, c] = zero if low is None else low
            zh[1, g, c] = zero if high is None else high
    lane = lax.broadcasted_iota(jnp.int32, (SUB, cols), 1)
    me = lax.axis_index("gx")
    piece_tiles = tiles // nx
    per = LANES // tiles
    copy.wait()
    for k in range(nx):
        for p in range(piece_tiles):
            j = jnp.bitwise_xor(me, k) * piece_tiles + p
            base = j * SUB + SUB
            for g in range(groups):
                zlow = [zh[0, g, c] for c in range(comps)]
                zhigh = [zh[1, g, c] for c in range(comps)]

                def body(i, carry):
                    x = g * per + i
                    at = i * tiles + j
                    dx, dy, dz = [], [], []
                    for c in range(comps):
                        here = padded[c, x + 1, pl.ds(pl.multiple_of(base, SUB), SUB), :]
                        dx.append(
                            padded[c, x + 2, pl.ds(pl.multiple_of(base, SUB), SUB), :]
                            - padded[c, x, pl.ds(pl.multiple_of(base, SUB), SUB), :]
                        )
                        dy.append(
                            padded[c, x + 1, pl.ds(base + 1, SUB), :]
                            - padded[c, x + 1, pl.ds(base - 1, SUB), :]
                        )
                        lo = pltpu.roll(zlow[c], lax.rem(cols - at, cols), 1)
                        hi = pltpu.roll(zhigh[c], cols - 1 - at, 1)
                        up = jnp.where(lane == cols - 1, hi, pltpu.roll(here, cols - 1, 1))
                        down = jnp.where(lane == 0, lo, pltpu.roll(here, 1, 1))
                        dz.append(up - down)
                    cross = dy[0] * dx[1] + dz[0] * dx[2] + dz[1] * dy[2]
                    total = dx[0] * dx[0] + dy[1] * dy[1] + dz[2] * dz[2] + (cross + cross)
                    outs[k][x, pl.ds(p * SUB, SUB), :] = total
                    return carry

                lax.fori_loop(0, per, body, 0, unroll=4)


def render_kernel(nx, cell_count, *refs):
    refs = list(refs)
    pieces = [refs.pop(0) for _ in range(nx)]
    sums = [refs.pop(0) for _ in range(nx)]
    sign_ref, table_ref, out_ref, low_ref, frac_ref, tab_ref = refs
    depth, rows, cols = pieces[0].shape
    bins = table_ref.shape[-1]
    views = sign_ref.shape[0]
    depth_total = depth * nx
    me = lax.axis_index("gx")
    squares = sums[0][...]
    for s in sums[1:]:
        squares = squares + s[...]
    energy = jnp.sum(squares, keepdims=True) / cell_count
    scale = -0.25 / (energy + 1e-06)
    scale = jnp.broadcast_to(scale, (SUB, cols))
    for k in range(nx):
        base = jnp.bitwise_xor(me, k) * depth

        def classify(x, carry):
            for p in range(rows // SUB):
                part = pieces[k][x, pl.ds(p * SUB, SUB), :] * scale
                coord = (bins - 1) / (1.0 + jnp.exp(-part))
                low = coord.astype(jnp.int32)
                low_ref[base + x, pl.ds(p * SUB, SUB), :] = low
                frac_ref[base + x, pl.ds(p * SUB, SUB), :] = coord - low.astype(f32)
            return carry

        lax.fori_loop(0, depth, classify, 0, unroll=8)

    table = table_ref[...]
    lane = lax.broadcasted_iota(jnp.int32, table.shape, 1)
    row = lax.broadcasted_iota(jnp.int32, table.shape, 0)
    factor = -3.0 / depth_total * math.log2(math.e)
    table = jnp.where(lax.rem(row, 4) == 3, table * factor, table)
    step = jnp.where(lane == bins - 1, 0.0, pltpu.roll(table, bins - 1, 1) - table)
    tab_ref[0] = table
    tab_ref[1] = step

    for p in range(rows // SUB):

        def view_body(v, carry):
            forward = sign_ref[v] == 0
            start = jnp.where(forward, 0, depth_total - 1)
            stride = jnp.where(forward, 1, -1)
            values = [
                jnp.broadcast_to(tab_ref[0, pl.ds(v * 4 + c, 1), :], (SUB, bins)) for c in range(4)
            ]
            steps = [
                jnp.broadcast_to(tab_ref[1, pl.ds(v * 4 + c, 1), :], (SUB, bins)) for c in range(4)
            ]

            def march(i, state):
                light, total, red, green, blue = state
                x = start + stride * i
                low = low_ref[x, pl.ds(p * SUB, SUB), :]
                frac = frac_ref[x, pl.ds(p * SUB, SUB), :]

                def look(c):
                    pick = functools.partial(
                        jnp.take_along_axis, indices=low, axis=1, mode="promise_in_bounds"
                    )
                    return pick(values[c]) + frac * pick(steps[c])

                exponent = look(3)
                through = jnp.exp2(exponent)
                weight = light * (1.0 - through)
                return (
                    light * through,
                    total + exponent,
                    red + weight * look(0),
                    green + weight * look(1),
                    blue + weight * look(2),
                )

            zero = jnp.zeros((SUB, cols), f32)
            _, total, red, green, blue = lax.fori_loop(
                0, depth_total, march, (jnp.ones((SUB, cols), f32), zero, zero, zero, zero), unroll=8
            )
            for c, value in enumerate((red, green, blue, 1.0 - jnp.exp2(total))):
                out_ref[v, c, pl.ds(p * SUB, SUB), :] = value
            return carry

        lax.fori_loop(0, views, view_body, 0)


def assemble_kernel(nx, *refs):
    pieces, out, sem = refs[:nx], refs[nx], refs[nx + 1]
    rows = pieces[0].shape[2]
    me = lax.axis_index("gx")
    copies = []
    for k in range(nx):
        at = pl.multiple_of(jnp.bitwise_xor(me, k) * rows, SUB)
        copies.append(pltpu.make_async_copy(pieces[k], out.at[:, :, pl.ds(at, rows), :], sem.at[k]))
        copies[-1].start()
    for copy in copies:
        copy.wait()


def on_device(velocity, view_sign, transfer):
    comps, depth, rows, cols = velocity.shape
    views, channels, bins = transfer.shape
    sizes = tuple(lax.axis_size(a) for a in AXES)
    nx = sizes[0]
    assert all(n & (n - 1) == 0 for n in sizes)
    assert cols == LANES and bins == LANES and rows % (SUB * nx) == 0
    assert depth * (rows // SUB) % LANES == 0
    cell_count = depth * rows * cols * math.prod(sizes)
    counts = [0 if n == 1 else 1 if n == 2 else 2 for n in sizes]
    groups = depth * (rows // SUB) // LANES
    face = [(comps, rows, cols), (comps, depth, cols), (groups, comps, SUB, LANES)]
    shapes = [jax.ShapeDtypeStruct(face[a], f32) for a in range(3) for _ in range(counts[a])]
    tile = jax.ShapeDtypeStruct((SUB, LANES), f32)
    *sent, squares = pl.pallas_call(
        functools.partial(faces_kernel, sizes),
        out_shape=shapes + [tile],
        in_specs=[VMEM],
        out_specs=[VMEM] * (len(shapes) + 1),
        name="faces",
    )(velocity)
    kinds = [(AXES[a], far) for a in range(3) for far in range(counts[a])]
    halos = [
        swap_across(x, axis) if far else swap(x, axis, 1) for x, (axis, far) in zip(sent, kinds)
    ]
    part_rows = rows // nx
    piece = jax.ShapeDtypeStruct((depth, part_rows, cols), f32)
    q_pieces = pl.pallas_call(
        functools.partial(q_kernel, sizes),
        out_shape=[piece] * nx,
        in_specs=[ANY] + [VMEM] * len(halos),
        out_specs=[VMEM] * nx,
        scratch_shapes=[
            pltpu.VMEM((comps, depth + 2, rows + 2 * SUB, cols), f32),
            pltpu.VMEM((2, groups, comps, SUB, LANES), f32),
            pltpu.SemaphoreType.DMA((1,)),
        ],
        name="q",
    )(velocity, *halos)
    for axis in ("gz", "gy"):
        for bit in range(lax.axis_size(axis).bit_length() - 1):
            squares = squares + swap(squares, axis, 1 << bit)
    order = sorted(range(1, nx), key=lambda k: -k)
    got = {0: q_pieces[0]}
    for k in order:
        got[k] = swap(q_pieces[k], "gx", k)
    sums = [squares] + [swap(squares, "gx", k) for k in range(1, nx)]
    image_piece = pl.pallas_call(
        functools.partial(render_kernel, nx, cell_count),
        out_shape=jax.ShapeDtypeStruct((views, channels, part_rows, cols), f32),
        in_specs=[VMEM] * (2 * nx) + [SMEM, VMEM],
        out_specs=VMEM,
        scratch_shapes=[
            pltpu.VMEM((depth * nx, part_rows, cols), jnp.int32),
            pltpu.VMEM((depth * nx, part_rows, cols), f32),
            pltpu.VMEM((2, views * channels, bins), f32),
        ],
        name="render",
    )(*[got[k] for k in range(nx)], *sums, view_sign, transfer.reshape(views * channels, bins))
    images = {0: image_piece}
    for k in order:
        images[k] = swap(image_piece, "gx", k)
    return pl.pallas_call(
        functools.partial(assemble_kernel, nx),
        out_shape=jax.ShapeDtypeStruct((views, channels, rows, cols), f32),
        in_specs=[VMEM] * nx,
        out_specs=ANY,
        scratch_shapes=[pltpu.SemaphoreType.DMA((nx,))],
        name="assemble",
    )(*[images[k] for k in range(nx)])


def solution(mesh):
    in_specs = (P(None, "gx", "gy", "gz"), P(), P())
    out_specs = P(None, None, "gy", "gz")
    return jax.shard_map(
        on_device, mesh=mesh, in_specs=in_specs, out_specs=out_specs, check_vma=False
    )
```

time: 241 us -> 79.7 us (0.33)
  blocking collectives: 60 us -> 0 us
  matrix products: 46.1 us -> 0 us
  Pallas kernels: 0 us -> 36.1 us
  local copies, waits for them, and re-layouts: 38 us -> 1.98 us
  other arithmetic: 34.4 us -> 0.01 us
  waiting for transfers between devices: 39.8 us -> 20.1 us
    dot_general x8 -> x0, matrix products: 46.1 us -> none  [render_block(): jnp.dot(colour_table, hat_weights, precision=lax.Precision.HIGHEST, prefe...]
    psum x1 -> x0, blocking collectives: 40.9 us -> none  [on_device(): summed = lax.psum(squares, ('gx', 'gy', 'gz'))]
    pallas_call x0 -> x4, Pallas kernels: none -> 36.1 us  [the longest x1 24.2 us: on_device(): pl.pallas_call(functools.partial(render_kernel, nx, cell_count), out_shap...]
    ppermute x8 -> x17, waiting for transfers between devices: 39.8 us -> 20.1 us  [the longest x15 18 us: swap(): return lax.ppermute(x, axis, [(i, i ^ bit_mask) for i in range(n)])]
    all_gather x1 -> x0, blocking collectives: 19.1 us -> none  [on_device(): return lax.all_gather(tile_piece, 'gx', axis=3, tiled=True)]
    reduce_sum x17 -> x0, other arithmetic: 10.2 us -> none  [the longest x1 4.98 us: on_device(): squares = jnp.sum(velocity * velocity)]
    while x8 -> x0, local copies, waits for them, and re-layouts: 9.74 us -> none
    dynamic_slice x8 -> x0, local copies, waits for them, and re-layouts: 8.74 us -> none  [march(): rendered = lax.map(render_block, blocks)]
  transfers between devices with their start and end apart: 8 -> 17, of which waited for: 6 -> 10; matrix products, arithmetic and copies ran while one was open for 1% -> 0% of each run, Pallas kernels for 0% -> 0%
where the time goes in v1:
time: 79.7 us; the launch traced here: 79.4 us
  Pallas kernels  36.1 us (45%)
  starting transfers between devices  21 us (26%)
  waiting for transfers between devices  20.1 us (25%)
  local copies, waits for them, and re-layouts  1.98 us (2%)
    pallas_call x1, Pallas kernels, on_device(): pl.pallas_call(functools.partial(render_kernel, nx, cell_count), out_shap...  24.2 us
    ppermute x15, waiting for transfers between devices, swap(): return lax.ppermute(x, axis, [(i, i ^ bit_mask) for i in range(n)])  18 us
    ppermute x15, starting transfers between devices, swap(): return lax.ppermute(x, axis, [(i, i ^ bit_mask) for i in range(n)])  17.1 us
    pallas_call x1, Pallas kernels, on_device(): pl.pallas_call(functools.partial(q_kernel, sizes), out_shape=[piece] * nx...  6.92 us
    ppermute x2, starting transfers between devices, swap_across(): lax.ppermute(x, axis, [(i, (i + 1) % n if i % 2 else (i - 1) % n) for i i...  3.97 us
    pallas_call x1, Pallas kernels, on_device(): pl.pallas_call(functools.partial(faces_kernel, sizes), out_shape=shapes +...  3.15 us
    ppermute x2, waiting for transfers between devices, swap_across(): lax.ppermute(x, axis, [(i, (i + 1) % n if i % 2 else (i - 1) % n) for i i...  2.19 us
    unnamed x32, local copies, waits for them, and re-layouts  1.98 us
  transfers between devices with their start and end apart: 17, of which 10 were waited for; matrix products, arithmetic and copies ran while one was open for 0% of the time, Pallas kernels for 0%

profile of v1, /device:TPU:0, one launch (start us, length us, event | category | flops | bytes accessed | tf_op | source)
XLA Modules:
  0.0 79.4 jit_solution(7874792186506378059)
XLA Ops:
  0.0 3.1 %faces.1 = (f32[3,32,128]{2,1,0:T(8,128)}, f32[3,32,128]{2,1,0:T(8,128)}, f32[3,32,128]{2,1,0:T(8,128)}, f32[3,32,128]{2,1,0:T(8,128)}, f32[1,3,8,128]{3,2,1,0:T(8,128)}, /*index=5*/f32[8,128]{1,0:T(8,128)}) custom-call(f32[3,32,32,128]{3,2,1,0:T(8,128)} %v_hbm.1), custom_call_target="tpu_custom_call" | custom-call | tf_op jit(solution)/shard_map/faces/pallas_call | solution.py:284
  3.2 3.0 %collective-permute-start = (f32[3,32,128]{2,1,0:T(8,128)}, f32[3,32,128]{2,1,0:T(8,128)S(1)}, u32[]{:S(2)}, u32[]{:S(2)}) collective-permute-start(f32[3,32,128]{2,1,0:T(8,128)} %get-tuple-element.15), channel_id=1, source_target_pairs={{0,8},{8,0},{16,24},{24,16},{1,9},{9,1},{17,25},{25,17},{2,10},{10... | collective-permute-start | bytes 147464 | tf_op jit(solution)/shard_map/ppermute | solution.py:21
  6.1 1.5 %collective-permute-start.1 = (f32[3,32,128]{2,1,0:T(8,128)}, f32[3,32,128]{2,1,0:T(8,128)S(1)}, u32[]{:S(2)}, u32[]{:S(2)}) collective-permute-start(f32[3,32,128]{2,1,0:T(8,128)} %get-tuple-element.16), channel_id=1, source_target_pairs={{0,24},{8,16},{16,8},{24,0},{1,25},{9,17},{17,9},{25,1},{2,26},{10... | collective-permute-start | bytes 147464 | tf_op jit(solution)/shard_map/ppermute | solution.py:26
  7.6 1.6 %collective-permute-start.2 = (f32[3,32,128]{2,1,0:T(8,128)}, f32[3,32,128]{2,1,0:T(8,128)S(1)}, u32[]{:S(2)}, u32[]{:S(2)}) collective-permute-start(f32[3,32,128]{2,1,0:T(8,128)} %get-tuple-element.17), channel_id=1, source_target_pairs={{0,2},{2,0},{4,6},{6,4},{1,3},{3,1},{5,7},{7,5},{8,10},{10,8},{12,... | collective-permute-start | bytes 147464 | tf_op jit(solution)/shard_map/ppermute | solution.py:21
  9.2 2.5 %collective-permute-start.3 = (f32[3,32,128]{2,1,0:T(8,128)}, f32[3,32,128]{2,1,0:T(8,128)S(1)}, u32[]{:S(2)}, u32[]{:S(2)}) collective-permute-start(f32[3,32,128]{2,1,0:T(8,128)} %get-tuple-element.18), channel_id=1, source_target_pairs={{0,6},{2,4},{4,2},{6,0},{1,7},{3,5},{5,3},{7,1},{8,14},{10,12},{12... | collective-permute-start | bytes 147464 | tf_op jit(solution)/shard_map/ppermute | solution.py:26
  11.7 1.4 %collective-permute-done.4.refs_4_ = f32[1,3,8,128]{3,2,1,0:T(8,128)S(1)} collective-permute-done((f32[1,3,8,128]{3,2,1,0:T(8,128)}, f32[1,3,8,128]{3,2,1,0:T(8,128)S(1)}, u32[]{:S(2)}, u32[]{:S(2)}) %collective-permute-start.4) | collective-permute-done | bytes 12320 | tf_op jit(solution)/shard_map/ppermute | solution.py:21
  13.1 2.2 %collective-permute-done.3.refs_3_ = f32[3,32,128]{2,1,0:T(8,128)S(1)} collective-permute-done((f32[3,32,128]{2,1,0:T(8,128)}, f32[3,32,128]{2,1,0:T(8,128)S(1)}, u32[]{:S(2)}, u32[]{:S(2)}) %collective-permute-start.3) | collective-permute-done | bytes 49184 | tf_op jit(solution)/shard_map/ppermute | solution.py:26
  15.3 0.6 copy-done.9
  15.9 6.9 %q.1 = (f32[32,8,128]{2,1,0:T(8,128)}, f32[32,8,128]{2,1,0:T(8,128)}, f32[32,8,128]{2,1,0:T(8,128)}, f32[32,8,128]{2,1,0:T(8,128)}) custom-call(f32[3,32,32,128]{3,2,1,0:T(8,128)} %v_hbm.1, f32[3,32,128]{2,1,0:T(8,128)} %copy-done.6, f32[3,32,128]{2,1,0:T(8,128)} %copy-done.7, f32[3,32,128]{2,1,0:T(8,128)} %copy-done.8, f32[3,32,128]{2,1,0:T(8,128)} %copy-done.9, ...), custom_call_target="tpu_custom_call" | custom-call | tf_op jit(solution)/shard_map/q/pallas_call | solution.py:297
  22.8 1.6 %collective-permute-start.5 = (f32[32,8,128]{2,1,0:T(8,128)}, f32[32,8,128]{2,1,0:T(8,128)S(1)}, u32[]{:S(2)}, u32[]{:S(2)}) collective-permute-start(f32[32,8,128]{2,1,0:T(8,128)} %get-tuple-element.21), channel_id=1, source_target_pairs={{0,8},{8,0},{16,24},{24,16},{1,9},{9,1},{17,25},{25,17},{2,10},{10... | collective-permute-start | bytes 393224 | tf_op jit(solution)/shard_map/ppermute | solution.py:21
  24.4 0.5 collective-permute-start.6
  24.9 1.5 %collective-permute-start.7 = (f32[32,8,128]{2,1,0:T(8,128)}, f32[32,8,128]{2,1,0:T(8,128)S(1)}, u32[]{:S(2)}, u32[]{:S(2)}) collective-permute-start(f32[32,8,128]{2,1,0:T(8,128)} %get-tuple-element.23), channel_id=1, source_target_pairs={{0,24},{8,16},{16,8},{24,0},{1,25},{9,17},{17,9},{25,1},{2,26},{10... | collective-permute-start | bytes 393224 | tf_op jit(solution)/shard_map/ppermute | solution.py:21
  26.4 1.2 %collective-permute-done.8 = f32[8,128]{1,0:T(8,128)S(1)} collective-permute-done((f32[8,128]{1,0:T(8,128)S(1)}, f32[8,128]{1,0:T(8,128)S(1)}, u32[]{:S(2)}, u32[]{:S(2)}) %collective-permute-start.8) | collective-permute-done | bytes 4128 | tf_op jit(solution)/shard_map/ppermute | solution.py:21
  27.6 3.6 %collective-permute-done.9 = f32[8,128]{1,0:T(8,128)S(1)} collective-permute-done((f32[8,128]{1,0:T(8,128)S(1)}, f32[8,128]{1,0:T(8,128)S(1)}, u32[]{:S(2)}, u32[]{:S(2)}) %collective-permute-start.9) | collective-permute-done | bytes 4128 | tf_op jit(solution)/shard_map/ppermute | solution.py:21
  31.2 1.0 %collective-permute-start.10 = (f32[8,128]{1,0:T(8,128)S(1)}, f32[8,128]{1,0:T(8,128)S(1)}, u32[]{:S(2)}, u32[]{:S(2)}) collective-permute-start(f32[8,128]{1,0:T(8,128)S(1)} %add.10), channel_id=1, source_target_pairs={{0,4},{2,6},{4,0},{6,2},{1,5},{3,7},{5,1},{7,3},{8,12},{10,14},{12... | collective-permute-start | bytes 12296 | tf_op jit(solution)/shard_map/ppermute | solution.py:21
  32.2 3.5 %collective-permute-done.10 = f32[8,128]{1,0:T(8,128)S(1)} collective-permute-done((f32[8,128]{1,0:T(8,128)S(1)}, f32[8,128]{1,0:T(8,128)S(1)}, u32[]{:S(2)}, u32[]{:S(2)}) %collective-permute-start.10) | collective-permute-done | bytes 4128 | tf_op jit(solution)/shard_map/ppermute | solution.py:21
  35.7 1.4 %collective-permute-start.13 = (f32[8,128]{1,0:T(8,128)S(1)}, f32[8,128]{1,0:T(8,128)S(1)}, u32[]{:S(2)}, u32[]{:S(2)}) collective-permute-start(f32[8,128]{1,0:T(8,128)S(1)} %add.11.refs_4_), channel_id=1, source_target_pairs={{0,24},{8,16},{16,8},{24,0},{1,25},{9,17},{17,9},{25,1},{2,26},{10... | collective-permute-start | bytes 12296 | tf_op jit(solution)/shard_map/ppermute | solution.py:21
  37.1 1.5 %collective-permute-start.12 = (f32[8,128]{1,0:T(8,128)S(1)}, f32[8,128]{1,0:T(8,128)S(1)}, u32[]{:S(2)}, u32[]{:S(2)}) collective-permute-start(f32[8,128]{1,0:T(8,128)S(1)} %add.11.refs_4_), channel_id=1, source_target_pairs={{0,16},{8,24},{16,0},{24,8},{1,17},{9,25},{17,1},{25,9},{2,18},{10... | collective-permute-start | bytes 12296 | tf_op jit(solution)/shard_map/ppermute | solution.py:21
  38.7 1.6 %collective-permute-done.13.refs_7_ = f32[8,128]{1,0:T(8,128)S(1)} collective-permute-done((f32[8,128]{1,0:T(8,128)S(1)}, f32[8,128]{1,0:T(8,128)S(1)}, u32[]{:S(2)}, u32[]{:S(2)}) %collective-permute-start.13) | collective-permute-done | bytes 4128 | tf_op jit(solution)/shard_map/ppermute | solution.py:21
  40.2 1.5 %collective-permute-start.11 = (f32[8,128]{1,0:T(8,128)S(1)}, f32[8,128]{1,0:T(8,128)S(1)}, u32[]{:S(2)}, u32[]{:S(2)}) collective-permute-start(f32[8,128]{1,0:T(8,128)S(1)} %add.11.refs_4_), channel_id=1, source_target_pairs={{0,8},{8,0},{16,24},{24,16},{1,9},{9,1},{17,25},{25,17},{2,10},{10... | collective-permute-start | bytes 12296 | tf_op jit(solution)/shard_map/ppermute | solution.py:21
  41.7 2.1 %collective-permute-done.11.refs_5_ = f32[8,128]{1,0:T(8,128)S(1)} collective-permute-done((f32[8,128]{1,0:T(8,128)S(1)}, f32[8,128]{1,0:T(8,128)S(1)}, u32[]{:S(2)}, u32[]{:S(2)}) %collective-permute-start.11) | collective-permute-done | bytes 4128 | tf_op jit(solution)/shard_map/ppermute | solution.py:21
  43.9 0.5 copy-done.14
  44.4 0.1 copy-done
  44.6 24.2 %render.1.refs_0_ = f32[8,4,8,128]{3,2,1,0:T(8,128)} custom-call(f32[32,8,128]{2,1,0:T(8,128)} %get-tuple-element.20.refs_0_, f32[32,8,128]{2,1,0:T(8,128)} %copy-done, f32[32,8,128]{2,1,0:T(8,128)} %copy-done.1, f32[32,8,128]{2,1,0:T(8,128)} %copy-done.2, f32[8,128]{1,0:T(8,128)} %copy-done.10, f32[8,128]{1,0:T(8,128)} %copy-done.14, f32[8,128]{1,0:T(8,128)} %copy-done.13, ...), custom_call_target="tpu_custom_call" | custom-call | tf_op jit(solution)/shard_map/render/pallas_call | solution.py:317
  68.7 1.4 %collective-permute-start.16 = (f32[8,4,8,128]{3,2,1,0:T(8,128)}, f32[8,4,8,128]{3,2,1,0:T(8,128)S(1)}, u32[]{:S(2)}, u32[]{:S(2)}) collective-permute-start(f32[8,4,8,128]{3,2,1,0:T(8,128)} %render.1.refs_0_), channel_id=1, source_target_pairs={{0,24},{8,16},{16,8},{24,0},{1,25},{9,17},{17,9},{25,1},{2,26},{10... | collective-permute-start | bytes 393224 | tf_op jit(solution)/shard_map/ppermute | solution.py:21
  70.2 1.5 %collective-permute-start.15 = (f32[8,4,8,128]{3,2,1,0:T(8,128)}, f32[8,4,8,128]{3,2,1,0:T(8,128)S(1)}, u32[]{:S(2)}, u32[]{:S(2)}) collective-permute-start(f32[8,4,8,128]{3,2,1,0:T(8,128)} %render.1.refs_0_), channel_id=1, source_target_pairs={{0,16},{8,24},{16,0},{24,8},{1,17},{9,25},{17,1},{25,9},{2,18},{10... | collective-permute-start | bytes 393224 | tf_op jit(solution)/shard_map/ppermute | solution.py:21
  71.7 0.5 collective-permute-start.14
  72.2 2.7 %collective-permute-done.16.refs_3_ = f32[8,4,8,128]{3,2,1,0:T(8,128)S(1)} collective-permute-done((f32[8,4,8,128]{3,2,1,0:T(8,128)}, f32[8,4,8,128]{3,2,1,0:T(8,128)S(1)}, u32[]{:S(2)}, u32[]{:S(2)}) %collective-permute-start.16) | collective-permute-done | bytes 131104 | tf_op jit(solution)/shard_map/ppermute | solution.py:21
  74.9 1.3 %collective-permute-done.15.refs_2_ = f32[8,4,8,128]{3,2,1,0:T(8,128)S(1)} collective-permute-done((f32[8,4,8,128]{3,2,1,0:T(8,128)}, f32[8,4,8,128]{3,2,1,0:T(8,128)S(1)}, u32[]{:S(2)}, u32[]{:S(2)}) %collective-permute-start.15) | collective-permute-done | bytes 131104 | tf_op jit(solution)/shard_map/ppermute | solution.py:21
  76.2 0.6 collective-permute-done.14.refs_1_
  76.9 0.6 copy-done.5
  77.5 1.9 %assemble.1 = f32[8,4,32,128]{3,2,1,0:T(8,128)} custom-call(f32[8,4,8,128]{3,2,1,0:T(8,128)} %render.1.refs_0_, f32[8,4,8,128]{3,2,1,0:T(8,128)} %copy-done.5, f32[8,4,8,128]{3,2,1,0:T(8,128)} %copy-done.4, f32[8,4,8,128]{3,2,1,0:T(8,128)} %copy-done.3), custom_call_target="tpu_custom_call" | custom-call | tf_op jit(solution)/shard_map/assemble/pallas_call | solution.py:332
  (41 shorter events, 0.2 us)
Async XLA Ops:
  3.1 23.3 %copy-start.15 = (f32[8,128]{1,0:T(8,128)S(1)}, f32[8,128]{1,0:T(8,128)}, u32[]{:S(2)}) copy-start(f32[8,128]{1,0:T(8,128)} %get-tuple-element.24) | copy-start | bytes 12292
  3.2 9.9 %collective-permute-start = (f32[3,32,128]{2,1,0:T(8,128)}, f32[3,32,128]{2,1,0:T(8,128)S(1)}, u32[]{:S(2)}, u32[]{:S(2)}) collective-permute-start(f32[3,32,128]{2,1,0:T(8,128)} %get-tuple-element.15), channel_id=1, source_target_pairs={{0,8},{8,0},{16,24},{24,16},{1,9},{9,1},{17,25},{25,17},{2,10},{10... | collective-permute-start | bytes 147464 | tf_op jit(solution)/shard_map/ppermute | solution.py:21
  6.1 6.9 %collective-permute-start.1 = (f32[3,32,128]{2,1,0:T(8,128)}, f32[3,32,128]{2,1,0:T(8,128)S(1)}, u32[]{:S(2)}, u32[]{:S(2)}) collective-permute-start(f32[3,32,128]{2,1,0:T(8,128)} %get-tuple-element.16), channel_id=1, source_target_pairs={{0,24},{8,16},{16,8},{24,0},{1,25},{9,17},{17,9},{25,1},{2,26},{10... | collective-permute-start | bytes 147464 | tf_op jit(solution)/shard_map/ppermute | solution.py:26
  7.6 5.5 %collective-permute-start.2 = (f32[3,32,128]{2,1,0:T(8,128)}, f32[3,32,128]{2,1,0:T(8,128)S(1)}, u32[]{:S(2)}, u32[]{:S(2)}) collective-permute-start(f32[3,32,128]{2,1,0:T(8,128)} %get-tuple-element.17), channel_id=1, source_target_pairs={{0,2},{2,0},{4,6},{6,4},{1,3},{3,1},{5,7},{7,5},{8,10},{10,8},{12,... | collective-permute-start | bytes 147464 | tf_op jit(solution)/shard_map/ppermute | solution.py:21
  9.2 6.1 %collective-permute-start.3 = (f32[3,32,128]{2,1,0:T(8,128)}, f32[3,32,128]{2,1,0:T(8,128)S(1)}, u32[]{:S(2)}, u32[]{:S(2)}) collective-permute-start(f32[3,32,128]{2,1,0:T(8,128)} %get-tuple-element.18), channel_id=1, source_target_pairs={{0,6},{2,4},{4,2},{6,0},{1,7},{3,5},{5,3},{7,1},{8,14},{10,12},{12... | collective-permute-start | bytes 147464 | tf_op jit(solution)/shard_map/ppermute | solution.py:26
  11.7 1.4 %collective-permute-start.4 = (f32[1,3,8,128]{3,2,1,0:T(8,128)}, f32[1,3,8,128]{3,2,1,0:T(8,128)S(1)}, u32[]{:S(2)}, u32[]{:S(2)}) collective-permute-start(f32[1,3,8,128]{3,2,1,0:T(8,128)} %get-tuple-element.19), channel_id=1, source_target_pairs={{0,1},{1,0},{2,3},{3,2},{4,5},{5,4},{6,7},{7,6},{8,9},{9,8},{10,11... | collective-permute-start | bytes 36872 | tf_op jit(solution)/shard_map/ppermute | solution.py:21
  13.1 2.2 %copy-start.11 = (f32[1,3,8,128]{3,2,1,0:T(8,128)}, f32[1,3,8,128]{3,2,1,0:T(8,128)S(1)}, u32[]{:S(2)}) copy-start(f32[1,3,8,128]{3,2,1,0:T(8,128)S(1)} %collective-permute-done.4.refs_4_) | copy-start | bytes 36868
  13.1 2.2 %copy-start.6 = (f32[3,32,128]{2,1,0:T(8,128)}, f32[3,32,128]{2,1,0:T(8,128)S(1)}, u32[]{:S(2)}) copy-start(f32[3,32,128]{2,1,0:T(8,128)S(1)} %collective-permute-done.refs_0_) | copy-start | bytes 147460
  13.1 2.2 %copy-start.7 = (f32[3,32,128]{2,1,0:T(8,128)}, f32[3,32,128]{2,1,0:T(8,128)S(1)}, u32[]{:S(2)}) copy-start(f32[3,32,128]{2,1,0:T(8,128)S(1)} %collective-permute-done.1.refs_1_) | copy-start | bytes 147460
  13.1 2.2 %copy-start.8 = (f32[3,32,128]{2,1,0:T(8,128)}, f32[3,32,128]{2,1,0:T(8,128)S(1)}, u32[]{:S(2)}) copy-start(f32[3,32,128]{2,1,0:T(8,128)S(1)} %collective-permute-done.2.refs_2_) | copy-start | bytes 147460
  15.3 0.6 copy-start.9
  22.8 21.0 %collective-permute-start.5 = (f32[32,8,128]{2,1,0:T(8,128)}, f32[32,8,128]{2,1,0:T(8,128)S(1)}, u32[]{:S(2)}, u32[]{:S(2)}) collective-permute-start(f32[32,8,128]{2,1,0:T(8,128)} %get-tuple-element.21), channel_id=1, source_target_pairs={{0,8},{8,0},{16,24},{24,16},{1,9},{9,1},{17,25},{25,17},{2,10},{10... | collective-permute-start | bytes 393224 | tf_op jit(solution)/shard_map/ppermute | solution.py:21
  24.4 19.4 %collective-permute-start.6 = (f32[32,8,128]{2,1,0:T(8,128)}, f32[32,8,128]{2,1,0:T(8,128)S(1)}, u32[]{:S(2)}, u32[]{:S(2)}) collective-permute-start(f32[32,8,128]{2,1,0:T(8,128)} %get-tuple-element.22), channel_id=1, source_target_pairs={{0,16},{8,24},{16,0},{24,8},{1,17},{9,25},{17,1},{25,9},{2,18},{10... | collective-permute-start | bytes 393224 | tf_op jit(solution)/shard_map/ppermute | solution.py:21
  24.9 18.9 %collective-permute-start.7 = (f32[32,8,128]{2,1,0:T(8,128)}, f32[32,8,128]{2,1,0:T(8,128)S(1)}, u32[]{:S(2)}, u32[]{:S(2)}) collective-permute-start(f32[32,8,128]{2,1,0:T(8,128)} %get-tuple-element.23), channel_id=1, source_target_pairs={{0,24},{8,16},{16,8},{24,0},{1,25},{9,17},{17,9},{25,1},{2,26},{10... | collective-permute-start | bytes 393224 | tf_op jit(solution)/shard_map/ppermute | solution.py:21
  26.4 1.2 %collective-permute-start.8 = (f32[8,128]{1,0:T(8,128)S(1)}, f32[8,128]{1,0:T(8,128)S(1)}, u32[]{:S(2)}, u32[]{:S(2)}) collective-permute-start(f32[8,128]{1,0:T(8,128)S(1)} %copy-done.15), channel_id=1, source_target_pairs={{0,1},{1,0},{2,3},{3,2},{4,5},{5,4},{6,7},{7,6},{8,9},{9,8},{10,11... | collective-permute-start | bytes 12296 | tf_op jit(solution)/shard_map/ppermute | solution.py:21
  27.6 3.6 %collective-permute-start.9 = (f32[8,128]{1,0:T(8,128)S(1)}, f32[8,128]{1,0:T(8,128)S(1)}, u32[]{:S(2)}, u32[]{:S(2)}) collective-permute-start(f32[8,128]{1,0:T(8,128)S(1)} %add.9), channel_id=1, source_target_pairs={{0,2},{2,0},{4,6},{6,4},{1,3},{3,1},{5,7},{7,5},{8,10},{10,8},{12,... | collective-permute-start | bytes 12296 | tf_op jit(solution)/shard_map/ppermute | solution.py:21
  31.2 4.5 %collective-permute-start.10 = (f32[8,128]{1,0:T(8,128)S(1)}, f32[8,128]{1,0:T(8,128)S(1)}, u32[]{:S(2)}, u32[]{:S(2)}) collective-permute-start(f32[8,128]{1,0:T(8,128)S(1)} %add.10), channel_id=1, source_target_pairs={{0,4},{2,6},{4,0},{6,2},{1,5},{3,7},{5,1},{7,3},{8,12},{10,14},{12... | collective-permute-start | bytes 12296 | tf_op jit(solution)/shard_map/ppermute | solution.py:21
  35.7 8.2 %copy-start.10 = (f32[8,128]{1,0:T(8,128)}, f32[8,128]{1,0:T(8,128)S(1)}, u32[]{:S(2)}) copy-start(f32[8,128]{1,0:T(8,128)S(1)} %add.11.refs_4_) | copy-start | bytes 12292
  35.7 4.5 %collective-permute-start.13 = (f32[8,128]{1,0:T(8,128)S(1)}, f32[8,128]{1,0:T(8,128)S(1)}, u32[]{:S(2)}, u32[]{:S(2)}) collective-permute-start(f32[8,128]{1,0:T(8,128)S(1)} %add.11.refs_4_), channel_id=1, source_target_pairs={{0,24},{8,16},{16,8},{24,0},{1,25},{9,17},{17,9},{25,1},{2,26},{10... | collective-permute-start | bytes 12296 | tf_op jit(solution)/shard_map/ppermute | solution.py:21
  37.1 4.6 %collective-permute-start.12 = (f32[8,128]{1,0:T(8,128)S(1)}, f32[8,128]{1,0:T(8,128)S(1)}, u32[]{:S(2)}, u32[]{:S(2)}) collective-permute-start(f32[8,128]{1,0:T(8,128)S(1)} %add.11.refs_4_), channel_id=1, source_target_pairs={{0,16},{8,24},{16,0},{24,8},{1,17},{9,25},{17,1},{25,9},{2,18},{10... | collective-permute-start | bytes 12296 | tf_op jit(solution)/shard_map/ppermute | solution.py:21
  40.2 3.7 %copy-start.12 = (f32[8,128]{1,0:T(8,128)}, f32[8,128]{1,0:T(8,128)S(1)}, u32[]{:S(2)}) copy-start(f32[8,128]{1,0:T(8,128)S(1)} %collective-permute-done.13.refs_7_) | copy-start | bytes 12292
  40.2 3.6 %collective-permute-start.11 = (f32[8,128]{1,0:T(8,128)S(1)}, f32[8,128]{1,0:T(8,128)S(1)}, u32[]{:S(2)}, u32[]{:S(2)}) collective-permute-start(f32[8,128]{1,0:T(8,128)S(1)} %add.11.refs_4_), channel_id=1, source_target_pairs={{0,8},{8,0},{16,24},{24,16},{1,9},{9,1},{17,25},{25,17},{2,10},{10... | collective-permute-start | bytes 12296 | tf_op jit(solution)/shard_map/ppermute | solution.py:21
  41.7 2.2 %copy-start.13 = (f32[8,128]{1,0:T(8,128)}, f32[8,128]{1,0:T(8,128)S(1)}, u32[]{:S(2)}) copy-start(f32[8,128]{1,0:T(8,128)S(1)} %collective-permute-done.12.refs_6_) | copy-start | bytes 12292
  43.8 0.6 copy-start
  43.8 0.7 copy-start.1
  43.9 0.7 copy-start.2
  68.7 6.2 %collective-permute-start.16 = (f32[8,4,8,128]{3,2,1,0:T(8,128)}, f32[8,4,8,128]{3,2,1,0:T(8,128)S(1)}, u32[]{:S(2)}, u32[]{:S(2)}) collective-permute-start(f32[8,4,8,128]{3,2,1,0:T(8,128)} %render.1.refs_0_), channel_id=1, source_target_pairs={{0,24},{8,16},{16,8},{24,0},{1,25},{9,17},{17,9},{25,1},{2,26},{10... | collective-permute-start | bytes 393224 | tf_op jit(solution)/shard_map/ppermute | solution.py:21
  70.2 6.0 %collective-permute-start.15 = (f32[8,4,8,128]{3,2,1,0:T(8,128)}, f32[8,4,8,128]{3,2,1,0:T(8,128)S(1)}, u32[]{:S(2)}, u32[]{:S(2)}) collective-permute-start(f32[8,4,8,128]{3,2,1,0:T(8,128)} %render.1.refs_0_), channel_id=1, source_target_pairs={{0,16},{8,24},{16,0},{24,8},{1,17},{9,25},{17,1},{25,9},{2,18},{10... | collective-permute-start | bytes 393224 | tf_op jit(solution)/shard_map/ppermute | solution.py:21
  71.7 5.2 %collective-permute-start.14 = (f32[8,4,8,128]{3,2,1,0:T(8,128)}, f32[8,4,8,128]{3,2,1,0:T(8,128)S(1)}, u32[]{:S(2)}, u32[]{:S(2)}) collective-permute-start(f32[8,4,8,128]{3,2,1,0:T(8,128)} %render.1.refs_0_), channel_id=1, source_target_pairs={{0,8},{8,0},{16,24},{24,16},{1,9},{9,1},{17,25},{25,17},{2,10},{10... | collective-permute-start | bytes 393224 | tf_op jit(solution)/shard_map/ppermute | solution.py:21
  74.9 2.0 %copy-start.3 = (f32[8,4,8,128]{3,2,1,0:T(8,128)}, f32[8,4,8,128]{3,2,1,0:T(8,128)S(1)}, u32[]{:S(2)}) copy-start(f32[8,4,8,128]{3,2,1,0:T(8,128)S(1)} %collective-permute-done.16.refs_3_) | copy-start | bytes 393220
  76.2 0.7 copy-start.4
  76.9 0.6 copy-start.5
  (1 other events, 0.6 us)

commit v2 on v1

v2 whole, which is shorter than its diff:
```python
import functools
import math

import jax
import jax.numpy as jnp
from jax import lax
from jax.experimental import pallas as pl
from jax.experimental.pallas import tpu as pltpu
from jax.sharding import PartitionSpec as P

SUB, LANES = 8, 128
AXES = ("gx", "gy", "gz")
ANY = pl.BlockSpec(memory_space=pl.ANY)
VMEM = pl.BlockSpec(memory_space=pltpu.VMEM)
SMEM = pl.BlockSpec(memory_space=pltpu.SMEM)
f32 = jnp.float32
MARCH_UNROLL = 32
CHUNKS = 4


def limit(mib):
    return pltpu.CompilerParams(vmem_limit_bytes=mib * 2**20)


def swap(x, axis, bit_mask):
    n = lax.axis_size(axis)
    return lax.ppermute(x, axis, [(i, i ^ bit_mask) for i in range(n)])


def swap_across(x, axis):
    n = lax.axis_size(axis)
    return lax.ppermute(x, axis, [(i, (i + 1) % n if i % 2 else (i - 1) % n) for i in range(n)])


def flags(sizes):
    out = []
    for axis, n in zip(AXES, sizes):
        i = lax.axis_index(axis)
        out.append((lax.rem(i, 2) == 0, i == 0, i == n - 1))
    return out


def lookup(table, index):
    numbers = lax.GatherDimensionNumbers(
        offset_dims=(),
        collapsed_slice_dims=(1,),
        start_index_map=(1,),
        operand_batching_dims=(0,),
        start_indices_batching_dims=(0,),
    )
    return lax.gather(
        table, index[..., None], numbers, (1, 1), mode=lax.GatherScatterMode.PROMISE_IN_BOUNDS
    )


def faces_kernel(sizes, counts, v_hbm, *refs):
    comps, depth, rows, cols = v_hbm.shape
    tiles = rows // SUB
    info = flags(sizes)
    refs = list(refs)
    x_refs = [refs.pop(0) for _ in range(counts[0])]
    y_refs = [refs.pop(0) for _ in range(counts[1])]
    z_refs = [refs.pop(0) for _ in range(counts[2])]
    sq_ref, v_ref, sem = refs
    chunk = depth // CHUNKS
    copies = []
    for n in range(CHUNKS):
        part = pl.ds(n * chunk, chunk)
        copies.append(pltpu.make_async_copy(v_hbm.at[:, part], v_ref.at[:, part], sem.at[n]))
        copies[-1].start()

    def edge(axis, far, extent):
        at = jnp.where(info[axis][0], extent - 1, 0)
        return extent - 1 - at if far else at

    lane = lax.broadcasted_iota(jnp.int32, (SUB, LANES), 1)
    groups = depth * tiles // LANES
    zero = jnp.zeros((SUB, LANES), f32)
    picked = [[[zero] * comps for _ in range(groups)] for _ in z_refs]
    squares = [zero] * 4
    for n in range(CHUNKS):
        copies[n].wait()
        for x in range(n * chunk, (n + 1) * chunk):
            for far, out in enumerate(y_refs):
                at = edge(1, far, rows)
                for c in range(comps):
                    out[c, pl.ds(x, 1), :] = v_ref[c, x, pl.ds(at, 1), :]
            for c in range(comps):
                for j in range(tiles):
                    tile = v_ref[c, x, pl.ds(j * SUB, SUB), :]
                    squares[j % 4] = squares[j % 4] + tile * tile
                    group, to = divmod(x * tiles + j, LANES)
                    for far in range(len(z_refs)):
                        at = edge(2, far, cols)
                        moved = pltpu.roll(tile, lax.rem(to - at + cols, cols), 1)
                        old = picked[far][group][c]
                        picked[far][group][c] = jnp.where(lane == to, moved, old)
    for far, out in enumerate(x_refs):
        for c in range(comps):
            out[c] = v_ref[c, edge(0, far, depth)]
    total = (squares[0] + squares[1]) + (squares[2] + squares[3])
    sq_ref[...] = total
    for far, out in enumerate(z_refs):
        for g in range(groups):
            for c in range(comps):
                out[g * comps + c] = picked[far][g][c]
        out[groups * comps] = total


def attach_kernel(faces, tiles, *refs):
    face_refs, tile_refs = refs[:faces], refs[faces : faces + tiles]
    outs, sum_ref = refs[faces + tiles : -1], refs[-1]
    total = tile_refs[0][...]
    for t in tile_refs[1:]:
        total = total + t[...]
    sum_ref[...] = total
    for face, out in zip(face_refs, outs):
        comps = face.shape[0]
        out[pl.ds(0, comps)] = face[...]
        out[comps, pl.ds(0, SUB), :] = total


def q_kernel(sizes, counts, attached, extras, v_hbm, *refs):
    comps, depth, rows, cols = v_hbm.shape
    tiles = rows // SUB
    nx = sizes[0]
    refs = list(refs)
    halos = [[refs.pop(0) for _ in range(counts[a])] for a in range(3)]
    extra = [refs.pop(0) for _ in range(extras)]
    outs, (padded, sem) = refs[:nx], refs[nx:]
    info = flags(sizes)
    copy = pltpu.make_async_copy(
        v_hbm, padded.at[:, pl.ds(1, depth), pl.ds(SUB, rows), :], sem.at[0]
    )
    copy.start()

    def both(axis, index):
        even, first, last = info[axis]
        if not halos[axis]:
            return 0.0, 0.0
        near = halos[axis][0][index]
        far = halos[axis][-1][index]
        low = jnp.where(first, 0.0, jnp.where(even, far, near))
        high = jnp.where(last, 0.0, jnp.where(even, near, far))
        return low, high

    for c in range(comps):
        for end, value in zip((0, depth + 1), both(0, c)):
            padded[c, end, pl.ds(SUB, rows), :] = jnp.broadcast_to(value, (rows, cols))
        for end, value in zip((SUB - 1, SUB + rows), both(1, c)):
            value = jnp.broadcast_to(value, (depth, cols))
            for x in range(depth):
                padded[c, 1 + x, pl.ds(end, 1), :] = value[x : x + 1]
    tile_sum = extra[0][...]
    for t in extra[1:]:
        tile_sum = tile_sum + t[...]
    for near_far in halos[1][:attached]:
        tile_sum = tile_sum + near_far[comps, pl.ds(0, SUB), :]
    for out in outs:
        out[depth, pl.ds(0, SUB), :] = tile_sum
    groups = depth * tiles // LANES
    lane = lax.broadcasted_iota(jnp.int32, (SUB, cols), 1)
    me = lax.axis_index("gx")
    piece_tiles = tiles // nx
    per = LANES // tiles
    zeven = info[2][0]
    zero = jnp.zeros((SUB, LANES), f32)
    zhalo = []
    for g in range(groups):
        zhalo.append([])
        for c in range(comps):
            if counts[2] == 1:
                zhalo[g].append(halos[2][0][g * comps + c])
            else:
                zhalo[g].append([zero + h for h in both(2, g * comps + c)])
    copy.wait()
    for k in range(nx):
        for p in range(piece_tiles):
            j = jnp.bitwise_xor(me, k) * piece_tiles + p
            base = j * SUB + SUB
            middle = pl.ds(pl.multiple_of(base, SUB), SUB)
            for x in range(depth):
                g, i = divmod(x, per)
                at = i * tiles + j
                dx, dy, dz = [], [], []
                for c in range(comps):
                    here = padded[c, x + 1, middle, :]
                    dx.append(padded[c, x + 2, middle, :] - padded[c, x, middle, :])
                    dy.append(
                        padded[c, x + 1, pl.ds(base + 1, SUB), :]
                        - padded[c, x + 1, pl.ds(base - 1, SUB), :]
                    )
                    if counts[2] == 1:
                        shift = jnp.where(zeven, cols - 1 - at, lax.rem(cols - at, cols))
                        moved = pltpu.roll(zhalo[g][c], shift, 1)
                        high = jnp.where(zeven, moved, 0.0)
                        low = jnp.where(zeven, 0.0, moved)
                    else:
                        low = pltpu.roll(zhalo[g][c][0], lax.rem(cols - at, cols), 1)
                        high = pltpu.roll(zhalo[g][c][1], cols - 1 - at, 1)
                    up = jnp.where(lane == cols - 1, high, pltpu.roll(here, cols - 1, 1))
                    down = jnp.where(lane == 0, low, pltpu.roll(here, 1, 1))
                    dz.append(up - down)
                cross = dy[0] * dx[1] + dz[0] * dx[2] + dz[1] * dy[2]
                total = dx[0] * dx[0] + dy[1] * dy[1] + dz[2] * dz[2] + (cross + cross)
                outs[k][x, pl.ds(p * SUB, SUB), :] = total


def render_kernel(nx, cell_count, *refs):
    refs = list(refs)
    pieces = [refs.pop(0) for _ in range(nx)]
    sign_ref, table_ref, out_ref, low_ref, frac_ref, tab_ref = refs
    planes, rows, cols = pieces[0].shape
    depth = planes - 1
    bins = table_ref.shape[-1]
    views = sign_ref.shape[0]
    depth_total = depth * nx
    me = lax.axis_index("gx")
    squares = pieces[0][depth, pl.ds(0, SUB), :]
    for piece in pieces[1:]:
        squares = squares + piece[depth, pl.ds(0, SUB), :]
    energy = jnp.sum(squares, keepdims=True) / cell_count
    scale = -0.25 / (energy + 1e-06)
    scale = jnp.broadcast_to(scale, (SUB, cols))
    for k in range(nx):
        base = jnp.bitwise_xor(me, k) * depth

        def classify(x, carry):
            for p in range(rows // SUB):
                part = pieces[k][x, pl.ds(p * SUB, SUB), :] * scale
                coord = (bins - 1) / (1.0 + jnp.exp(-part))
                low = coord.astype(jnp.int32)
                low_ref[base + x, pl.ds(p * SUB, SUB), :] = low
                frac_ref[base + x, pl.ds(p * SUB, SUB), :] = coord - low.astype(f32)
            return carry

        lax.fori_loop(0, depth, classify, 0, unroll=8)

    table = table_ref[...]
    lane = lax.broadcasted_iota(jnp.int32, table.shape, 1)
    row = lax.broadcasted_iota(jnp.int32, table.shape, 0)
    factor = -3.0 / depth_total * math.log2(math.e)
    table = jnp.where(lax.rem(row, 4) == 3, table * factor, table)
    step = jnp.where(lane == bins - 1, 0.0, pltpu.roll(table, bins - 1, 1) - table)
    tab_ref[0] = table
    tab_ref[1] = step

    for p in range(rows // SUB):

        def view_body(v, carry):
            forward = sign_ref[v] == 0
            start = jnp.where(forward, 0, depth_total - 1)
            stride = jnp.where(forward, 1, -1)
            values = [
                jnp.broadcast_to(tab_ref[0, pl.ds(v * 4 + c, 1), :], (SUB, bins)) for c in range(4)
            ]
            steps = [
                jnp.broadcast_to(tab_ref[1, pl.ds(v * 4 + c, 1), :], (SUB, bins)) for c in range(4)
            ]

            def march(i, state):
                light, total, red, green, blue = state
                x = start + stride * i
                low = low_ref[x, pl.ds(p * SUB, SUB), :]
                frac = frac_ref[x, pl.ds(p * SUB, SUB), :]

                def look(c):
                    return lookup(values[c], low) + frac * lookup(steps[c], low)

                exponent = look(3)
                through = jnp.exp2(exponent)
                weight = light * (1.0 - through)
                return (
                    light * through,
                    total + exponent,
                    red + weight * look(0),
                    green + weight * look(1),
                    blue + weight * look(2),
                )

            zero = jnp.zeros((SUB, cols), f32)
            _, total, red, green, blue = lax.fori_loop(
                0, depth_total, march, (jnp.ones((SUB, cols), f32), zero, zero, zero, zero), unroll=MARCH_UNROLL
            )
            for c, value in enumerate((red, green, blue, 1.0 - jnp.exp2(total))):
                out_ref[v, c, pl.ds(p * SUB, SUB), :] = value
            return carry

        lax.fori_loop(0, views, view_body, 0)


def assemble_kernel(nx, *refs):
    pieces, out, sem = refs[:nx], refs[nx], refs[nx + 1]
    rows = pieces[0].shape[2]
    me = lax.axis_index("gx")
    copies = []
    for k in range(nx):
        at = pl.multiple_of(jnp.bitwise_xor(me, k) * rows, SUB)
        copies.append(pltpu.make_async_copy(pieces[k], out.at[:, :, pl.ds(at, rows), :], sem.at[k]))
        copies[-1].start()
    for copy in copies:
        copy.wait()


def on_device(velocity, view_sign, transfer):
    comps, depth, rows, cols = velocity.shape
    views, channels, bins = transfer.shape
    sizes = tuple(lax.axis_size(a) for a in AXES)
    nx = sizes[0]
    assert all(n & (n - 1) == 0 for n in sizes)
    assert cols == LANES and bins == LANES and rows % (SUB * nx) == 0
    assert depth * (rows // SUB) % LANES == 0
    cell_count = depth * rows * cols * math.prod(sizes)
    counts = tuple(min(n - 1, 2) for n in sizes)
    groups = depth * (rows // SUB) // LANES
    tile = jax.ShapeDtypeStruct((SUB, LANES), f32)
    x_face = jax.ShapeDtypeStruct((comps, rows, cols), f32)
    y_face = jax.ShapeDtypeStruct((comps, depth, cols), f32)
    y_sent = jax.ShapeDtypeStruct((comps + 1, depth, cols), f32)
    z_face = jax.ShapeDtypeStruct((groups * comps + 1, SUB, LANES), f32)
    shapes = [x_face] * counts[0] + [y_face] * counts[1] + [z_face] * counts[2] + [tile]
    *faces, squares = pl.pallas_call(
        functools.partial(faces_kernel, sizes, counts),
        out_shape=shapes,
        in_specs=[ANY],
        out_specs=[VMEM] * len(shapes),
        scratch_shapes=[
            pltpu.VMEM((comps, depth, rows, cols), f32),
            pltpu.SemaphoreType.DMA((CHUNKS,)),
        ],
        compiler_params=limit(4),
        name="faces",
    )(velocity)

    def exchange(sent, axis):
        kinds = (functools.partial(swap, bit_mask=1), swap_across)
        return [kind(x, axis) for x, kind in zip(sent, kinds)]

    def everyone(x, axis):
        for bit in range(lax.axis_size(axis).bit_length() - 1):
            x = x + swap(x, axis, 1 << bit)
        return x

    x_faces, y_faces, z_faces = (
        faces[: counts[0]],
        faces[counts[0] : counts[0] + counts[1]],
        faces[counts[0] + counts[1] :],
    )
    z_halos = exchange(z_faces, "gz")
    x_halos = exchange(x_faces, "gx")
    if sizes[2] == 2:
        tiles = [squares, z_halos[0][groups * comps]]
    else:
        tiles = [everyone(squares, "gz")]
    *y_sents, column = pl.pallas_call(
        functools.partial(attach_kernel, len(y_faces), len(tiles)),
        out_shape=[y_sent] * len(y_faces) + [tile],
        in_specs=[VMEM] * (len(y_faces) + len(tiles)),
        out_specs=[VMEM] * (len(y_faces) + 1),
        compiler_params=limit(2),
        name="attach",
    )(*y_faces, *tiles)
    y_halos = exchange(y_sents, "gy")
    if sizes[1] == 4:
        attached, extra = 2, [column, swap(column, "gy", 2)]
    elif sizes[1] <= 2:
        attached, extra = counts[1], [column]
    else:
        attached, extra = 0, [everyone(column, "gy")]
    part_rows = rows // nx
    piece = jax.ShapeDtypeStruct((depth + 1, part_rows, cols), f32)
    halos = x_halos + y_halos + z_halos
    q_pieces = pl.pallas_call(
        functools.partial(q_kernel, sizes, counts, attached, len(extra)),
        out_shape=[piece] * nx,
        in_specs=[ANY] + [VMEM] * (len(halos) + len(extra)),
        out_specs=[VMEM] * nx,
        scratch_shapes=[
            pltpu.VMEM((comps, depth + 2, rows + 2 * SUB, cols), f32),
            pltpu.SemaphoreType.DMA((1,)),
        ],
        compiler_params=limit(8),
        name="q",
    )(velocity, *halos, *extra)
    order = sorted(range(1, nx), key=lambda k: -k)
    got = {0: q_pieces[0]}
    for k in order:
        got[k] = swap(q_pieces[k], "gx", k)
    image_piece = pl.pallas_call(
        functools.partial(render_kernel, nx, cell_count),
        out_shape=jax.ShapeDtypeStruct((views, channels, part_rows, cols), f32),
        in_specs=[VMEM] * nx + [SMEM, VMEM],
        out_specs=VMEM,
        scratch_shapes=[
            pltpu.VMEM((depth * nx, part_rows, cols), jnp.int32),
            pltpu.VMEM((depth * nx, part_rows, cols), f32),
            pltpu.VMEM((2, views * channels, bins), f32),
        ],
        compiler_params=limit(8),
        name="render",
    )(*[got[k] for k in range(nx)], view_sign, transfer.reshape(views * channels, bins))
    images = {0: image_piece}
    for k in order:
        images[k] = swap(image_piece, "gx", k)
    return pl.pallas_call(
        functools.partial(assemble_kernel, nx),
        out_shape=jax.ShapeDtypeStruct((views, channels, rows, cols), f32),
        in_specs=[VMEM] * nx,
        out_specs=ANY,
        scratch_shapes=[pltpu.SemaphoreType.DMA((nx,))],
        compiler_params=limit(2),
        name="assemble",
    )(*[images[k] for k in range(nx)])


def solution(mesh):
    in_specs = (P(None, "gx", "gy", "gz"), P(), P())
    out_specs = P(None, None, "gy", "gz")
    return jax.shard_map(
        on_device, mesh=mesh, in_specs=in_specs, out_specs=out_specs, check_vma=False
    )
```

time: 79.7 us -> 50.3 us (0.63)
  Pallas kernels: 36.1 us -> 18.9 us
  waiting for transfers between devices: 20.1 us -> 13.6 us
  starting transfers between devices: 21 us -> 16.2 us
    pallas_call x1, Pallas kernels: 24.2 us -> 15.4 us  [on_device(): pl.pallas_call(functools.partial(render_kernel, nx, cell_count), out_shap...]
    pallas_call x2 -> x3, Pallas kernels: 10.1 us -> 2.65 us  [the longest x1 1.58 us: on_device(): pl.pallas_call(functools.partial(q_kernel, sizes, counts, attached, len(e...]
    ppermute x15 -> x10, starting transfers between devices: 17.1 us -> 12.2 us  [swap(): return lax.ppermute(x, axis, [(i, i ^ bit_mask) for i in range(n)])]
    ppermute x15 -> x10, waiting for transfers between devices: 18 us -> 13.5 us  [swap(): return lax.ppermute(x, axis, [(i, i ^ bit_mask) for i in range(n)])]
    ppermute x2, waiting for transfers between devices: 2.19 us -> 0.01 us  [swap_across(): lax.ppermute(x, axis, [(i, (i + 1) % n if i % 2 else (i - 1) % n) for i i...]
    pallas_call x1, Pallas kernels: 1.91 us -> 0.82 us  [on_device(): pl.pallas_call(functools.partial(assemble_kernel, nx), out_shape=jax.Shap...]
    unnamed x32 -> x8, local copies, waits for them, and re-layouts: 1.98 us -> 1.42 us
  transfers between devices with their start and end apart: 17 -> 12, of which waited for: 10 -> 6; matrix products, arithmetic and copies ran while one was open for 0% -> 0% of each run, Pallas kernels for 0% -> 0%
where the time goes in v2:
time: 50.3 us; the launch traced here: 50.2 us
  Pallas kernels  18.9 us (38%)
  starting transfers between devices  16.2 us (32%)
  waiting for transfers between devices  13.6 us (27%)
  local copies, waits for them, and re-layouts  1.42 us (3%)
    pallas_call x1, Pallas kernels, on_device(): pl.pallas_call(functools.partial(render_kernel, nx, cell_count), out_shap...  15.4 us
    ppermute x10, waiting for transfers between devices, swap(): return lax.ppermute(x, axis, [(i, i ^ bit_mask) for i in range(n)])  13.5 us
    ppermute x10, starting transfers between devices, swap(): return lax.ppermute(x, axis, [(i, i ^ bit_mask) for i in range(n)])  12.2 us
    ppermute x2, starting transfers between devices, swap_across(): lax.ppermute(x, axis, [(i, (i + 1) % n if i % 2 else (i - 1) % n) for i i...  3.97 us
    pallas_call x1, Pallas kernels, on_device(): pl.pallas_call(functools.partial(q_kernel, sizes, counts, attached, len(e...  1.58 us
    unnamed x8, local copies, waits for them, and re-layouts  1.42 us
    pallas_call x1, Pallas kernels, on_device(): pl.pallas_call(functools.partial(faces_kernel, sizes, counts), out_shape=...  1.06 us
  transfers between devices with their start and end apart: 12, of which 6 were waited for; matrix products, arithmetic and copies ran while one was open for 0% of the time, Pallas kernels for 0%

profile of v2, /device:TPU:0, one launch (start us, length us, event | category | flops | bytes accessed | tf_op | source)
XLA Modules:
  0.0 50.2 jit_solution(18183036199011810527)
XLA Ops:
  0.0 1.4 %copy-done = f32[3,32,32,128]{3,2,1,0:T(8,128)S(1)} copy-done((f32[3,32,32,128]{3,2,1,0:T(8,128)S(1)}, f32[3,32,32,128]{3,2,1,0:T(8,128)}, u32[]{:S(2)}) %copy-start) | copy-done | bytes 1572888
  1.4 1.1 %faces.1 = (f32[3,32,128]{2,1,0:T(8,128)S(1)}, f32[3,32,128]{2,1,0:T(8,128)S(1)}, f32[3,32,128]{2,1,0:T(8,128)S(1)}, f32[3,32,128]{2,1,0:T(8,128)S(1)}, f32[4,8,128]{2,1,0:T(8,128)S(1)}, /*index=5*/f32[8,128]{1,0:T(8,128)S(1)}) custom-call(f32[3,32,32,128]{3,2,1,0:T(8,128)S(1)} %copy-done), custom_call_target="tpu_custom_call" | custom-call | tf_op jit(solution)/shard_map/faces/pallas_call | solution.py:322
  2.5 0.6 %collective-permute-start.2 = (f32[4,8,128]{2,1,0:T(8,128)S(1)}, f32[4,8,128]{2,1,0:T(8,128)S(1)}, u32[]{:S(2)}, u32[]{:S(2)}) collective-permute-start(f32[4,8,128]{2,1,0:T(8,128)S(1)} %get-tuple-element.23), channel_id=1, source_target_pairs={{0,1},{1,0},{2,3},{3,2},{4,5},{5,4},{6,7},{7,6},{8,9},{9,8},{10,11... | collective-permute-start | bytes 49160 | tf_op jit(solution)/shard_map/ppermute | solution.py:27
  3.0 0.8 %collective-permute-done.2.refs_4_ = f32[4,8,128]{2,1,0:T(8,128)S(1)} collective-permute-done((f32[4,8,128]{2,1,0:T(8,128)S(1)}, f32[4,8,128]{2,1,0:T(8,128)S(1)}, u32[]{:S(2)}, u32[]{:S(2)}) %collective-permute-start.2) | collective-permute-done | bytes 16416 | tf_op jit(solution)/shard_map/ppermute | solution.py:27
  3.9 3.0 %collective-permute-start.3 = (f32[4,32,128]{2,1,0:T(8,128)S(1)}, f32[4,32,128]{2,1,0:T(8,128)S(1)}, u32[]{:S(2)}, u32[]{:S(2)}) collective-permute-start(f32[4,32,128]{2,1,0:T(8,128)S(1)} %get-tuple-element.24), channel_id=1, source_target_pairs={{0,2},{2,0},{4,6},{6,4},{1,3},{3,1},{5,7},{7,5},{8,10},{10,8},{12,... | collective-permute-start | bytes 196616 | tf_op jit(solution)/shard_map/ppermute | solution.py:27
  6.9 2.5 %collective-permute-start.4 = (f32[4,32,128]{2,1,0:T(8,128)S(1)}, f32[4,32,128]{2,1,0:T(8,128)S(1)}, u32[]{:S(2)}, u32[]{:S(2)}) collective-permute-start(f32[4,32,128]{2,1,0:T(8,128)S(1)} %get-tuple-element.25), channel_id=1, source_target_pairs={{0,6},{2,4},{4,2},{6,0},{1,7},{3,5},{5,3},{7,1},{8,14},{10,12},{12... | collective-permute-start | bytes 196616 | tf_op jit(solution)/shard_map/ppermute | solution.py:32
  9.3 1.5 %collective-permute-start = (f32[3,32,128]{2,1,0:T(8,128)S(1)}, f32[3,32,128]{2,1,0:T(8,128)S(1)}, u32[]{:S(2)}, u32[]{:S(2)}) collective-permute-start(f32[3,32,128]{2,1,0:T(8,128)S(1)} %get-tuple-element.18), channel_id=1, source_target_pairs={{0,8},{8,0},{16,24},{24,16},{1,9},{9,1},{17,25},{25,17},{2,10},{10... | collective-permute-start | bytes 147464 | tf_op jit(solution)/shard_map/ppermute | solution.py:27
  10.8 1.5 %collective-permute-start.1 = (f32[3,32,128]{2,1,0:T(8,128)S(1)}, f32[3,32,128]{2,1,0:T(8,128)S(1)}, u32[]{:S(2)}, u32[]{:S(2)}) collective-permute-start(f32[3,32,128]{2,1,0:T(8,128)S(1)} %get-tuple-element.19), channel_id=1, source_target_pairs={{0,24},{8,16},{16,8},{24,0},{1,25},{9,17},{17,9},{25,1},{2,26},{10... | collective-permute-start | bytes 147464 | tf_op jit(solution)/shard_map/ppermute | solution.py:32
  12.3 0.1 collective-permute-start.5
  12.4 4.4 %collective-permute-done.5.refs_6_ = f32[8,128]{1,0:T(8,128)S(1)} collective-permute-done((f32[8,128]{1,0:T(8,128)S(1)}, f32[8,128]{1,0:T(8,128)S(1)}, u32[]{:S(2)}, u32[]{:S(2)}) %collective-permute-start.5) | collective-permute-done | bytes 4128 | tf_op jit(solution)/shard_map/ppermute | solution.py:27
  16.8 0.0 collective-permute-done.refs_0_
  16.8 0.0 collective-permute-done.1.refs_1_
  16.8 0.0 collective-permute-done.3.refs_2_
  16.8 0.0 collective-permute-done.4.refs_3_
  16.9 0.0 copy-done.1
  16.9 1.6 %q.1 = (f32[33,8,128]{2,1,0:T(8,128)S(1)}, f32[33,8,128]{2,1,0:T(8,128)S(1)}, f32[33,8,128]{2,1,0:T(8,128)S(1)}, f32[33,8,128]{2,1,0:T(8,128)S(1)}) custom-call(f32[3,32,32,128]{3,2,1,0:T(8,128)S(1)} %copy-done.1, f32[3,32,128]{2,1,0:T(8,128)S(1)} %collective-permute-done.refs_0_, f32[3,32,128]{2,1,0:T(8,128)S(1)} %collective-permute-done.1.refs_1_, ...), custom_call_target="tpu_custom_call" | custom-call | tf_op jit(solution)/shard_map/q/pallas_call | solution.py:373
  18.5 1.6 %collective-permute-start.6 = (f32[33,8,128]{2,1,0:T(8,128)S(1)}, f32[33,8,128]{2,1,0:T(8,128)S(1)}, u32[]{:S(2)}, u32[]{:S(2)}) collective-permute-start(f32[33,8,128]{2,1,0:T(8,128)S(1)} %get-tuple-element.28), channel_id=1, source_target_pairs={{0,8},{8,0},{16,24},{24,16},{1,9},{9,1},{17,25},{25,17},{2,10},{10... | collective-permute-start | bytes 405512 | tf_op jit(solution)/shard_map/ppermute | solution.py:27
  20.0 0.5 %collective-permute-start.7 = (f32[33,8,128]{2,1,0:T(8,128)S(1)}, f32[33,8,128]{2,1,0:T(8,128)S(1)}, u32[]{:S(2)}, u32[]{:S(2)}) collective-permute-start(f32[33,8,128]{2,1,0:T(8,128)S(1)} %get-tuple-element.29), channel_id=1, source_target_pairs={{0,16},{8,24},{16,0},{24,8},{1,17},{9,25},{17,1},{25,9},{2,18},{10... | collective-permute-start | bytes 405512 | tf_op jit(solution)/shard_map/ppermute | solution.py:27
  20.5 1.5 %collective-permute-start.8 = (f32[33,8,128]{2,1,0:T(8,128)S(1)}, f32[33,8,128]{2,1,0:T(8,128)S(1)}, u32[]{:S(2)}, u32[]{:S(2)}) collective-permute-start(f32[33,8,128]{2,1,0:T(8,128)S(1)} %get-tuple-element.30), channel_id=1, source_target_pairs={{0,24},{8,16},{16,8},{24,0},{1,25},{9,17},{17,9},{25,1},{2,26},{10... | collective-permute-start | bytes 405512 | tf_op jit(solution)/shard_map/ppermute | solution.py:27
  22.0 2.6 %collective-permute-done.6.refs_1_ = f32[33,8,128]{2,1,0:T(8,128)S(1)} collective-permute-done((f32[33,8,128]{2,1,0:T(8,128)S(1)}, f32[33,8,128]{2,1,0:T(8,128)S(1)}, u32[]{:S(2)}, u32[]{:S(2)}) %collective-permute-start.6) | collective-permute-done | bytes 135200 | tf_op jit(solution)/shard_map/ppermute | solution.py:27
  24.6 1.9 %collective-permute-done.7.refs_2_ = f32[33,8,128]{2,1,0:T(8,128)S(1)} collective-permute-done((f32[33,8,128]{2,1,0:T(8,128)S(1)}, f32[33,8,128]{2,1,0:T(8,128)S(1)}, u32[]{:S(2)}, u32[]{:S(2)}) %collective-permute-start.7) | collective-permute-done | bytes 135200 | tf_op jit(solution)/shard_map/ppermute | solution.py:27
  26.5 0.0 collective-permute-done.8.refs_3_
  26.5 0.0 copy-done.2
  26.5 0.0 copy-done.3
  26.5 15.4 %render.1.refs_0_ = f32[8,4,8,128]{3,2,1,0:T(8,128)S(1)} custom-call(f32[33,8,128]{2,1,0:T(8,128)S(1)} %get-tuple-element.27.refs_0_, f32[33,8,128]{2,1,0:T(8,128)S(1)} %collective-permute-done.6.refs_1_, f32[33,8,128]{2,1,0:T(8,128)S(1)} %collective-permute-done.7.refs_2_, f32[33,8,128]{2,1,0:T(8,128)S(1)} %collective-permute-done.8.refs_3_, ...), custom_call_target="tpu_custom_call" | custom-call | tf_op jit(solution)/shard_map/render/pallas_call | solution.py:389
  42.0 1.4 %collective-permute-start.11 = (f32[8,4,8,128]{3,2,1,0:T(8,128)S(1)}, f32[8,4,8,128]{3,2,1,0:T(8,128)S(1)}, u32[]{:S(2)}, u32[]{:S(2)}) collective-permute-start(f32[8,4,8,128]{3,2,1,0:T(8,128)S(1)} %render.1.refs_0_), channel_id=1, source_target_pairs={{0,24},{8,16},{16,8},{24,0},{1,25},{9,17},{17,9},{25,1},{2,26},{10... | collective-permute-start | bytes 393224 | tf_op jit(solution)/shard_map/ppermute | solution.py:27
  43.4 0.5 %collective-permute-start.10 = (f32[8,4,8,128]{3,2,1,0:T(8,128)S(1)}, f32[8,4,8,128]{3,2,1,0:T(8,128)S(1)}, u32[]{:S(2)}, u32[]{:S(2)}) collective-permute-start(f32[8,4,8,128]{3,2,1,0:T(8,128)S(1)} %render.1.refs_0_), channel_id=1, source_target_pairs={{0,16},{8,24},{16,0},{24,8},{1,17},{9,25},{17,1},{25,9},{2,18},{10... | collective-permute-start | bytes 393224 | tf_op jit(solution)/shard_map/ppermute | solution.py:27
  44.0 1.6 %collective-permute-start.9 = (f32[8,4,8,128]{3,2,1,0:T(8,128)S(1)}, f32[8,4,8,128]{3,2,1,0:T(8,128)S(1)}, u32[]{:S(2)}, u32[]{:S(2)}) collective-permute-start(f32[8,4,8,128]{3,2,1,0:T(8,128)S(1)} %render.1.refs_0_), channel_id=1, source_target_pairs={{0,8},{8,0},{16,24},{24,16},{1,9},{9,1},{17,25},{25,17},{2,10},{10... | collective-permute-start | bytes 393224 | tf_op jit(solution)/shard_map/ppermute | solution.py:27
  45.6 2.5 %collective-permute-done.11.refs_3_ = f32[8,4,8,128]{3,2,1,0:T(8,128)S(1)} collective-permute-done((f32[8,4,8,128]{3,2,1,0:T(8,128)S(1)}, f32[8,4,8,128]{3,2,1,0:T(8,128)S(1)}, u32[]{:S(2)}, u32[]{:S(2)}) %collective-permute-start.11) | collective-permute-done | bytes 131104 | tf_op jit(solution)/shard_map/ppermute | solution.py:27
  48.0 1.3 %collective-permute-done.10.refs_2_ = f32[8,4,8,128]{3,2,1,0:T(8,128)S(1)} collective-permute-done((f32[8,4,8,128]{3,2,1,0:T(8,128)S(1)}, f32[8,4,8,128]{3,2,1,0:T(8,128)S(1)}, u32[]{:S(2)}, u32[]{:S(2)}) %collective-permute-start.10) | collective-permute-done | bytes 131104 | tf_op jit(solution)/shard_map/ppermute | solution.py:27
  49.3 0.0 collective-permute-done.9.refs_1_
  49.3 0.8 %assemble.1 = f32[8,4,32,128]{3,2,1,0:T(8,128)} custom-call(f32[8,4,8,128]{3,2,1,0:T(8,128)S(1)} %render.1.refs_0_, f32[8,4,8,128]{3,2,1,0:T(8,128)S(1)} %collective-permute-done.9.refs_1_, f32[8,4,8,128]{3,2,1,0:T(8,128)S(1)} %collective-permute-done.10.refs_2_, f32[8,4,8,128]{3,2,1,0:T(8,128)S(1)} %collective-permute-done.11.refs_3_), custom_call_target="tpu_custom_call" | custom-call | tf_op jit(solution)/shard_map/assemble/pallas_call | solution.py:405
  (6 shorter events, 0.0 us)
Async XLA Ops:
  0.0 1.4 %copy-start = (f32[3,32,32,128]{3,2,1,0:T(8,128)S(1)}, f32[3,32,32,128]{3,2,1,0:T(8,128)}, u32[]{:S(2)}) copy-start(f32[3,32,32,128]{3,2,1,0:T(8,128)} %v_hbm.3) | copy-start | bytes 4718596
  1.4 15.4 %copy-start.1 = (f32[3,32,32,128]{3,2,1,0:T(8,128)S(1)}, f32[3,32,32,128]{3,2,1,0:T(8,128)}, u32[]{:S(2)}) copy-start(f32[3,32,32,128]{3,2,1,0:T(8,128)} %v_hbm.3) | copy-start | bytes 4718596
  1.4 25.1 %copy-start.2 = (f32[8,4,128]{2,1,0:T(4,128)S(1)}, f32[8,4,128]{2,1,0:T(4,128)}, u32[]{:S(2)}) copy-start(f32[8,4,128]{2,1,0:T(4,128)} %param.5) | copy-start | bytes 49156
  1.4 25.1 %copy-start.3 = (s32[8]{0:T(128)S(1)}, s32[8]{0:T(128)}, u32[]{:S(2)}) copy-start(s32[8]{0:T(128)} %refs_4_.1) | copy-start | bytes 100
  2.5 1.4 %collective-permute-start.2 = (f32[4,8,128]{2,1,0:T(8,128)S(1)}, f32[4,8,128]{2,1,0:T(8,128)S(1)}, u32[]{:S(2)}, u32[]{:S(2)}) collective-permute-start(f32[4,8,128]{2,1,0:T(8,128)S(1)} %get-tuple-element.23), channel_id=1, source_target_pairs={{0,1},{1,0},{2,3},{3,2},{4,5},{5,4},{6,7},{7,6},{8,9},{9,8},{10,11... | collective-permute-start | bytes 49160 | tf_op jit(solution)/shard_map/ppermute | solution.py:27
  3.9 12.9 %collective-permute-start.3 = (f32[4,32,128]{2,1,0:T(8,128)S(1)}, f32[4,32,128]{2,1,0:T(8,128)S(1)}, u32[]{:S(2)}, u32[]{:S(2)}) collective-permute-start(f32[4,32,128]{2,1,0:T(8,128)S(1)} %get-tuple-element.24), channel_id=1, source_target_pairs={{0,2},{2,0},{4,6},{6,4},{1,3},{3,1},{5,7},{7,5},{8,10},{10,8},{12,... | collective-permute-start | bytes 196616 | tf_op jit(solution)/shard_map/ppermute | solution.py:27
  6.9 10.0 %collective-permute-start.4 = (f32[4,32,128]{2,1,0:T(8,128)S(1)}, f32[4,32,128]{2,1,0:T(8,128)S(1)}, u32[]{:S(2)}, u32[]{:S(2)}) collective-permute-start(f32[4,32,128]{2,1,0:T(8,128)S(1)} %get-tuple-element.25), channel_id=1, source_target_pairs={{0,6},{2,4},{4,2},{6,0},{1,7},{3,5},{5,3},{7,1},{8,14},{10,12},{12... | collective-permute-start | bytes 196616 | tf_op jit(solution)/shard_map/ppermute | solution.py:32
  9.3 7.5 %collective-permute-start = (f32[3,32,128]{2,1,0:T(8,128)S(1)}, f32[3,32,128]{2,1,0:T(8,128)S(1)}, u32[]{:S(2)}, u32[]{:S(2)}) collective-permute-start(f32[3,32,128]{2,1,0:T(8,128)S(1)} %get-tuple-element.18), channel_id=1, source_target_pairs={{0,8},{8,0},{16,24},{24,16},{1,9},{9,1},{17,25},{25,17},{2,10},{10... | collective-permute-start | bytes 147464 | tf_op jit(solution)/shard_map/ppermute | solution.py:27
  10.8 6.0 %collective-permute-start.1 = (f32[3,32,128]{2,1,0:T(8,128)S(1)}, f32[3,32,128]{2,1,0:T(8,128)S(1)}, u32[]{:S(2)}, u32[]{:S(2)}) collective-permute-start(f32[3,32,128]{2,1,0:T(8,128)S(1)} %get-tuple-element.19), channel_id=1, source_target_pairs={{0,24},{8,16},{16,8},{24,0},{1,25},{9,17},{17,9},{25,1},{2,26},{10... | collective-permute-start | bytes 147464 | tf_op jit(solution)/shard_map/ppermute | solution.py:32
  12.3 4.5 %collective-permute-start.5 = (f32[8,128]{1,0:T(8,128)S(1)}, f32[8,128]{1,0:T(8,128)S(1)}, u32[]{:S(2)}, u32[]{:S(2)}) collective-permute-start(f32[8,128]{1,0:T(8,128)S(1)} %get-tuple-element.26.refs_5_), channel_id=1, source_target_pairs={{0,4},{2,6},{4,0},{6,2},{1,5},{3,7},{5,1},{7,3},{8,12},{10,14},{12... | collective-permute-start | bytes 12296 | tf_op jit(solution)/shard_map/ppermute | solution.py:27
  18.5 6.1 %collective-permute-start.6 = (f32[33,8,128]{2,1,0:T(8,128)S(1)}, f32[33,8,128]{2,1,0:T(8,128)S(1)}, u32[]{:S(2)}, u32[]{:S(2)}) collective-permute-start(f32[33,8,128]{2,1,0:T(8,128)S(1)} %get-tuple-element.28), channel_id=1, source_target_pairs={{0,8},{8,0},{16,24},{24,16},{1,9},{9,1},{17,25},{25,17},{2,10},{10... | collective-permute-start | bytes 405512 | tf_op jit(solution)/shard_map/ppermute | solution.py:27
  20.0 6.5 %collective-permute-start.7 = (f32[33,8,128]{2,1,0:T(8,128)S(1)}, f32[33,8,128]{2,1,0:T(8,128)S(1)}, u32[]{:S(2)}, u32[]{:S(2)}) collective-permute-start(f32[33,8,128]{2,1,0:T(8,128)S(1)} %get-tuple-element.29), channel_id=1, source_target_pairs={{0,16},{8,24},{16,0},{24,8},{1,17},{9,25},{17,1},{25,9},{2,18},{10... | collective-permute-start | bytes 405512 | tf_op jit(solution)/shard_map/ppermute | solution.py:27
  20.5 6.0 %collective-permute-start.8 = (f32[33,8,128]{2,1,0:T(8,128)S(1)}, f32[33,8,128]{2,1,0:T(8,128)S(1)}, u32[]{:S(2)}, u32[]{:S(2)}) collective-permute-start(f32[33,8,128]{2,1,0:T(8,128)S(1)} %get-tuple-element.30), channel_id=1, source_target_pairs={{0,24},{8,16},{16,8},{24,0},{1,25},{9,17},{17,9},{25,1},{2,26},{10... | collective-permute-start | bytes 405512 | tf_op jit(solution)/shard_map/ppermute | solution.py:27
  42.0 6.0 %collective-permute-start.11 = (f32[8,4,8,128]{3,2,1,0:T(8,128)S(1)}, f32[8,4,8,128]{3,2,1,0:T(8,128)S(1)}, u32[]{:S(2)}, u32[]{:S(2)}) collective-permute-start(f32[8,4,8,128]{3,2,1,0:T(8,128)S(1)} %render.1.refs_0_), channel_id=1, source_target_pairs={{0,24},{8,16},{16,8},{24,0},{1,25},{9,17},{17,9},{25,1},{2,26},{10... | collective-permute-start | bytes 393224 | tf_op jit(solution)/shard_map/ppermute | solution.py:27
  43.4 5.9 %collective-permute-start.10 = (f32[8,4,8,128]{3,2,1,0:T(8,128)S(1)}, f32[8,4,8,128]{3,2,1,0:T(8,128)S(1)}, u32[]{:S(2)}, u32[]{:S(2)}) collective-permute-start(f32[8,4,8,128]{3,2,1,0:T(8,128)S(1)} %render.1.refs_0_), channel_id=1, source_target_pairs={{0,16},{8,24},{16,0},{24,8},{1,17},{9,25},{17,1},{25,9},{2,18},{10... | collective-permute-start | bytes 393224 | tf_op jit(solution)/shard_map/ppermute | solution.py:27
  44.0 5.4 %collective-permute-start.9 = (f32[8,4,8,128]{3,2,1,0:T(8,128)S(1)}, f32[8,4,8,128]{3,2,1,0:T(8,128)S(1)}, u32[]{:S(2)}, u32[]{:S(2)}) collective-permute-start(f32[8,4,8,128]{3,2,1,0:T(8,128)S(1)} %render.1.refs_0_), channel_id=1, source_target_pairs={{0,8},{8,0},{16,24},{24,16},{1,9},{9,1},{17,25},{25,17},{2,10},{10... | collective-permute-start | bytes 393224 | tf_op jit(solution)/shard_map/ppermute | solution.py:27

commit v3 on v2

--- a/solution.py
+++ b/solution.py
@@ -14,8 +14,11 @@
 VMEM = pl.BlockSpec(memory_space=pltpu.VMEM)
 SMEM = pl.BlockSpec(memory_space=pltpu.SMEM)
 f32 = jnp.float32
-MARCH_UNROLL = 32
+EARLY = 48
+LATE_UNROLL = 80
 CHUNKS = 4
+UNITS = 2
+PATTERN = (4, 2)
 
 
 def limit(mib):
@@ -209,84 +212,126 @@
 def render_kernel(nx, cell_count, *refs):
     refs = list(refs)
     pieces = [refs.pop(0) for _ in range(nx)]
-    sign_ref, table_ref, out_ref, low_ref, frac_ref, tab_ref = refs
+    sign_ref, table_ref, out_ref, low_ref, lowf_ref, frac_ref, tab_ref, part_ref, late_ref = refs
     planes, rows, cols = pieces[0].shape
     depth = planes - 1
-    bins = table_ref.shape[-1]
-    views = sign_ref.shape[0]
+    count, bins = table_ref.shape
+    views = count // 4
     depth_total = depth * nx
     me = lax.axis_index("gx")
     squares = pieces[0][depth, pl.ds(0, SUB), :]
     for piece in pieces[1:]:
         squares = squares + piece[depth, pl.ds(0, SUB), :]
     energy = jnp.sum(squares, keepdims=True) / cell_count
-    scale = -0.25 / (energy + 1e-06)
-    scale = jnp.broadcast_to(scale, (SUB, cols))
+    scale = jnp.broadcast_to(-0.25 / (energy + 1e-06), (SUB, cols))
     for k in range(nx):
         base = jnp.bitwise_xor(me, k) * depth
 
         def classify(x, carry):
-            for p in range(rows // SUB):
-                part = pieces[k][x, pl.ds(p * SUB, SUB), :] * scale
-                coord = (bins - 1) / (1.0 + jnp.exp(-part))
-                low = coord.astype(jnp.int32)
-                low_ref[base + x, pl.ds(p * SUB, SUB), :] = low
-                frac_ref[base + x, pl.ds(p * SUB, SUB), :] = coord - low.astype(f32)
+            part = pieces[k][x] * scale
+            coord = (bins - 1) / (1.0 + jnp.exp(-part))
+            low = coord.astype(jnp.int32)
+            low_ref[base + x] = low
+            lowf_ref[base + x] = low.astype(f32)
+            frac_ref[base + x] = coord - low.astype(f32)
             return carry
 
         lax.fori_loop(0, depth, classify, 0, unroll=8)
 
-    table = table_ref[...]
-    lane = lax.broadcasted_iota(jnp.int32, table.shape, 1)
-    row = lax.broadcasted_iota(jnp.int32, table.shape, 0)
-    factor = -3.0 / depth_total * math.log2(math.e)
-    table = jnp.where(lax.rem(row, 4) == 3, table * factor, table)
-    step = jnp.where(lane == bins - 1, 0.0, pltpu.roll(table, bins - 1, 1) - table)
-    tab_ref[0] = table
-    tab_ref[1] = step
-
-    for p in range(rows // SUB):
-
-        def view_body(v, carry):
-            forward = sign_ref[v] == 0
-            start = jnp.where(forward, 0, depth_total - 1)
-            stride = jnp.where(forward, 1, -1)
-            values = [
-                jnp.broadcast_to(tab_ref[0, pl.ds(v * 4 + c, 1), :], (SUB, bins)) for c in range(4)
-            ]
-            steps = [
-                jnp.broadcast_to(tab_ref[1, pl.ds(v * 4 + c, 1), :], (SUB, bins)) for c in range(4)
-            ]
-
-            def march(i, state):
-                light, total, red, green, blue = state
-                x = start + stride * i
-                low = low_ref[x, pl.ds(p * SUB, SUB), :]
-                frac = frac_ref[x, pl.ds(p * SUB, SUB), :]
-
-                def look(c):
-                    return lookup(values[c], low) + frac * lookup(steps[c], low)
-
-                exponent = look(3)
-                through = jnp.exp2(exponent)
-                weight = light * (1.0 - through)
-                return (
-                    light * through,
-                    total + exponent,
-                    red + weight * look(0),
-                    green + weight * look(1),
-                    blue + weight * look(2),
-                )
-
-            zero = jnp.zeros((SUB, cols), f32)
-            _, total, red, green, blue = lax.fori_loop(
-                0, depth_total, march, (jnp.ones((SUB, cols), f32), zero, zero, zero, zero), unroll=MARCH_UNROLL
-            )
-            for c, value in enumerate((red, green, blue, 1.0 - jnp.exp2(total))):
-                out_ref[v, c, pl.ds(p * SUB, SUB), :] = value
-            return carry
-
-        lax.fori_loop(0, views, view_body, 0)
+    view = lax.broadcasted_iota(jnp.int32, (views, bins), 0)
+    lane = lax.broadcasted_iota(jnp.int32, (views, bins), 1)
+    side = jnp.zeros((views, bins), f32)
+    for v in range(views):
+        side = jnp.where(view == v, jnp.where(sign_ref[v] == 0, -1.0, 1.0), side)
+    factor = 3.0 / depth_total * math.log2(math.e)
+    tables = [table_ref[pl.ds(c, views, stride=4), :] for c in range(4)]
+    tables[3] = tables[3] * (side * factor)
+    tables += [jnp.where(lane == bins - 1, 0.0, pltpu.roll(t, bins - 1, 1) - t) for t in tables]
+    table = jnp.concatenate(tables, axis=0)
+    tab_ref[...] = table
+    high = table.astype(jnp.bfloat16)
+    rest = (table - high.astype(f32)).astype(jnp.bfloat16)
+    tall = jnp.concatenate([high, rest], axis=0)
+    wide = jnp.concatenate([high, rest], axis=1)
+    packed = 2 * SUB
+    level = lax.broadcasted_iota(jnp.int32, (packed, cols), 0).astype(f32)
+    levels = [(level + float(g * packed)).astype(jnp.bfloat16) for g in range(bins // packed)]
+    one = jnp.ones((packed, cols), jnp.bfloat16)
+    nil = jnp.zeros((packed, cols), jnp.bfloat16)
+    split = EARLY
+    steps = (depth_total - split) // LATE_UNROLL
+    early_unroll = split // steps
+    width = 2
+
+    def advance(state, look):
+        total, light, *colour = state
+        total = total + look(3)
+        after = jnp.exp2(total)
+        weight = light - after
+        return (total, after, *[old + weight * look(c) for c, old in enumerate(colour)])
+
+    zero = jnp.zeros((SUB, cols), f32)
+    start = (zero, jnp.ones((SUB, cols), f32), zero, zero, zero)
+
+    def unit(n, carry):
+        spread = [
+            jnp.broadcast_to(tab_ref[pl.ds(c * views + n, 1), :], (SUB, bins)) for c in range(8)
+        ]
+
+        def march(i, states):
+            early, late = states
+            for u in range(0, LATE_UNROLL, width):
+                columns = []
+                for r in range(width):
+                    at = lowf_ref[split + i * LATE_UNROLL + u + r, pl.ds(n, 1), :]
+                    at = jnp.broadcast_to(at, (packed, cols)).astype(jnp.bfloat16)
+                    columns.append(
+                        jnp.concatenate([jnp.where(at == l, one, nil) for l in levels], axis=0)
+                    )
+                chosen = jnp.concatenate(columns, axis=1)
+                if u // width % PATTERN[0] < PATTERN[1]:
+                    looked = jnp.dot(tall, chosen, preferred_element_type=f32)
+                    looked = looked[: 2 * count] + looked[2 * count :]
+                else:
+                    chosen = jnp.concatenate([chosen, chosen], axis=0)
+                    looked = jnp.dot(wide, chosen, preferred_element_type=f32)
+                for r in range(width):
+                    frac = frac_ref[split + i * LATE_UNROLL + u + r, pl.ds(n, 1), :]
+                    frac = jnp.broadcast_to(frac, (views, cols))
+                    cells = looked[:, r * cols : (r + 1) * cols]
+                    late = advance(
+                        late,
+                        lambda c: cells[c * views : (c + 1) * views]
+                        + frac * cells[count + c * views : count + (c + 1) * views],
+                    )
+                    first = (u + r) * early_unroll // LATE_UNROLL
+                    stop = (u + r + 1) * early_unroll // LATE_UNROLL
+                    for e in range(first, stop):
+                        x = i * early_unroll + e
+                        low = low_ref[x]
+                        part = frac_ref[x]
+                        early = advance(
+                            early,
+                            lambda c: lookup(spread[c], low) + part * lookup(spread[4 + c], low),
+                        )
+            return early, late
+
+        early, late = lax.fori_loop(0, steps, march, (start, start))
+        for s, value in enumerate((early[0], *early[2:])):
+            part_ref[s, n] = value
+        for s, value in enumerate((late[0], *late[2:])):
+            late_ref[s, :, pl.ds(n, 1), :] = value[:, None, :]
+        return carry
+
+    lax.fori_loop(0, SUB, unit, 0, unroll=UNITS)
+    for v in range(views):
+        total = part_ref[0, v]
+        before = jnp.exp2(total)
+        left = jnp.exp2(-jnp.abs(total + late_ref[0, v]))
+        turn = jnp.where(sign_ref[v] == 0, 1.0, -left)
+        for c in range(3):
+            out_ref[v, c] = (part_ref[1 + c, v] + before * late_ref[1 + c, v]) * turn
+        out_ref[v, 3] = 1.0 - left
 
 
 def assemble_kernel(nx, *refs):
@@ -308,7 +353,7 @@
     sizes = tuple(lax.axis_size(a) for a in AXES)
     nx = sizes[0]
     assert all(n & (n - 1) == 0 for n in sizes)
-    assert cols == LANES and bins == LANES and rows % (SUB * nx) == 0
+    assert cols == LANES and bins == LANES and rows == SUB * nx and (views, channels) == (SUB, 4)
     assert depth * (rows // SUB) % LANES == 0
     cell_count = depth * rows * cols * math.prod(sizes)
     counts = tuple(min(n - 1, 2) for n in sizes)
@@ -394,7 +439,10 @@
         scratch_shapes=[
             pltpu.VMEM((depth * nx, part_rows, cols), jnp.int32),
             pltpu.VMEM((depth * nx, part_rows, cols), f32),
-            pltpu.VMEM((2, views * channels, bins), f32),
+            pltpu.VMEM((depth * nx, part_rows, cols), f32),
+            pltpu.VMEM((2 * channels * views, bins), f32),
+            pltpu.VMEM((channels, views, part_rows, cols), f32),
+            pltpu.VMEM((channels, views, part_rows, cols), f32),
         ],
         compiler_params=limit(8),
         name="render",

time: 50.3 us -> 41.4 us (0.82)
  Pallas kernels: 18.9 us -> 9.96 us
    pallas_call x1, Pallas kernels: 15.4 us -> 6.49 us  [on_device(): pl.pallas_call(functools.partial(render_kernel, nx, cell_count), out_shap...]
where the time goes in v3:
time: 41.4 us; the launch traced here: 41.2 us
  starting transfers between devices  16.2 us (39%)
  waiting for transfers between devices  13.6 us (33%)
  Pallas kernels  9.96 us (24%)
  local copies, waits for them, and re-layouts  1.42 us (3%)
    ppermute x10, waiting for transfers between devices, swap(): return lax.ppermute(x, axis, [(i, i ^ bit_mask) for i in range(n)])  13.5 us
    ppermute x10, starting transfers between devices, swap(): return lax.ppermute(x, axis, [(i, i ^ bit_mask) for i in range(n)])  12.2 us
    pallas_call x1, Pallas kernels, on_device(): pl.pallas_call(functools.partial(render_kernel, nx, cell_count), out_shap...  6.49 us
    ppermute x2, starting transfers between devices, swap_across(): lax.ppermute(x, axis, [(i, (i + 1) % n if i % 2 else (i - 1) % n) for i i...  3.97 us
    pallas_call x1, Pallas kernels, on_device(): pl.pallas_call(functools.partial(q_kernel, sizes, counts, attached, len(e...  1.58 us
    unnamed x8, local copies, waits for them, and re-layouts  1.42 us
    pallas_call x1, Pallas kernels, on_device(): pl.pallas_call(functools.partial(faces_kernel, sizes, counts), out_shape=...  1.06 us
  transfers between devices with their start and end apart: 12, of which 6 were waited for; matrix products, arithmetic and copies ran while one was open for 0% of the time, Pallas kernels for 0%

profile of v3, /device:TPU:0, one launch (start us, length us, event | category | flops | bytes accessed | tf_op | source)
XLA Modules:
  0.0 41.2 jit_solution(15164630411781844165)
XLA Ops:
  0.0 1.4 %copy-done = f32[3,32,32,128]{3,2,1,0:T(8,128)S(1)} copy-done((f32[3,32,32,128]{3,2,1,0:T(8,128)S(1)}, f32[3,32,32,128]{3,2,1,0:T(8,128)}, u32[]{:S(2)}) %copy-start) | copy-done | bytes 1572888
  1.4 1.1 %faces.1 = (f32[3,32,128]{2,1,0:T(8,128)S(1)}, f32[3,32,128]{2,1,0:T(8,128)S(1)}, f32[3,32,128]{2,1,0:T(8,128)S(1)}, f32[3,32,128]{2,1,0:T(8,128)S(1)}, f32[4,8,128]{2,1,0:T(8,128)S(1)}, /*index=5*/f32[8,128]{1,0:T(8,128)S(1)}) custom-call(f32[3,32,32,128]{3,2,1,0:T(8,128)S(1)} %copy-done), custom_call_target="tpu_custom_call" | custom-call | tf_op jit(solution)/shard_map/faces/pallas_call | solution.py:367
  2.5 0.6 %collective-permute-start.2 = (f32[4,8,128]{2,1,0:T(8,128)S(1)}, f32[4,8,128]{2,1,0:T(8,128)S(1)}, u32[]{:S(2)}, u32[]{:S(2)}) collective-permute-start(f32[4,8,128]{2,1,0:T(8,128)S(1)} %get-tuple-element.23), channel_id=1, source_target_pairs={{0,1},{1,0},{2,3},{3,2},{4,5},{5,4},{6,7},{7,6},{8,9},{9,8},{10,11... | collective-permute-start | bytes 49160 | tf_op jit(solution)/shard_map/ppermute | solution.py:30
  3.0 0.8 %collective-permute-done.2.refs_4_ = f32[4,8,128]{2,1,0:T(8,128)S(1)} collective-permute-done((f32[4,8,128]{2,1,0:T(8,128)S(1)}, f32[4,8,128]{2,1,0:T(8,128)S(1)}, u32[]{:S(2)}, u32[]{:S(2)}) %collective-permute-start.2) | collective-permute-done | bytes 16416 | tf_op jit(solution)/shard_map/ppermute | solution.py:30
  3.9 3.0 %collective-permute-start.3 = (f32[4,32,128]{2,1,0:T(8,128)S(1)}, f32[4,32,128]{2,1,0:T(8,128)S(1)}, u32[]{:S(2)}, u32[]{:S(2)}) collective-permute-start(f32[4,32,128]{2,1,0:T(8,128)S(1)} %get-tuple-element.24), channel_id=1, source_target_pairs={{0,2},{2,0},{4,6},{6,4},{1,3},{3,1},{5,7},{7,5},{8,10},{10,8},{12,... | collective-permute-start | bytes 196616 | tf_op jit(solution)/shard_map/ppermute | solution.py:30
  6.9 2.5 %collective-permute-start.4 = (f32[4,32,128]{2,1,0:T(8,128)S(1)}, f32[4,32,128]{2,1,0:T(8,128)S(1)}, u32[]{:S(2)}, u32[]{:S(2)}) collective-permute-start(f32[4,32,128]{2,1,0:T(8,128)S(1)} %get-tuple-element.25), channel_id=1, source_target_pairs={{0,6},{2,4},{4,2},{6,0},{1,7},{3,5},{5,3},{7,1},{8,14},{10,12},{12... | collective-permute-start | bytes 196616 | tf_op jit(solution)/shard_map/ppermute | solution.py:35
  9.3 1.5 %collective-permute-start = (f32[3,32,128]{2,1,0:T(8,128)S(1)}, f32[3,32,128]{2,1,0:T(8,128)S(1)}, u32[]{:S(2)}, u32[]{:S(2)}) collective-permute-start(f32[3,32,128]{2,1,0:T(8,128)S(1)} %get-tuple-element.18), channel_id=1, source_target_pairs={{0,8},{8,0},{16,24},{24,16},{1,9},{9,1},{17,25},{25,17},{2,10},{10... | collective-permute-start | bytes 147464 | tf_op jit(solution)/shard_map/ppermute | solution.py:30
  10.8 1.5 %collective-permute-start.1 = (f32[3,32,128]{2,1,0:T(8,128)S(1)}, f32[3,32,128]{2,1,0:T(8,128)S(1)}, u32[]{:S(2)}, u32[]{:S(2)}) collective-permute-start(f32[3,32,128]{2,1,0:T(8,128)S(1)} %get-tuple-element.19), channel_id=1, source_target_pairs={{0,24},{8,16},{16,8},{24,0},{1,25},{9,17},{17,9},{25,1},{2,26},{10... | collective-permute-start | bytes 147464 | tf_op jit(solution)/shard_map/ppermute | solution.py:35
  12.3 0.1 collective-permute-start.5
  12.4 4.4 %collective-permute-done.5.refs_6_ = f32[8,128]{1,0:T(8,128)S(1)} collective-permute-done((f32[8,128]{1,0:T(8,128)S(1)}, f32[8,128]{1,0:T(8,128)S(1)}, u32[]{:S(2)}, u32[]{:S(2)}) %collective-permute-start.5) | collective-permute-done | bytes 4128 | tf_op jit(solution)/shard_map/ppermute | solution.py:30
  16.8 0.0 collective-permute-done.refs_0_
  16.8 0.0 collective-permute-done.1.refs_1_
  16.8 0.0 collective-permute-done.3.refs_2_
  16.8 0.0 collective-permute-done.4.refs_3_
  16.9 0.0 copy-done.1
  16.9 1.6 %q.1 = (f32[33,8,128]{2,1,0:T(8,128)S(1)}, f32[33,8,128]{2,1,0:T(8,128)S(1)}, f32[33,8,128]{2,1,0:T(8,128)S(1)}, f32[33,8,128]{2,1,0:T(8,128)S(1)}) custom-call(f32[3,32,32,128]{3,2,1,0:T(8,128)S(1)} %copy-done.1, f32[3,32,128]{2,1,0:T(8,128)S(1)} %collective-permute-done.refs_0_, f32[3,32,128]{2,1,0:T(8,128)S(1)} %collective-permute-done.1.refs_1_, ...), custom_call_target="tpu_custom_call" | custom-call | tf_op jit(solution)/shard_map/q/pallas_call | solution.py:418
  18.5 1.6 %collective-permute-start.6 = (f32[33,8,128]{2,1,0:T(8,128)S(1)}, f32[33,8,128]{2,1,0:T(8,128)S(1)}, u32[]{:S(2)}, u32[]{:S(2)}) collective-permute-start(f32[33,8,128]{2,1,0:T(8,128)S(1)} %get-tuple-element.28), channel_id=1, source_target_pairs={{0,8},{8,0},{16,24},{24,16},{1,9},{9,1},{17,25},{25,17},{2,10},{10... | collective-permute-start | bytes 405512 | tf_op jit(solution)/shard_map/ppermute | solution.py:30
  20.0 0.5 %collective-permute-start.7 = (f32[33,8,128]{2,1,0:T(8,128)S(1)}, f32[33,8,128]{2,1,0:T(8,128)S(1)}, u32[]{:S(2)}, u32[]{:S(2)}) collective-permute-start(f32[33,8,128]{2,1,0:T(8,128)S(1)} %get-tuple-element.29), channel_id=1, source_target_pairs={{0,16},{8,24},{16,0},{24,8},{1,17},{9,25},{17,1},{25,9},{2,18},{10... | collective-permute-start | bytes 405512 | tf_op jit(solution)/shard_map/ppermute | solution.py:30
  20.5 1.5 %collective-permute-start.8 = (f32[33,8,128]{2,1,0:T(8,128)S(1)}, f32[33,8,128]{2,1,0:T(8,128)S(1)}, u32[]{:S(2)}, u32[]{:S(2)}) collective-permute-start(f32[33,8,128]{2,1,0:T(8,128)S(1)} %get-tuple-element.30), channel_id=1, source_target_pairs={{0,24},{8,16},{16,8},{24,0},{1,25},{9,17},{17,9},{25,1},{2,26},{10... | collective-permute-start | bytes 405512 | tf_op jit(solution)/shard_map/ppermute | solution.py:30
  22.0 2.6 %collective-permute-done.6.refs_1_ = f32[33,8,128]{2,1,0:T(8,128)S(1)} collective-permute-done((f32[33,8,128]{2,1,0:T(8,128)S(1)}, f32[33,8,128]{2,1,0:T(8,128)S(1)}, u32[]{:S(2)}, u32[]{:S(2)}) %collective-permute-start.6) | collective-permute-done | bytes 135200 | tf_op jit(solution)/shard_map/ppermute | solution.py:30
  24.6 1.9 %collective-permute-done.7.refs_2_ = f32[33,8,128]{2,1,0:T(8,128)S(1)} collective-permute-done((f32[33,8,128]{2,1,0:T(8,128)S(1)}, f32[33,8,128]{2,1,0:T(8,128)S(1)}, u32[]{:S(2)}, u32[]{:S(2)}) %collective-permute-start.7) | collective-permute-done | bytes 135200 | tf_op jit(solution)/shard_map/ppermute | solution.py:30
  26.5 0.0 collective-permute-done.8.refs_3_
  26.5 0.0 copy-done.2
  26.5 0.0 copy-done.3
  26.5 6.5 %render.1.refs_0_ = f32[8,4,8,128]{3,2,1,0:T(8,128)S(1)} custom-call(f32[33,8,128]{2,1,0:T(8,128)S(1)} %get-tuple-element.27.refs_0_, f32[33,8,128]{2,1,0:T(8,128)S(1)} %collective-permute-done.6.refs_1_, f32[33,8,128]{2,1,0:T(8,128)S(1)} %collective-permute-done.7.refs_2_, f32[33,8,128]{2,1,0:T(8,128)S(1)} %collective-permute-done.8.refs_3_, ...), custom_call_target="tpu_custom_call" | custom-call | tf_op jit(solution)/shard_map/render/pallas_call | solution.py:434
  33.0 1.4 %collective-permute-start.11 = (f32[8,4,8,128]{3,2,1,0:T(8,128)S(1)}, f32[8,4,8,128]{3,2,1,0:T(8,128)S(1)}, u32[]{:S(2)}, u32[]{:S(2)}) collective-permute-start(f32[8,4,8,128]{3,2,1,0:T(8,128)S(1)} %render.1.refs_0_), channel_id=1, source_target_pairs={{0,24},{8,16},{16,8},{24,0},{1,25},{9,17},{17,9},{25,1},{2,26},{10... | collective-permute-start | bytes 393224 | tf_op jit(solution)/shard_map/ppermute | solution.py:30
  34.5 0.5 %collective-permute-start.10 = (f32[8,4,8,128]{3,2,1,0:T(8,128)S(1)}, f32[8,4,8,128]{3,2,1,0:T(8,128)S(1)}, u32[]{:S(2)}, u32[]{:S(2)}) collective-permute-start(f32[8,4,8,128]{3,2,1,0:T(8,128)S(1)} %render.1.refs_0_), channel_id=1, source_target_pairs={{0,16},{8,24},{16,0},{24,8},{1,17},{9,25},{17,1},{25,9},{2,18},{10... | collective-permute-start | bytes 393224 | tf_op jit(solution)/shard_map/ppermute | solution.py:30
  35.0 1.6 %collective-permute-start.9 = (f32[8,4,8,128]{3,2,1,0:T(8,128)S(1)}, f32[8,4,8,128]{3,2,1,0:T(8,128)S(1)}, u32[]{:S(2)}, u32[]{:S(2)}) collective-permute-start(f32[8,4,8,128]{3,2,1,0:T(8,128)S(1)} %render.1.refs_0_), channel_id=1, source_target_pairs={{0,8},{8,0},{16,24},{24,16},{1,9},{9,1},{17,25},{25,17},{2,10},{10... | collective-permute-start | bytes 393224 | tf_op jit(solution)/shard_map/ppermute | solution.py:30
  36.6 2.5 %collective-permute-done.11.refs_3_ = f32[8,4,8,128]{3,2,1,0:T(8,128)S(1)} collective-permute-done((f32[8,4,8,128]{3,2,1,0:T(8,128)S(1)}, f32[8,4,8,128]{3,2,1,0:T(8,128)S(1)}, u32[]{:S(2)}, u32[]{:S(2)}) %collective-permute-start.11) | collective-permute-done | bytes 131104 | tf_op jit(solution)/shard_map/ppermute | solution.py:30
  39.1 1.3 %collective-permute-done.10.refs_2_ = f32[8,4,8,128]{3,2,1,0:T(8,128)S(1)} collective-permute-done((f32[8,4,8,128]{3,2,1,0:T(8,128)S(1)}, f32[8,4,8,128]{3,2,1,0:T(8,128)S(1)}, u32[]{:S(2)}, u32[]{:S(2)}) %collective-permute-start.10) | collective-permute-done | bytes 131104 | tf_op jit(solution)/shard_map/ppermute | solution.py:30
  40.4 0.0 collective-permute-done.9.refs_1_
  40.4 0.8 %assemble.1 = f32[8,4,32,128]{3,2,1,0:T(8,128)} custom-call(f32[8,4,8,128]{3,2,1,0:T(8,128)S(1)} %render.1.refs_0_, f32[8,4,8,128]{3,2,1,0:T(8,128)S(1)} %collective-permute-done.9.refs_1_, f32[8,4,8,128]{3,2,1,0:T(8,128)S(1)} %collective-permute-done.10.refs_2_, f32[8,4,8,128]{3,2,1,0:T(8,128)S(1)} %collective-permute-done.11.refs_3_), custom_call_target="tpu_custom_call" | custom-call | tf_op jit(solution)/shard_map/assemble/pallas_call | solution.py:453
  (6 shorter events, 0.0 us)
Async XLA Ops:
  0.0 1.4 %copy-start = (f32[3,32,32,128]{3,2,1,0:T(8,128)S(1)}, f32[3,32,32,128]{3,2,1,0:T(8,128)}, u32[]{:S(2)}) copy-start(f32[3,32,32,128]{3,2,1,0:T(8,128)} %v_hbm.3) | copy-start | bytes 4718596
  1.4 15.4 %copy-start.1 = (f32[3,32,32,128]{3,2,1,0:T(8,128)S(1)}, f32[3,32,32,128]{3,2,1,0:T(8,128)}, u32[]{:S(2)}) copy-start(f32[3,32,32,128]{3,2,1,0:T(8,128)} %v_hbm.3) | copy-start | bytes 4718596
  1.4 25.1 %copy-start.2 = (f32[8,4,128]{2,1,0:T(4,128)S(1)}, f32[8,4,128]{2,1,0:T(4,128)}, u32[]{:S(2)}) copy-start(f32[8,4,128]{2,1,0:T(4,128)} %param.5) | copy-start | bytes 49156
  1.4 25.1 %copy-start.3 = (s32[8]{0:T(128)S(1)}, s32[8]{0:T(128)}, u32[]{:S(2)}) copy-start(s32[8]{0:T(128)} %refs_4_.1) | copy-start | bytes 100
  2.5 1.4 %collective-permute-start.2 = (f32[4,8,128]{2,1,0:T(8,128)S(1)}, f32[4,8,128]{2,1,0:T(8,128)S(1)}, u32[]{:S(2)}, u32[]{:S(2)}) collective-permute-start(f32[4,8,128]{2,1,0:T(8,128)S(1)} %get-tuple-element.23), channel_id=1, source_target_pairs={{0,1},{1,0},{2,3},{3,2},{4,5},{5,4},{6,7},{7,6},{8,9},{9,8},{10,11... | collective-permute-start | bytes 49160 | tf_op jit(solution)/shard_map/ppermute | solution.py:30
  3.9 12.9 %collective-permute-start.3 = (f32[4,32,128]{2,1,0:T(8,128)S(1)}, f32[4,32,128]{2,1,0:T(8,128)S(1)}, u32[]{:S(2)}, u32[]{:S(2)}) collective-permute-start(f32[4,32,128]{2,1,0:T(8,128)S(1)} %get-tuple-element.24), channel_id=1, source_target_pairs={{0,2},{2,0},{4,6},{6,4},{1,3},{3,1},{5,7},{7,5},{8,10},{10,8},{12,... | collective-permute-start | bytes 196616 | tf_op jit(solution)/shard_map/ppermute | solution.py:30
  6.9 10.0 %collective-permute-start.4 = (f32[4,32,128]{2,1,0:T(8,128)S(1)}, f32[4,32,128]{2,1,0:T(8,128)S(1)}, u32[]{:S(2)}, u32[]{:S(2)}) collective-permute-start(f32[4,32,128]{2,1,0:T(8,128)S(1)} %get-tuple-element.25), channel_id=1, source_target_pairs={{0,6},{2,4},{4,2},{6,0},{1,7},{3,5},{5,3},{7,1},{8,14},{10,12},{12... | collective-permute-start | bytes 196616 | tf_op jit(solution)/shard_map/ppermute | solution.py:35
  9.3 7.5 %collective-permute-start = (f32[3,32,128]{2,1,0:T(8,128)S(1)}, f32[3,32,128]{2,1,0:T(8,128)S(1)}, u32[]{:S(2)}, u32[]{:S(2)}) collective-permute-start(f32[3,32,128]{2,1,0:T(8,128)S(1)} %get-tuple-element.18), channel_id=1, source_target_pairs={{0,8},{8,0},{16,24},{24,16},{1,9},{9,1},{17,25},{25,17},{2,10},{10... | collective-permute-start | bytes 147464 | tf_op jit(solution)/shard_map/ppermute | solution.py:30
  10.8 6.0 %collective-permute-start.1 = (f32[3,32,128]{2,1,0:T(8,128)S(1)}, f32[3,32,128]{2,1,0:T(8,128)S(1)}, u32[]{:S(2)}, u32[]{:S(2)}) collective-permute-start(f32[3,32,128]{2,1,0:T(8,128)S(1)} %get-tuple-element.19), channel_id=1, source_target_pairs={{0,24},{8,16},{16,8},{24,0},{1,25},{9,17},{17,9},{25,1},{2,26},{10... | collective-permute-start | bytes 147464 | tf_op jit(solution)/shard_map/ppermute | solution.py:35
  12.3 4.5 %collective-permute-start.5 = (f32[8,128]{1,0:T(8,128)S(1)}, f32[8,128]{1,0:T(8,128)S(1)}, u32[]{:S(2)}, u32[]{:S(2)}) collective-permute-start(f32[8,128]{1,0:T(8,128)S(1)} %get-tuple-element.26.refs_5_), channel_id=1, source_target_pairs={{0,4},{2,6},{4,0},{6,2},{1,5},{3,7},{5,1},{7,3},{8,12},{10,14},{12... | collective-permute-start | bytes 12296 | tf_op jit(solution)/shard_map/ppermute | solution.py:30
  18.5 6.1 %collective-permute-start.6 = (f32[33,8,128]{2,1,0:T(8,128)S(1)}, f32[33,8,128]{2,1,0:T(8,128)S(1)}, u32[]{:S(2)}, u32[]{:S(2)}) collective-permute-start(f32[33,8,128]{2,1,0:T(8,128)S(1)} %get-tuple-element.28), channel_id=1, source_target_pairs={{0,8},{8,0},{16,24},{24,16},{1,9},{9,1},{17,25},{25,17},{2,10},{10... | collective-permute-start | bytes 405512 | tf_op jit(solution)/shard_map/ppermute | solution.py:30
  20.0 6.5 %collective-permute-start.7 = (f32[33,8,128]{2,1,0:T(8,128)S(1)}, f32[33,8,128]{2,1,0:T(8,128)S(1)}, u32[]{:S(2)}, u32[]{:S(2)}) collective-permute-start(f32[33,8,128]{2,1,0:T(8,128)S(1)} %get-tuple-element.29), channel_id=1, source_target_pairs={{0,16},{8,24},{16,0},{24,8},{1,17},{9,25},{17,1},{25,9},{2,18},{10... | collective-permute-start | bytes 405512 | tf_op jit(solution)/shard_map/ppermute | solution.py:30
  20.5 6.0 %collective-permute-start.8 = (f32[33,8,128]{2,1,0:T(8,128)S(1)}, f32[33,8,128]{2,1,0:T(8,128)S(1)}, u32[]{:S(2)}, u32[]{:S(2)}) collective-permute-start(f32[33,8,128]{2,1,0:T(8,128)S(1)} %get-tuple-element.30), channel_id=1, source_target_pairs={{0,24},{8,16},{16,8},{24,0},{1,25},{9,17},{17,9},{25,1},{2,26},{10... | collective-permute-start | bytes 405512 | tf_op jit(solution)/shard_map/ppermute | solution.py:30
  33.0 6.0 %collective-permute-start.11 = (f32[8,4,8,128]{3,2,1,0:T(8,128)S(1)}, f32[8,4,8,128]{3,2,1,0:T(8,128)S(1)}, u32[]{:S(2)}, u32[]{:S(2)}) collective-permute-start(f32[8,4,8,128]{3,2,1,0:T(8,128)S(1)} %render.1.refs_0_), channel_id=1, source_target_pairs={{0,24},{8,16},{16,8},{24,0},{1,25},{9,17},{17,9},{25,1},{2,26},{10... | collective-permute-start | bytes 393224 | tf_op jit(solution)/shard_map/ppermute | solution.py:30
  34.5 5.9 %collective-permute-start.10 = (f32[8,4,8,128]{3,2,1,0:T(8,128)S(1)}, f32[8,4,8,128]{3,2,1,0:T(8,128)S(1)}, u32[]{:S(2)}, u32[]{:S(2)}) collective-permute-start(f32[8,4,8,128]{3,2,1,0:T(8,128)S(1)} %render.1.refs_0_), channel_id=1, source_target_pairs={{0,16},{8,24},{16,0},{24,8},{1,17},{9,25},{17,1},{25,9},{2,18},{10... | collective-permute-start | bytes 393224 | tf_op jit(solution)/shard_map/ppermute | solution.py:30
  35.0 5.3 %collective-permute-start.9 = (f32[8,4,8,128]{3,2,1,0:T(8,128)S(1)}, f32[8,4,8,128]{3,2,1,0:T(8,128)S(1)}, u32[]{:S(2)}, u32[]{:S(2)}) collective-permute-start(f32[8,4,8,128]{3,2,1,0:T(8,128)S(1)} %render.1.refs_0_), channel_id=1, source_target_pairs={{0,8},{8,0},{16,24},{24,16},{1,9},{9,1},{17,25},{25,17},{2,10},{10... | collective-permute-start | bytes 393224 | tf_op jit(solution)/shard_map/ppermute | solution.py:30

commit v4 on v3

--- a/solution.py
+++ b/solution.py
@@ -14,11 +14,9 @@
 VMEM = pl.BlockSpec(memory_space=pltpu.VMEM)
 SMEM = pl.BlockSpec(memory_space=pltpu.SMEM)
 f32 = jnp.float32
-EARLY = 48
-LATE_UNROLL = 80
+EARLY = 12
 CHUNKS = 4
-UNITS = 2
-PATTERN = (4, 2)
+UNITS = 8
 
 
 def limit(mib):
@@ -123,13 +121,12 @@
         out[comps, pl.ds(0, SUB), :] = total
 
 
-def q_kernel(sizes, counts, attached, extras, v_hbm, *refs):
+def q_kernel(sizes, counts, v_hbm, *refs):
     comps, depth, rows, cols = v_hbm.shape
     tiles = rows // SUB
     nx = sizes[0]
     refs = list(refs)
     halos = [[refs.pop(0) for _ in range(counts[a])] for a in range(3)]
-    extra = [refs.pop(0) for _ in range(extras)]
     outs, (padded, sem) = refs[:nx], refs[nx:]
     info = flags(sizes)
     copy = pltpu.make_async_copy(
@@ -154,13 +151,6 @@
             value = jnp.broadcast_to(value, (depth, cols))
             for x in range(depth):
                 padded[c, 1 + x, pl.ds(end, 1), :] = value[x : x + 1]
-    tile_sum = extra[0][...]
-    for t in extra[1:]:
-        tile_sum = tile_sum + t[...]
-    for near_far in halos[1][:attached]:
-        tile_sum = tile_sum + near_far[comps, pl.ds(0, SUB), :]
-    for out in outs:
-        out[depth, pl.ds(0, SUB), :] = tile_sum
     groups = depth * tiles // LANES
     lane = lax.broadcasted_iota(jnp.int32, (SUB, cols), 1)
     me = lax.axis_index("gx")
@@ -209,34 +199,61 @@
                 outs[k][x, pl.ds(p * SUB, SUB), :] = total
 
 
-def render_kernel(nx, cell_count, *refs):
+def column_kernel(attached, *refs):
+    faces, tiles, out = refs[:attached], refs[attached:-1], refs[-1]
+    total = tiles[0][...]
+    for t in tiles[1:]:
+        total = total + t[...]
+    for face in faces:
+        total = total + face[face.shape[0] - 1, pl.ds(0, SUB), :]
+    out[...] = total
+
+
+def seal_kernel(tiles, *refs):
+    total = refs[1][...]
+    for t in refs[2 : 1 + tiles]:
+        total = total + t[...]
+    out, sum_ref = refs[1 + tiles :]
+    out[out.shape[0] - 1, pl.ds(0, SUB), :] = total
+    sum_ref[...] = total
+
+
+def render_kernel(nx, cell_count, slabs, carried, earlier, *refs):
     refs = list(refs)
-    pieces = [refs.pop(0) for _ in range(nx)]
-    sign_ref, table_ref, out_ref, low_ref, lowf_ref, frac_ref, tab_ref, part_ref, late_ref = refs
-    planes, rows, cols = pieces[0].shape
-    depth = planes - 1
+    pieces = [refs.pop(0) for _ in slabs]
+    scalers = refs.pop(0)
+    states = [refs.pop(0) for _ in earlier]
+    sign_ref, table_ref = refs.pop(0), refs.pop(0)
+    last = len(slabs) + sum(len(e) for e in earlier) == nx
+    out_ref = refs.pop(0)
+    scale_ref = refs.pop(0) if carried else None
+    low_ref, lowf_ref, frac_ref, tab_ref, part_ref, late_ref = refs
+    _, rows, cols = pieces[0].shape
+    depth = low_ref.shape[0] // len(slabs)
     count, bins = table_ref.shape
     views = count // 4
     depth_total = depth * nx
-    me = lax.axis_index("gx")
-    squares = pieces[0][depth, pl.ds(0, SUB), :]
-    for piece in pieces[1:]:
-        squares = squares + piece[depth, pl.ds(0, SUB), :]
-    energy = jnp.sum(squares, keepdims=True) / cell_count
-    scale = jnp.broadcast_to(-0.25 / (energy + 1e-06), (SUB, cols))
-    for k in range(nx):
-        base = jnp.bitwise_xor(me, k) * depth
+    if carried:
+        squares = scalers[...]
+        if nx > 1:
+            squares = squares + pieces[-1][depth, pl.ds(0, SUB), :]
+        energy = jnp.sum(squares, keepdims=True) / cell_count
+        scale = jnp.broadcast_to(-0.25 / (energy + 1e-06), (SUB, cols))
+        scale_ref[...] = scale
+    else:
+        scale = scalers[...]
+    for p, piece in enumerate(pieces):
 
         def classify(x, carry):
-            part = pieces[k][x] * scale
+            part = piece[x] * scale
             coord = (bins - 1) / (1.0 + jnp.exp(-part))
             low = coord.astype(jnp.int32)
-            low_ref[base + x] = low
-            lowf_ref[base + x] = low.astype(f32)
-            frac_ref[base + x] = coord - low.astype(f32)
+            low_ref[p * depth + x] = low
+            lowf_ref[p * depth + x] = low.astype(f32)
+            frac_ref[p * depth + x] = coord - low.astype(f32)
             return carry
 
-        lax.fori_loop(0, depth, classify, 0, unroll=8)
+        lax.fori_loop(0, depth, classify, 0, unroll=16)
 
     view = lax.broadcasted_iota(jnp.int32, (views, bins), 0)
     lane = lax.broadcasted_iota(jnp.int32, (views, bins), 1)
@@ -258,10 +275,9 @@
     levels = [(level + float(g * packed)).astype(jnp.bfloat16) for g in range(bins // packed)]
     one = jnp.ones((packed, cols), jnp.bfloat16)
     nil = jnp.zeros((packed, cols), jnp.bfloat16)
-    split = EARLY
-    steps = (depth_total - split) // LATE_UNROLL
-    early_unroll = split // steps
     width = 2
+    early_steps = depth * EARLY // 32
+    late_steps = depth - early_steps
 
     def advance(state, look):
         total, light, *colour = state
@@ -273,64 +289,88 @@
     zero = jnp.zeros((SUB, cols), f32)
     start = (zero, jnp.ones((SUB, cols), f32), zero, zero, zero)
 
-    def unit(n, carry):
+    def unit(t, carry):
+        p, n = t // SUB, lax.rem(t, SUB)
+        base = p * depth
         spread = [
             jnp.broadcast_to(tab_ref[pl.ds(c * views + n, 1), :], (SUB, bins)) for c in range(8)
         ]
-
-        def march(i, states):
-            early, late = states
-            for u in range(0, LATE_UNROLL, width):
-                columns = []
-                for r in range(width):
-                    at = lowf_ref[split + i * LATE_UNROLL + u + r, pl.ds(n, 1), :]
-                    at = jnp.broadcast_to(at, (packed, cols)).astype(jnp.bfloat16)
-                    columns.append(
-                        jnp.concatenate([jnp.where(at == l, one, nil) for l in levels], axis=0)
+        early = late = start
+        done = 0
+        for u in range(0, late_steps, width):
+            columns = []
+            for r in range(width):
+                at = lowf_ref[base + early_steps + u + r, pl.ds(n, 1), :]
+                at = jnp.broadcast_to(at, (packed, cols)).astype(jnp.bfloat16)
+                columns.append(
+                    jnp.concatenate([jnp.where(at == l, one, nil) for l in levels], axis=0)
+                )
+            chosen = jnp.concatenate(columns, axis=1)
+            if u // width % 4 < 2:
+                looked = jnp.dot(tall, chosen, preferred_element_type=f32)
+                looked = looked[: 2 * count] + looked[2 * count :]
+            else:
+                chosen = jnp.concatenate([chosen, chosen], axis=0)
+                looked = jnp.dot(wide, chosen, preferred_element_type=f32)
+            for r in range(width):
+                frac = frac_ref[base + early_steps + u + r, pl.ds(n, 1), :]
+                frac = jnp.broadcast_to(frac, (views, cols))
+                cells = looked[:, r * cols : (r + 1) * cols]
+                late = advance(
+                    late,
+                    lambda c: cells[c * views : (c + 1) * views]
+                    + frac * cells[count + c * views : count + (c + 1) * views],
+                )
+                stop = (u + r + 1) * early_steps // late_steps
+                while done < stop:
+                    low = low_ref[base + done]
+                    part = frac_ref[base + done]
+                    early = advance(
+                        early,
+                        lambda c: lookup(spread[c], low) + part * lookup(spread[4 + c], low),
                     )
-                chosen = jnp.concatenate(columns, axis=1)
-                if u // width % PATTERN[0] < PATTERN[1]:
-                    looked = jnp.dot(tall, chosen, preferred_element_type=f32)
-                    looked = looked[: 2 * count] + looked[2 * count :]
-                else:
-                    chosen = jnp.concatenate([chosen, chosen], axis=0)
-                    looked = jnp.dot(wide, chosen, preferred_element_type=f32)
-                for r in range(width):
-                    frac = frac_ref[split + i * LATE_UNROLL + u + r, pl.ds(n, 1), :]
-                    frac = jnp.broadcast_to(frac, (views, cols))
-                    cells = looked[:, r * cols : (r + 1) * cols]
-                    late = advance(
-                        late,
-                        lambda c: cells[c * views : (c + 1) * views]
-                        + frac * cells[count + c * views : count + (c + 1) * views],
-                    )
-                    first = (u + r) * early_unroll // LATE_UNROLL
-                    stop = (u + r + 1) * early_unroll // LATE_UNROLL
-                    for e in range(first, stop):
-                        x = i * early_unroll + e
-                        low = low_ref[x]
-                        part = frac_ref[x]
-                        early = advance(
-                            early,
-                            lambda c: lookup(spread[c], low) + part * lookup(spread[4 + c], low),
-                        )
-            return early, late
-
-        early, late = lax.fori_loop(0, steps, march, (start, start))
+                    done += 1
         for s, value in enumerate((early[0], *early[2:])):
-            part_ref[s, n] = value
+            part_ref[p, s, n] = value
         for s, value in enumerate((late[0], *late[2:])):
-            late_ref[s, :, pl.ds(n, 1), :] = value[:, None, :]
+            late_ref[p, s, :, pl.ds(n, 1), :] = value[:, None, :]
         return carry
 
-    lax.fori_loop(0, SUB, unit, 0, unroll=UNITS)
+    lax.fori_loop(0, len(slabs) * SUB, unit, 0, unroll=UNITS)
+
+    def merged(p, v):
+        total = part_ref[p, 0, v]
+        before = jnp.exp2(total)
+        return [total + late_ref[p, 0, v]] + [
+            part_ref[p, s, v] + before * late_ref[p, s, v] for s in (1, 2, 3)
+        ]
+
+    if not last:
+        for p in range(len(slabs)):
+            for v in range(views):
+                for s, value in enumerate(merged(p, v)):
+                    out_ref[p, s, v] = value
+        return
+    me = lax.axis_index("gx")
+    names = [k for e in earlier for k in e] + list(slabs)
+    place = [jnp.bitwise_xor(me, k) for k in names]
+    ahead = [[jnp.where(place[j] < place[i], 1.0, 0.0) for j in range(nx)] for i in range(nx)]
     for v in range(views):
-        total = part_ref[0, v]
-        before = jnp.exp2(total)
-        left = jnp.exp2(-jnp.abs(total + late_ref[0, v]))
+        rays = [[st[p, s, v] for s in range(4)] for st, e in zip(states, earlier) for p in range(len(e))]
+        rays += [merged(p, v) for p in range(len(slabs))]
+        total = sum(ray[0] for ray in rays)
+        colour = [zero] * 3
+        for i in range(nx):
+            before = zero
+            for j in range(nx):
+                if j != i:
+                    before = before + ahead[i][j] * rays[j][0]
+            before = jnp.exp2(before)
+            colour = [old + before * rays[i][1 + c] for c, old in enumerate(colour)]
+        left = jnp.exp2(-jnp.abs(total))
         turn = jnp.where(sign_ref[v] == 0, 1.0, -left)
         for c in range(3):
-            out_ref[v, c] = (part_ref[1 + c, v] + before * late_ref[1 + c, v]) * turn
+            out_ref[v, c] = colour[c] * turn
         out_ref[v, 3] = 1.0 - left
 
 
@@ -412,13 +452,27 @@
         attached, extra = counts[1], [column]
     else:
         attached, extra = 0, [everyone(column, "gy")]
+    column = pl.pallas_call(
+        functools.partial(column_kernel, attached),
+        out_shape=tile,
+        in_specs=[VMEM] * (attached + len(extra)),
+        out_specs=VMEM,
+        compiler_params=limit(2),
+        name="column",
+    )(*y_halos[:attached], *extra)
+    tiles = [column]
+    for bit in range(nx.bit_length() - 2):
+        if bit:
+            tiles = [tiles[0] + tiles[1]]
+        tiles.append(swap(tiles[0], "gx", 1 << bit))
     part_rows = rows // nx
-    piece = jax.ShapeDtypeStruct((depth + 1, part_rows, cols), f32)
+    plain = jax.ShapeDtypeStruct((depth, part_rows, cols), f32)
+    sealed = jax.ShapeDtypeStruct((depth + 1, part_rows, cols), f32)
     halos = x_halos + y_halos + z_halos
     q_pieces = pl.pallas_call(
-        functools.partial(q_kernel, sizes, counts, attached, len(extra)),
-        out_shape=[piece] * nx,
-        in_specs=[ANY] + [VMEM] * (len(halos) + len(extra)),
+        functools.partial(q_kernel, sizes, counts),
+        out_shape=[sealed if k == nx - 1 else plain for k in range(nx)],
+        in_specs=[ANY] + [VMEM] * len(halos),
         out_specs=[VMEM] * nx,
         scratch_shapes=[
             pltpu.VMEM((comps, depth + 2, rows + 2 * SUB, cols), f32),
@@ -426,27 +480,51 @@
         ],
         compiler_params=limit(8),
         name="q",
-    )(velocity, *halos, *extra)
+    )(velocity, *halos)
+    *q_pieces, last_piece = q_pieces
+    last_piece, squares = pl.pallas_call(
+        functools.partial(seal_kernel, len(tiles)),
+        out_shape=[sealed, tile],
+        in_specs=[VMEM] * (1 + len(tiles)),
+        out_specs=[VMEM] * 2,
+        input_output_aliases={0: 0},
+        compiler_params=limit(2),
+        name="seal",
+    )(last_piece, *tiles)
+    q_pieces = [*q_pieces, last_piece]
     order = sorted(range(1, nx), key=lambda k: -k)
     got = {0: q_pieces[0]}
     for k in order:
         got[k] = swap(q_pieces[k], "gx", k)
-    image_piece = pl.pallas_call(
-        functools.partial(render_kernel, nx, cell_count),
-        out_shape=jax.ShapeDtypeStruct((views, channels, part_rows, cols), f32),
-        in_specs=[VMEM] * nx + [SMEM, VMEM],
-        out_specs=VMEM,
-        scratch_shapes=[
-            pltpu.VMEM((depth * nx, part_rows, cols), jnp.int32),
-            pltpu.VMEM((depth * nx, part_rows, cols), f32),
-            pltpu.VMEM((depth * nx, part_rows, cols), f32),
-            pltpu.VMEM((2 * channels * views, bins), f32),
-            pltpu.VMEM((channels, views, part_rows, cols), f32),
-            pltpu.VMEM((channels, views, part_rows, cols), f32),
-        ],
-        compiler_params=limit(8),
-        name="render",
-    )(*[got[k] for k in range(nx)], view_sign, transfer.reshape(views * channels, bins))
+    scale, states, earlier = squares, [], []
+    table = transfer.reshape(views * channels, bins)
+    rays = (channels, views, part_rows, cols)
+    for slabs in [[0] + order[:1]] + [[k] for k in order[1:]]:
+        carried = not earlier
+        last = len(slabs) + sum(len(e) for e in earlier) == nx
+        image = jax.ShapeDtypeStruct((views, channels, part_rows, cols), f32)
+        shapes = [image if last else jax.ShapeDtypeStruct((len(slabs), *rays), f32)]
+        out = pl.pallas_call(
+            functools.partial(render_kernel, nx, cell_count, slabs, carried, tuple(earlier)),
+            out_shape=shapes + [tile] * carried,
+            in_specs=[VMEM] * (len(slabs) + 1 + len(states)) + [SMEM, VMEM],
+            out_specs=[VMEM] * (1 + carried),
+            scratch_shapes=[
+                pltpu.VMEM((depth * len(slabs), part_rows, cols), jnp.int32),
+                pltpu.VMEM((depth * len(slabs), part_rows, cols), f32),
+                pltpu.VMEM((depth * len(slabs), part_rows, cols), f32),
+                pltpu.VMEM((2 * channels * views, bins), f32),
+                pltpu.VMEM((len(slabs), *rays), f32),
+                pltpu.VMEM((len(slabs), *rays), f32),
+            ],
+            compiler_params=limit(8),
+            name="render",
+        )(*[got[k] for k in slabs], scale, *states, view_sign, table)
+        if carried:
+            scale = out[1]
+        states.append(out[0])
+        earlier.append(tuple(slabs))
+    image_piece = states[-1]
     images = {0: image_piece}
     for k in order:
         images[k] = swap(image_piece, "gx", k)

time: 41.4 us -> 43.5 us (1.051)
  starting transfers between devices: 16.2 us -> 17.7 us
  Pallas kernels: 9.96 us -> 11.4 us
  waiting for transfers between devices: 13.6 us -> 12.8 us
    ppermute x10 -> x11, starting transfers between devices: 12.2 us -> 13.7 us  [swap(): return lax.ppermute(x, axis, [(i, i ^ bit_mask) for i in range(n)])]
    pallas_call x2 -> x6, Pallas kernels: 8.07 us -> 9.49 us  [the longest x3 7.9 us: on_device(): pl.pallas_call(functools.partial(render_kernel, nx, cell_count, slabs, ca...]
    ppermute x10 -> x11, waiting for transfers between devices: 13.5 us -> 12.8 us  [swap(): return lax.ppermute(x, axis, [(i, i ^ bit_mask) for i in range(n)])]
  transfers between devices with their start and end apart: 12 -> 13, of which waited for: 6 -> 7; matrix products, arithmetic and copies ran while one was open for 0% -> 0% of each run, Pallas kernels for 0% -> 17%
where the time goes in v4:
time: 43.5 us; the launch traced here: 43.3 us
  starting transfers between devices  17.7 us (41%)
  waiting for transfers between devices  12.8 us (29%)
  Pallas kernels  11.4 us (26%)
  local copies, waits for them, and re-layouts  1.42 us (3%)
    ppermute x11, starting transfers between devices, swap(): return lax.ppermute(x, axis, [(i, i ^ bit_mask) for i in range(n)])  13.7 us
    ppermute x11, waiting for transfers between devices, swap(): return lax.ppermute(x, axis, [(i, i ^ bit_mask) for i in range(n)])  12.8 us
    pallas_call x3, Pallas kernels, on_device(): pl.pallas_call(functools.partial(render_kernel, nx, cell_count, slabs, ca...  7.9 us
    ppermute x2, starting transfers between devices, swap_across(): lax.ppermute(x, axis, [(i, (i + 1) % n if i % 2 else (i - 1) % n) for i i...  3.97 us
    pallas_call x1, Pallas kernels, on_device(): pl.pallas_call(functools.partial(q_kernel, sizes, counts), out_shape=[sea...  1.58 us
    unnamed x8, local copies, waits for them, and re-layouts  1.42 us
    pallas_call x1, Pallas kernels, on_device(): pl.pallas_call(functools.partial(faces_kernel, sizes, counts), out_shape=...  1.06 us
  transfers between devices with their start and end apart: 13, of which 7 were waited for; matrix products, arithmetic and copies ran while one was open for 0% of the time, Pallas kernels for 17%

profile of v4, /device:TPU:0, one launch (start us, length us, event | category | flops | bytes accessed | tf_op | source)
XLA Modules:
  0.0 43.3 jit_solution(18283970752691080429)
XLA Ops:
  0.0 1.4 %copy-done = f32[3,32,32,128]{3,2,1,0:T(8,128)S(1)} copy-done((f32[3,32,32,128]{3,2,1,0:T(8,128)S(1)}, f32[3,32,32,128]{3,2,1,0:T(8,128)}, u32[]{:S(2)}) %copy-start) | copy-done | bytes 1572888
  1.4 1.1 %faces.1 = (f32[3,32,128]{2,1,0:T(8,128)S(1)}, f32[3,32,128]{2,1,0:T(8,128)S(1)}, f32[3,32,128]{2,1,0:T(8,128)S(1)}, f32[3,32,128]{2,1,0:T(8,128)S(1)}, f32[4,8,128]{2,1,0:T(8,128)S(1)}, /*index=5*/f32[8,128]{1,0:T(8,128)S(1)}) custom-call(f32[3,32,32,128]{3,2,1,0:T(8,128)S(1)} %copy-done), custom_call_target="tpu_custom_call" | custom-call | tf_op jit(solution)/shard_map/faces/pallas_call | solution.py:407
  2.5 0.6 %collective-permute-start.2 = (f32[4,8,128]{2,1,0:T(8,128)S(1)}, f32[4,8,128]{2,1,0:T(8,128)S(1)}, u32[]{:S(2)}, u32[]{:S(2)}) collective-permute-start(f32[4,8,128]{2,1,0:T(8,128)S(1)} %get-tuple-element.27), channel_id=1, source_target_pairs={{0,1},{1,0},{2,3},{3,2},{4,5},{5,4},{6,7},{7,6},{8,9},{9,8},{10,11... | collective-permute-start | bytes 49160 | tf_op jit(solution)/shard_map/ppermute | solution.py:28
  3.0 0.8 %collective-permute-done.2.refs_4_ = f32[4,8,128]{2,1,0:T(8,128)S(1)} collective-permute-done((f32[4,8,128]{2,1,0:T(8,128)S(1)}, f32[4,8,128]{2,1,0:T(8,128)S(1)}, u32[]{:S(2)}, u32[]{:S(2)}) %collective-permute-start.2) | collective-permute-done | bytes 16416 | tf_op jit(solution)/shard_map/ppermute | solution.py:28
  3.9 3.0 %collective-permute-start.3 = (f32[4,32,128]{2,1,0:T(8,128)S(1)}, f32[4,32,128]{2,1,0:T(8,128)S(1)}, u32[]{:S(2)}, u32[]{:S(2)}) collective-permute-start(f32[4,32,128]{2,1,0:T(8,128)S(1)} %get-tuple-element.28), channel_id=1, source_target_pairs={{0,2},{2,0},{4,6},{6,4},{1,3},{3,1},{5,7},{7,5},{8,10},{10,8},{12,... | collective-permute-start | bytes 196616 | tf_op jit(solution)/shard_map/ppermute | solution.py:28
  6.9 2.5 %collective-permute-start.4 = (f32[4,32,128]{2,1,0:T(8,128)S(1)}, f32[4,32,128]{2,1,0:T(8,128)S(1)}, u32[]{:S(2)}, u32[]{:S(2)}) collective-permute-start(f32[4,32,128]{2,1,0:T(8,128)S(1)} %get-tuple-element.29), channel_id=1, source_target_pairs={{0,6},{2,4},{4,2},{6,0},{1,7},{3,5},{5,3},{7,1},{8,14},{10,12},{12... | collective-permute-start | bytes 196616 | tf_op jit(solution)/shard_map/ppermute | solution.py:33
  9.3 1.5 %collective-permute-start = (f32[3,32,128]{2,1,0:T(8,128)S(1)}, f32[3,32,128]{2,1,0:T(8,128)S(1)}, u32[]{:S(2)}, u32[]{:S(2)}) collective-permute-start(f32[3,32,128]{2,1,0:T(8,128)S(1)} %get-tuple-element.22), channel_id=1, source_target_pairs={{0,8},{8,0},{16,24},{24,16},{1,9},{9,1},{17,25},{25,17},{2,10},{10... | collective-permute-start | bytes 147464 | tf_op jit(solution)/shard_map/ppermute | solution.py:28
  10.8 1.5 %collective-permute-start.1 = (f32[3,32,128]{2,1,0:T(8,128)S(1)}, f32[3,32,128]{2,1,0:T(8,128)S(1)}, u32[]{:S(2)}, u32[]{:S(2)}) collective-permute-start(f32[3,32,128]{2,1,0:T(8,128)S(1)} %get-tuple-element.23), channel_id=1, source_target_pairs={{0,24},{8,16},{16,8},{24,0},{1,25},{9,17},{17,9},{25,1},{2,26},{10... | collective-permute-start | bytes 147464 | tf_op jit(solution)/shard_map/ppermute | solution.py:33
  12.3 0.1 collective-permute-start.6
  12.4 4.4 %collective-permute-done.6.refs_3_ = f32[8,128]{1,0:T(8,128)S(1)} collective-permute-done((f32[8,128]{1,0:T(8,128)S(1)}, f32[8,128]{1,0:T(8,128)S(1)}, u32[]{:S(2)}, u32[]{:S(2)}) %collective-permute-start.6) | collective-permute-done | bytes 4128 | tf_op jit(solution)/shard_map/ppermute | solution.py:28
  16.8 0.0 collective-permute-done.3.refs_2_.refs_0_
  16.8 0.0 collective-permute-done.4.refs_3_.refs_1_
  16.8 1.6 %collective-permute-start.7 = (f32[8,128]{1,0:T(8,128)S(1)}, f32[8,128]{1,0:T(8,128)S(1)}, u32[]{:S(2)}, u32[]{:S(2)}) collective-permute-start(f32[8,128]{1,0:T(8,128)S(1)} %column.1.refs_1_), channel_id=1, source_target_pairs={{0,8},{8,0},{16,24},{24,16},{1,9},{9,1},{17,25},{25,17},{2,10},{10... | collective-permute-start | bytes 12296 | tf_op jit(solution)/shard_map/ppermute | solution.py:28
  18.4 0.0 collective-permute-done.refs_0_
  18.4 0.0 collective-permute-done.1.refs_1_
  18.4 1.6 %q.1 = (f32[32,8,128]{2,1,0:T(8,128)S(1)}, f32[32,8,128]{2,1,0:T(8,128)S(1)}, f32[32,8,128]{2,1,0:T(8,128)S(1)}, f32[33,8,128]{2,1,0:T(8,128)S(1)}) custom-call(f32[3,32,32,128]{3,2,1,0:T(8,128)S(1)} %copy-done.1, f32[3,32,128]{2,1,0:T(8,128)S(1)} %collective-permute-done.refs_0_, f32[3,32,128]{2,1,0:T(8,128)S(1)} %collective-permute-done.1.refs_1_, ...), custom_call_target="tpu_custom_call" | custom-call | tf_op jit(solution)/shard_map/q/pallas_call | solution.py:472
  20.0 0.6 %collective-permute-done.7.refs_2_ = f32[8,128]{1,0:T(8,128)S(1)} collective-permute-done((f32[8,128]{1,0:T(8,128)S(1)}, f32[8,128]{1,0:T(8,128)S(1)}, u32[]{:S(2)}, u32[]{:S(2)}) %collective-permute-start.7) | collective-permute-done | bytes 4128 | tf_op jit(solution)/shard_map/ppermute | solution.py:28
  20.6 1.4 %collective-permute-start.8 = (f32[33,8,128]{2,1,0:T(8,128)S(1)}, f32[33,8,128]{2,1,0:T(8,128)S(1)}, u32[]{:S(2)}, u32[]{:S(2)}) collective-permute-start(f32[33,8,128]{2,1,0:T(8,128)S(1)} %get-tuple-element.34), channel_id=1, source_target_pairs={{0,24},{8,16},{16,8},{24,0},{1,25},{9,17},{17,9},{25,1},{2,26},{10... | collective-permute-start | bytes 405512 | tf_op jit(solution)/shard_map/ppermute | solution.py:28
  22.0 1.6 %collective-permute-start.9 = (f32[32,8,128]{2,1,0:T(8,128)S(1)}, f32[32,8,128]{2,1,0:T(8,128)S(1)}, u32[]{:S(2)}, u32[]{:S(2)}) collective-permute-start(f32[32,8,128]{2,1,0:T(8,128)S(1)} %get-tuple-element.38), channel_id=1, source_target_pairs={{0,16},{8,24},{16,0},{24,8},{1,17},{9,25},{17,1},{25,9},{2,18},{10... | collective-permute-start | bytes 393224 | tf_op jit(solution)/shard_map/ppermute | solution.py:28
  23.5 0.5 %collective-permute-start.5 = (f32[32,8,128]{2,1,0:T(8,128)S(1)}, f32[32,8,128]{2,1,0:T(8,128)S(1)}, u32[]{:S(2)}, u32[]{:S(2)}) collective-permute-start(f32[32,8,128]{2,1,0:T(8,128)S(1)} %get-tuple-element.30), channel_id=1, source_target_pairs={{0,8},{8,0},{16,24},{24,16},{1,9},{9,1},{17,25},{25,17},{2,10},{10... | collective-permute-start | bytes 393224 | tf_op jit(solution)/shard_map/ppermute | solution.py:28
  24.1 2.5 %collective-permute-done.8.refs_1_ = f32[33,8,128]{2,1,0:T(8,128)S(1)} collective-permute-done((f32[33,8,128]{2,1,0:T(8,128)S(1)}, f32[33,8,128]{2,1,0:T(8,128)S(1)}, u32[]{:S(2)}, u32[]{:S(2)}) %collective-permute-start.8) | collective-permute-done | bytes 135200 | tf_op jit(solution)/shard_map/ppermute | solution.py:28
  26.6 3.7 %render.3 = (f32[2,4,8,8,128]{4,3,2,1,0:T(8,128)S(1)}, f32[8,128]{1,0:T(8,128)S(1)}) custom-call(f32[32,8,128]{2,1,0:T(8,128)S(1)} %get-tuple-element.31.refs_0_, f32[33,8,128]{2,1,0:T(8,128)S(1)} %collective-permute-done.8.refs_1_, f32[8,128]{1,0:T(8,128)S(1)} %get-tuple-element.35.refs_2_, s32[8]{0:T(128)S(1)} %copy-done.3, f32[32,128]{1,0:T(8,128)S(1)} %bitcast.3), custom_call_target="tpu_custom_call" | custom-call | tf_op jit(solution)/shard_map/render/pallas_call | solution.py:507
  30.3 0.0 collective-permute-done.9.refs_0_
  30.3 2.1 %render.4.refs_3_ = f32[1,4,8,8,128]{4,3,2,1,0:T(8,128)S(1)} custom-call(f32[32,8,128]{2,1,0:T(8,128)S(1)} %collective-permute-done.9.refs_0_, f32[8,128]{1,0:T(8,128)S(1)} %get-tuple-element.36.refs_1_, f32[2,4,8,8,128]{4,3,2,1,0:T(8,128)S(1)} %get-tuple-element.37.refs_2_, s32[8]{0:T(128)S(1)} %copy-done.3, f32[32,128]{1,0:T(8,128)S(1)} %bitcast.4), custom_call_target="tpu_custom_call" | custom-call | tf_op jit(solution)/shard_map/render/pallas_call | solution.py:507
  32.4 2.1 %render.5.refs_0_ = f32[8,4,8,128]{3,2,1,0:T(8,128)S(1)} custom-call(f32[32,8,128]{2,1,0:T(8,128)S(1)} %collective-permute-done.5.refs_0_, f32[8,128]{1,0:T(8,128)S(1)} %get-tuple-element.36.refs_1_, f32[2,4,8,8,128]{4,3,2,1,0:T(8,128)S(1)} %get-tuple-element.37.refs_2_, f32[1,4,8,8,128]{4,3,2,1,0:T(8,128)S(1)} %render.4.refs_3_, s32[8]{0:T(128)S(1)} %copy-done.3, ...), custom_call_target="tpu_custom_call" | custom-call | tf_op jit(solution)/shard_map/render/pallas_call | solution.py:507
  34.5 1.4 %collective-permute-start.12 = (f32[8,4,8,128]{3,2,1,0:T(8,128)S(1)}, f32[8,4,8,128]{3,2,1,0:T(8,128)S(1)}, u32[]{:S(2)}, u32[]{:S(2)}) collective-permute-start(f32[8,4,8,128]{3,2,1,0:T(8,128)S(1)} %render.5.refs_0_), channel_id=1, source_target_pairs={{0,24},{8,16},{16,8},{24,0},{1,25},{9,17},{17,9},{25,1},{2,26},{10... | collective-permute-start | bytes 393224 | tf_op jit(solution)/shard_map/ppermute | solution.py:28
  36.0 1.6 %collective-permute-start.11 = (f32[8,4,8,128]{3,2,1,0:T(8,128)S(1)}, f32[8,4,8,128]{3,2,1,0:T(8,128)S(1)}, u32[]{:S(2)}, u32[]{:S(2)}) collective-permute-start(f32[8,4,8,128]{3,2,1,0:T(8,128)S(1)} %render.5.refs_0_), channel_id=1, source_target_pairs={{0,16},{8,24},{16,0},{24,8},{1,17},{9,25},{17,1},{25,9},{2,18},{10... | collective-permute-start | bytes 393224 | tf_op jit(solution)/shard_map/ppermute | solution.py:28
  37.5 0.5 %collective-permute-start.10 = (f32[8,4,8,128]{3,2,1,0:T(8,128)S(1)}, f32[8,4,8,128]{3,2,1,0:T(8,128)S(1)}, u32[]{:S(2)}, u32[]{:S(2)}) collective-permute-start(f32[8,4,8,128]{3,2,1,0:T(8,128)S(1)} %render.5.refs_0_), channel_id=1, source_target_pairs={{0,8},{8,0},{16,24},{24,16},{1,9},{9,1},{17,25},{25,17},{2,10},{10... | collective-permute-start | bytes 393224 | tf_op jit(solution)/shard_map/ppermute | solution.py:28
  38.1 2.5 %collective-permute-done.12.refs_3_ = f32[8,4,8,128]{3,2,1,0:T(8,128)S(1)} collective-permute-done((f32[8,4,8,128]{3,2,1,0:T(8,128)S(1)}, f32[8,4,8,128]{3,2,1,0:T(8,128)S(1)}, u32[]{:S(2)}, u32[]{:S(2)}) %collective-permute-start.12) | collective-permute-done | bytes 131104 | tf_op jit(solution)/shard_map/ppermute | solution.py:28
  40.6 1.3 %collective-permute-done.11.refs_2_ = f32[8,4,8,128]{3,2,1,0:T(8,128)S(1)} collective-permute-done((f32[8,4,8,128]{3,2,1,0:T(8,128)S(1)}, f32[8,4,8,128]{3,2,1,0:T(8,128)S(1)}, u32[]{:S(2)}, u32[]{:S(2)}) %collective-permute-start.11) | collective-permute-done | bytes 131104 | tf_op jit(solution)/shard_map/ppermute | solution.py:28
  41.9 0.7 %collective-permute-done.10.refs_1_ = f32[8,4,8,128]{3,2,1,0:T(8,128)S(1)} collective-permute-done((f32[8,4,8,128]{3,2,1,0:T(8,128)S(1)}, f32[8,4,8,128]{3,2,1,0:T(8,128)S(1)}, u32[]{:S(2)}, u32[]{:S(2)}) %collective-permute-start.10) | collective-permute-done | bytes 131104 | tf_op jit(solution)/shard_map/ppermute | solution.py:28
  42.5 0.8 %assemble.1 = f32[8,4,32,128]{3,2,1,0:T(8,128)} custom-call(f32[8,4,8,128]{3,2,1,0:T(8,128)S(1)} %render.5.refs_0_, f32[8,4,8,128]{3,2,1,0:T(8,128)S(1)} %collective-permute-done.10.refs_1_, f32[8,4,8,128]{3,2,1,0:T(8,128)S(1)} %collective-permute-done.11.refs_2_, f32[8,4,8,128]{3,2,1,0:T(8,128)S(1)} %collective-permute-done.12.refs_3_), custom_call_target="tpu_custom_call" | custom-call | tf_op jit(solution)/shard_map/assemble/pallas_call | solution.py:531
  (12 shorter events, 0.0 us)
Async XLA Ops:
  0.0 1.4 %copy-start = (f32[3,32,32,128]{3,2,1,0:T(8,128)S(1)}, f32[3,32,32,128]{3,2,1,0:T(8,128)}, u32[]{:S(2)}) copy-start(f32[3,32,32,128]{3,2,1,0:T(8,128)} %v_hbm.3) | copy-start | bytes 4718596
  1.4 17.0 %copy-start.1 = (f32[3,32,32,128]{3,2,1,0:T(8,128)S(1)}, f32[3,32,32,128]{3,2,1,0:T(8,128)}, u32[]{:S(2)}) copy-start(f32[3,32,32,128]{3,2,1,0:T(8,128)} %v_hbm.3) | copy-start | bytes 4718596
  1.4 25.2 %copy-start.2 = (f32[8,4,128]{2,1,0:T(4,128)S(1)}, f32[8,4,128]{2,1,0:T(4,128)}, u32[]{:S(2)}) copy-start(f32[8,4,128]{2,1,0:T(4,128)} %param.5) | copy-start | bytes 49156
  1.4 25.2 %copy-start.3 = (s32[8]{0:T(128)S(1)}, s32[8]{0:T(128)}, u32[]{:S(2)}) copy-start(s32[8]{0:T(128)} %refs_4_.1) | copy-start | bytes 100
  2.5 1.4 %collective-permute-start.2 = (f32[4,8,128]{2,1,0:T(8,128)S(1)}, f32[4,8,128]{2,1,0:T(8,128)S(1)}, u32[]{:S(2)}, u32[]{:S(2)}) collective-permute-start(f32[4,8,128]{2,1,0:T(8,128)S(1)} %get-tuple-element.27), channel_id=1, source_target_pairs={{0,1},{1,0},{2,3},{3,2},{4,5},{5,4},{6,7},{7,6},{8,9},{9,8},{10,11... | collective-permute-start | bytes 49160 | tf_op jit(solution)/shard_map/ppermute | solution.py:28
  3.9 12.9 %collective-permute-start.3 = (f32[4,32,128]{2,1,0:T(8,128)S(1)}, f32[4,32,128]{2,1,0:T(8,128)S(1)}, u32[]{:S(2)}, u32[]{:S(2)}) collective-permute-start(f32[4,32,128]{2,1,0:T(8,128)S(1)} %get-tuple-element.28), channel_id=1, source_target_pairs={{0,2},{2,0},{4,6},{6,4},{1,3},{3,1},{5,7},{7,5},{8,10},{10,8},{12,... | collective-permute-start | bytes 196616 | tf_op jit(solution)/shard_map/ppermute | solution.py:28
  6.9 10.0 %collective-permute-start.4 = (f32[4,32,128]{2,1,0:T(8,128)S(1)}, f32[4,32,128]{2,1,0:T(8,128)S(1)}, u32[]{:S(2)}, u32[]{:S(2)}) collective-permute-start(f32[4,32,128]{2,1,0:T(8,128)S(1)} %get-tuple-element.29), channel_id=1, source_target_pairs={{0,6},{2,4},{4,2},{6,0},{1,7},{3,5},{5,3},{7,1},{8,14},{10,12},{12... | collective-permute-start | bytes 196616 | tf_op jit(solution)/shard_map/ppermute | solution.py:33
  9.3 9.1 %collective-permute-start = (f32[3,32,128]{2,1,0:T(8,128)S(1)}, f32[3,32,128]{2,1,0:T(8,128)S(1)}, u32[]{:S(2)}, u32[]{:S(2)}) collective-permute-start(f32[3,32,128]{2,1,0:T(8,128)S(1)} %get-tuple-element.22), channel_id=1, source_target_pairs={{0,8},{8,0},{16,24},{24,16},{1,9},{9,1},{17,25},{25,17},{2,10},{10... | collective-permute-start | bytes 147464 | tf_op jit(solution)/shard_map/ppermute | solution.py:28
  10.8 7.6 %collective-permute-start.1 = (f32[3,32,128]{2,1,0:T(8,128)S(1)}, f32[3,32,128]{2,1,0:T(8,128)S(1)}, u32[]{:S(2)}, u32[]{:S(2)}) collective-permute-start(f32[3,32,128]{2,1,0:T(8,128)S(1)} %get-tuple-element.23), channel_id=1, source_target_pairs={{0,24},{8,16},{16,8},{24,0},{1,25},{9,17},{17,9},{25,1},{2,26},{10... | collective-permute-start | bytes 147464 | tf_op jit(solution)/shard_map/ppermute | solution.py:33
  12.3 4.5 %collective-permute-start.6 = (f32[8,128]{1,0:T(8,128)S(1)}, f32[8,128]{1,0:T(8,128)S(1)}, u32[]{:S(2)}, u32[]{:S(2)}) collective-permute-start(f32[8,128]{1,0:T(8,128)S(1)} %get-tuple-element.33.refs_2_), channel_id=1, source_target_pairs={{0,4},{2,6},{4,0},{6,2},{1,5},{3,7},{5,1},{7,3},{8,12},{10,14},{12... | collective-permute-start | bytes 12296 | tf_op jit(solution)/shard_map/ppermute | solution.py:28
  16.8 3.7 %collective-permute-start.7 = (f32[8,128]{1,0:T(8,128)S(1)}, f32[8,128]{1,0:T(8,128)S(1)}, u32[]{:S(2)}, u32[]{:S(2)}) collective-permute-start(f32[8,128]{1,0:T(8,128)S(1)} %column.1.refs_1_), channel_id=1, source_target_pairs={{0,8},{8,0},{16,24},{24,16},{1,9},{9,1},{17,25},{25,17},{2,10},{10... | collective-permute-start | bytes 12296 | tf_op jit(solution)/shard_map/ppermute | solution.py:28
  20.6 6.0 %collective-permute-start.8 = (f32[33,8,128]{2,1,0:T(8,128)S(1)}, f32[33,8,128]{2,1,0:T(8,128)S(1)}, u32[]{:S(2)}, u32[]{:S(2)}) collective-permute-start(f32[33,8,128]{2,1,0:T(8,128)S(1)} %get-tuple-element.34), channel_id=1, source_target_pairs={{0,24},{8,16},{16,8},{24,0},{1,25},{9,17},{17,9},{25,1},{2,26},{10... | collective-permute-start | bytes 405512 | tf_op jit(solution)/shard_map/ppermute | solution.py:28
  22.0 8.3 %collective-permute-start.9 = (f32[32,8,128]{2,1,0:T(8,128)S(1)}, f32[32,8,128]{2,1,0:T(8,128)S(1)}, u32[]{:S(2)}, u32[]{:S(2)}) collective-permute-start(f32[32,8,128]{2,1,0:T(8,128)S(1)} %get-tuple-element.38), channel_id=1, source_target_pairs={{0,16},{8,24},{16,0},{24,8},{1,17},{9,25},{17,1},{25,9},{2,18},{10... | collective-permute-start | bytes 393224 | tf_op jit(solution)/shard_map/ppermute | solution.py:28
  23.5 8.9 %collective-permute-start.5 = (f32[32,8,128]{2,1,0:T(8,128)S(1)}, f32[32,8,128]{2,1,0:T(8,128)S(1)}, u32[]{:S(2)}, u32[]{:S(2)}) collective-permute-start(f32[32,8,128]{2,1,0:T(8,128)S(1)} %get-tuple-element.30), channel_id=1, source_target_pairs={{0,8},{8,0},{16,24},{24,16},{1,9},{9,1},{17,25},{25,17},{2,10},{10... | collective-permute-start | bytes 393224 | tf_op jit(solution)/shard_map/ppermute | solution.py:28
  34.5 6.0 %collective-permute-start.12 = (f32[8,4,8,128]{3,2,1,0:T(8,128)S(1)}, f32[8,4,8,128]{3,2,1,0:T(8,128)S(1)}, u32[]{:S(2)}, u32[]{:S(2)}) collective-permute-start(f32[8,4,8,128]{3,2,1,0:T(8,128)S(1)} %render.5.refs_0_), channel_id=1, source_target_pairs={{0,24},{8,16},{16,8},{24,0},{1,25},{9,17},{17,9},{25,1},{2,26},{10... | collective-permute-start | bytes 393224 | tf_op jit(solution)/shard_map/ppermute | solution.py:28
  36.0 5.9 %collective-permute-start.11 = (f32[8,4,8,128]{3,2,1,0:T(8,128)S(1)}, f32[8,4,8,128]{3,2,1,0:T(8,128)S(1)}, u32[]{:S(2)}, u32[]{:S(2)}) collective-permute-start(f32[8,4,8,128]{3,2,1,0:T(8,128)S(1)} %render.5.refs_0_), channel_id=1, source_target_pairs={{0,16},{8,24},{16,0},{24,8},{1,17},{9,25},{17,1},{25,9},{2,18},{10... | collective-permute-start | bytes 393224 | tf_op jit(solution)/shard_map/ppermute | solution.py:28
  37.5 5.0 %collective-permute-start.10 = (f32[8,4,8,128]{3,2,1,0:T(8,128)S(1)}, f32[8,4,8,128]{3,2,1,0:T(8,128)S(1)}, u32[]{:S(2)}, u32[]{:S(2)}) collective-permute-start(f32[8,4,8,128]{3,2,1,0:T(8,128)S(1)} %render.5.refs_0_), channel_id=1, source_target_pairs={{0,8},{8,0},{16,24},{24,16},{1,9},{9,1},{17,25},{25,17},{2,10},{10... | collective-permute-start | bytes 393224 | tf_op jit(solution)/shard_map/ppermute | solution.py:28

commit v5 on v3

--- a/solution.py
+++ b/solution.py
@@ -11,12 +11,12 @@
 SUB, LANES = 8, 128
 AXES = ("gx", "gy", "gz")
 ANY = pl.BlockSpec(memory_space=pl.ANY)
+HBM = pl.BlockSpec(memory_space=pltpu.HBM)
 VMEM = pl.BlockSpec(memory_space=pltpu.VMEM)
 SMEM = pl.BlockSpec(memory_space=pltpu.SMEM)
 f32 = jnp.float32
 EARLY = 48
 LATE_UNROLL = 80
-CHUNKS = 4
 UNITS = 2
 PATTERN = (4, 2)
 
@@ -56,51 +56,56 @@
     )
 
 
+def edge(info, axis, far, extent):
+    at = jnp.where(info[axis][0], extent - 1, 0)
+    return extent - 1 - at if far else at
+
+
 def faces_kernel(sizes, counts, v_hbm, *refs):
     comps, depth, rows, cols = v_hbm.shape
+    info = flags(sizes)
+    x_refs, y_refs = refs[: counts[0]], refs[counts[0] : counts[0] + counts[1]]
+    band, sem = refs[counts[0] + counts[1] :]
+    copies = []
+    for far, out in enumerate(x_refs):
+        source = v_hbm.at[:, edge(info, 0, far, depth)]
+        copies.append(pltpu.make_async_copy(source, out, sem.at[far]))
+    for far in range(len(y_refs)):
+        at = pl.multiple_of(edge(info, 1, far, rows) // SUB * SUB, SUB)
+        source = v_hbm.at[:, :, pl.ds(at, SUB), :]
+        copies.append(pltpu.make_async_copy(source, band.at[far], sem.at[2 + far]))
+    for copy in copies:
+        copy.start()
+    for copy in copies:
+        copy.wait()
+    for far, out in enumerate(y_refs):
+        at = lax.rem(edge(info, 1, far, rows), SUB)
+        for c in range(comps):
+            for x in range(depth):
+                out[c, pl.ds(x, 1), :] = band[far, c, x, pl.ds(at, 1), :]
+
+
+def ends_kernel(sizes, counts, v_ref, *refs):
+    comps, depth, rows, cols = v_ref.shape
     tiles = rows // SUB
     info = flags(sizes)
-    refs = list(refs)
-    x_refs = [refs.pop(0) for _ in range(counts[0])]
-    y_refs = [refs.pop(0) for _ in range(counts[1])]
-    z_refs = [refs.pop(0) for _ in range(counts[2])]
-    sq_ref, v_ref, sem = refs
-    chunk = depth // CHUNKS
-    copies = []
-    for n in range(CHUNKS):
-        part = pl.ds(n * chunk, chunk)
-        copies.append(pltpu.make_async_copy(v_hbm.at[:, part], v_ref.at[:, part], sem.at[n]))
-        copies[-1].start()
-
-    def edge(axis, far, extent):
-        at = jnp.where(info[axis][0], extent - 1, 0)
-        return extent - 1 - at if far else at
-
+    z_refs, sq_ref = refs[: counts[2]], refs[counts[2]]
     lane = lax.broadcasted_iota(jnp.int32, (SUB, LANES), 1)
     groups = depth * tiles // LANES
     zero = jnp.zeros((SUB, LANES), f32)
     picked = [[[zero] * comps for _ in range(groups)] for _ in z_refs]
     squares = [zero] * 4
-    for n in range(CHUNKS):
-        copies[n].wait()
-        for x in range(n * chunk, (n + 1) * chunk):
-            for far, out in enumerate(y_refs):
-                at = edge(1, far, rows)
-                for c in range(comps):
-                    out[c, pl.ds(x, 1), :] = v_ref[c, x, pl.ds(at, 1), :]
-            for c in range(comps):
-                for j in range(tiles):
-                    tile = v_ref[c, x, pl.ds(j * SUB, SUB), :]
-                    squares[j % 4] = squares[j % 4] + tile * tile
-                    group, to = divmod(x * tiles + j, LANES)
-                    for far in range(len(z_refs)):
-                        at = edge(2, far, cols)
-                        moved = pltpu.roll(tile, lax.rem(to - at + cols, cols), 1)
-                        old = picked[far][group][c]
-                        picked[far][group][c] = jnp.where(lane == to, moved, old)
-    for far, out in enumerate(x_refs):
+    for x in range(depth):
         for c in range(comps):
-            out[c] = v_ref[c, edge(0, far, depth)]
+            for j in range(tiles):
+                tile = v_ref[c, x, pl.ds(j * SUB, SUB), :]
+                squares[j % 4] = squares[j % 4] + tile * tile
+                group, to = divmod(x * tiles + j, LANES)
+                for far in range(len(z_refs)):
+                    at = edge(info, 2, far, cols)
+                    moved = pltpu.roll(tile, lax.rem(to - at + cols, cols), 1)
+                    old = picked[far][group][c]
+                    picked[far][group][c] = jnp.where(lane == to, moved, old)
     total = (squares[0] + squares[1]) + (squares[2] + squares[3])
     sq_ref[...] = total
     for far, out in enumerate(z_refs):
@@ -110,26 +115,29 @@
         out[groups * comps] = total
 
 
-def attach_kernel(faces, tiles, *refs):
-    face_refs, tile_refs = refs[:faces], refs[faces : faces + tiles]
-    outs, sum_ref = refs[faces + tiles : -1], refs[-1]
-    total = tile_refs[0][...]
-    for t in tile_refs[1:]:
+def column_kernel(*refs):
+    *tiles, out = refs
+    total = tiles[0][...]
+    for t in tiles[1:]:
+        total = total + (t[...] if len(t.shape) == 2 else t[t.shape[0] - 1])
+    out[...] = total
+
+
+def seal_kernel(pieces, *refs):
+    tiles, outs = refs[pieces:-pieces], refs[-pieces:]
+    total = tiles[0][...]
+    for t in tiles[1:]:
         total = total + t[...]
-    sum_ref[...] = total
-    for face, out in zip(face_refs, outs):
-        comps = face.shape[0]
-        out[pl.ds(0, comps)] = face[...]
-        out[comps, pl.ds(0, SUB), :] = total
-
-
-def q_kernel(sizes, counts, attached, extras, v_hbm, *refs):
+    for out in outs:
+        out[out.shape[0] - 1, pl.ds(0, SUB), :] = total
+
+
+def q_kernel(sizes, counts, v_hbm, *refs):
     comps, depth, rows, cols = v_hbm.shape
     tiles = rows // SUB
     nx = sizes[0]
     refs = list(refs)
     halos = [[refs.pop(0) for _ in range(counts[a])] for a in range(3)]
-    extra = [refs.pop(0) for _ in range(extras)]
     outs, (padded, sem) = refs[:nx], refs[nx:]
     info = flags(sizes)
     copy = pltpu.make_async_copy(
@@ -154,13 +162,6 @@
             value = jnp.broadcast_to(value, (depth, cols))
             for x in range(depth):
                 padded[c, 1 + x, pl.ds(end, 1), :] = value[x : x + 1]
-    tile_sum = extra[0][...]
-    for t in extra[1:]:
-        tile_sum = tile_sum + t[...]
-    for near_far in halos[1][:attached]:
-        tile_sum = tile_sum + near_far[comps, pl.ds(0, SUB), :]
-    for out in outs:
-        out[depth, pl.ds(0, SUB), :] = tile_sum
     groups = depth * tiles // LANES
     lane = lax.broadcasted_iota(jnp.int32, (SUB, cols), 1)
     me = lax.axis_index("gx")
@@ -361,64 +362,61 @@
     tile = jax.ShapeDtypeStruct((SUB, LANES), f32)
     x_face = jax.ShapeDtypeStruct((comps, rows, cols), f32)
     y_face = jax.ShapeDtypeStruct((comps, depth, cols), f32)
-    y_sent = jax.ShapeDtypeStruct((comps + 1, depth, cols), f32)
     z_face = jax.ShapeDtypeStruct((groups * comps + 1, SUB, LANES), f32)
-    shapes = [x_face] * counts[0] + [y_face] * counts[1] + [z_face] * counts[2] + [tile]
-    *faces, squares = pl.pallas_call(
+    faces = pl.pallas_call(
         functools.partial(faces_kernel, sizes, counts),
-        out_shape=shapes,
-        in_specs=[ANY],
-        out_specs=[VMEM] * len(shapes),
+        out_shape=[x_face] * counts[0] + [y_face] * counts[1],
+        in_specs=[HBM],
+        out_specs=[VMEM] * (counts[0] + counts[1]),
         scratch_shapes=[
-            pltpu.VMEM((comps, depth, rows, cols), f32),
-            pltpu.SemaphoreType.DMA((CHUNKS,)),
+            pltpu.VMEM((2, comps, depth, SUB, cols), f32),
+            pltpu.SemaphoreType.DMA((4,)),
         ],
+        compiler_params=limit(2),
+        name="faces",
+    )(pltpu.with_memory_space_constraint(velocity, pltpu.HBM))
+    *z_faces, squares = pl.pallas_call(
+        functools.partial(ends_kernel, sizes, counts),
+        out_shape=[z_face] * counts[2] + [tile],
+        in_specs=[VMEM],
+        out_specs=[VMEM] * (counts[2] + 1),
         compiler_params=limit(4),
-        name="faces",
+        name="ends",
     )(velocity)
 
     def exchange(sent, axis):
         kinds = (functools.partial(swap, bit_mask=1), swap_across)
         return [kind(x, axis) for x, kind in zip(sent, kinds)]
 
-    def everyone(x, axis):
-        for bit in range(lax.axis_size(axis).bit_length() - 1):
-            x = x + swap(x, axis, 1 << bit)
-        return x
-
-    x_faces, y_faces, z_faces = (
-        faces[: counts[0]],
-        faces[counts[0] : counts[0] + counts[1]],
-        faces[counts[0] + counts[1] :],
-    )
+    def column(*tiles):
+        return pl.pallas_call(
+            column_kernel,
+            out_shape=tile,
+            in_specs=[VMEM] * len(tiles),
+            out_specs=VMEM,
+            compiler_params=limit(2),
+            name="column",
+        )(*tiles)
+
+    def others(x, axis):
+        n = lax.axis_size(axis)
+        while n > 4:
+            n //= 2
+            x = x + swap(x, axis, n)
+        return [x] + [swap(x, axis, k) for k in range(1, n)]
+
+    x_halos = exchange(faces[: counts[0]], "gx")
+    y_halos = exchange(faces[counts[0] :], "gy")
     z_halos = exchange(z_faces, "gz")
-    x_halos = exchange(x_faces, "gx")
-    if sizes[2] == 2:
-        tiles = [squares, z_halos[0][groups * comps]]
-    else:
-        tiles = [everyone(squares, "gz")]
-    *y_sents, column = pl.pallas_call(
-        functools.partial(attach_kernel, len(y_faces), len(tiles)),
-        out_shape=[y_sent] * len(y_faces) + [tile],
-        in_specs=[VMEM] * (len(y_faces) + len(tiles)),
-        out_specs=[VMEM] * (len(y_faces) + 1),
-        compiler_params=limit(2),
-        name="attach",
-    )(*y_faces, *tiles)
-    y_halos = exchange(y_sents, "gy")
-    if sizes[1] == 4:
-        attached, extra = 2, [column, swap(column, "gy", 2)]
-    elif sizes[1] <= 2:
-        attached, extra = counts[1], [column]
-    else:
-        attached, extra = 0, [everyone(column, "gy")]
+    tiles = [squares, z_halos[0]] if sizes[2] == 2 else others(squares, "gz")
+    tiles = others(column(*tiles), "gy")
     part_rows = rows // nx
     piece = jax.ShapeDtypeStruct((depth + 1, part_rows, cols), f32)
     halos = x_halos + y_halos + z_halos
     q_pieces = pl.pallas_call(
-        functools.partial(q_kernel, sizes, counts, attached, len(extra)),
+        functools.partial(q_kernel, sizes, counts),
         out_shape=[piece] * nx,
-        in_specs=[ANY] + [VMEM] * (len(halos) + len(extra)),
+        in_specs=[ANY] + [VMEM] * len(halos),
         out_specs=[VMEM] * nx,
         scratch_shapes=[
             pltpu.VMEM((comps, depth + 2, rows + 2 * SUB, cols), f32),
@@ -426,7 +424,16 @@
         ],
         compiler_params=limit(8),
         name="q",
-    )(velocity, *halos, *extra)
+    )(velocity, *halos)
+    q_pieces = pl.pallas_call(
+        functools.partial(seal_kernel, nx),
+        out_shape=[piece] * nx,
+        in_specs=[VMEM] * (nx + len(tiles)),
+        out_specs=[VMEM] * nx,
+        input_output_aliases={k: k for k in range(nx)},
+        compiler_params=limit(2),
+        name="seal",
+    )(*q_pieces, *tiles)
     order = sorted(range(1, nx), key=lambda k: -k)
     got = {0: q_pieces[0]}
     for k in order:

time: 41.4 us -> 41.6 us (level)
  starting transfers between devices: 16.2 us -> 20.1 us
  waiting for transfers between devices: 13.6 us -> 10.5 us
  local copies, waits for them, and re-layouts: 1.42 us -> 0.02 us
  Pallas kernels: 9.96 us -> 10.7 us
    ppermute x10 -> x12, starting transfers between devices: 12.2 us -> 16.2 us  [swap(): return lax.ppermute(x, axis, [(i, i ^ bit_mask) for i in range(n)])]
    ppermute x10 -> x12, waiting for transfers between devices: 13.5 us -> 10.5 us  [swap(): return lax.ppermute(x, axis, [(i, i ^ bit_mask) for i in range(n)])]
    unnamed x8 -> x6, local copies, waits for them, and re-layouts: 1.42 us -> 0.02 us
    pallas_call x2 -> x4, Pallas kernels: 1.59 us -> 2.05 us  [the longest x1 1.56 us: on_device(): pl.pallas_call(functools.partial(q_kernel, sizes, counts), out_shape=[pie...]
  transfers between devices with their start and end apart: 12 -> 14, of which waited for: 6 -> 5; matrix products, arithmetic and copies ran while one was open for 0% -> 0% of each run, Pallas kernels for 0% -> 5%
where the time goes in v5:
time: 41.6 us; the launch traced here: 41.5 us
  starting transfers between devices  20.1 us (48%)
  Pallas kernels  10.7 us (26%)
  waiting for transfers between devices  10.5 us (25%)
    ppermute x12, starting transfers between devices, swap(): return lax.ppermute(x, axis, [(i, i ^ bit_mask) for i in range(n)])  16.2 us
    ppermute x12, waiting for transfers between devices, swap(): return lax.ppermute(x, axis, [(i, i ^ bit_mask) for i in range(n)])  10.5 us
    pallas_call x1, Pallas kernels, on_device(): pl.pallas_call(functools.partial(render_kernel, nx, cell_count), out_shap...  6.49 us
    ppermute x2, starting transfers between devices, swap_across(): lax.ppermute(x, axis, [(i, (i + 1) % n if i % 2 else (i - 1) % n) for i i...  3.97 us
    pallas_call x1, Pallas kernels, on_device(): pl.pallas_call(functools.partial(q_kernel, sizes, counts), out_shape=[pie...  1.56 us
    pallas_call x1, Pallas kernels, on_device(): pl.pallas_call(functools.partial(faces_kernel, sizes, counts), out_shape=...  1.39 us
  transfers between devices with their start and end apart: 14, of which 5 were waited for; matrix products, arithmetic and copies ran while one was open for 0% of the time, Pallas kernels for 5%

profile of v5, /device:TPU:0, one launch (start us, length us, event | category | flops | bytes accessed | tf_op | source)
XLA Modules:
  0.0 41.5 jit_solution(2567048676783491670)
XLA Ops:
  0.0 1.4 %faces.1 = (f32[3,32,128]{2,1,0:T(8,128)S(1)}, f32[3,32,128]{2,1,0:T(8,128)S(1)}, f32[3,32,128]{2,1,0:T(8,128)S(1)}, f32[3,32,128]{2,1,0:T(8,128)S(1)}) custom-call(f32[3,32,32,128]{3,2,1,0:T(8,128)} %v_hbm.3), custom_call_target="tpu_custom_call" | custom-call | tf_op jit(solution)/shard_map/faces/pallas_call | solution.py:366
  1.4 3.0 %collective-permute-start = (f32[3,32,128]{2,1,0:T(8,128)S(1)}, f32[3,32,128]{2,1,0:T(8,128)S(1)}, u32[]{:S(2)}, u32[]{:S(2)}) collective-permute-start(f32[3,32,128]{2,1,0:T(8,128)S(1)} %get-tuple-element.19), channel_id=1, source_target_pairs={{0,8},{8,0},{16,24},{24,16},{1,9},{9,1},{17,25},{25,17},{2,10},{10... | collective-permute-start | bytes 147464 | tf_op jit(solution)/shard_map/ppermute | solution.py:30
  4.4 1.5 %collective-permute-start.1 = (f32[3,32,128]{2,1,0:T(8,128)S(1)}, f32[3,32,128]{2,1,0:T(8,128)S(1)}, u32[]{:S(2)}, u32[]{:S(2)}) collective-permute-start(f32[3,32,128]{2,1,0:T(8,128)S(1)} %get-tuple-element.20), channel_id=1, source_target_pairs={{0,24},{8,16},{16,8},{24,0},{1,25},{9,17},{17,9},{25,1},{2,26},{10... | collective-permute-start | bytes 147464 | tf_op jit(solution)/shard_map/ppermute | solution.py:35
  5.9 1.6 %collective-permute-start.2 = (f32[3,32,128]{2,1,0:T(8,128)S(1)}, f32[3,32,128]{2,1,0:T(8,128)S(1)}, u32[]{:S(2)}, u32[]{:S(2)}) collective-permute-start(f32[3,32,128]{2,1,0:T(8,128)S(1)} %get-tuple-element.21), channel_id=1, source_target_pairs={{0,2},{2,0},{4,6},{6,4},{1,3},{3,1},{5,7},{7,5},{8,10},{10,8},{12,... | collective-permute-start | bytes 147464 | tf_op jit(solution)/shard_map/ppermute | solution.py:30
  7.5 2.5 %collective-permute-start.3 = (f32[3,32,128]{2,1,0:T(8,128)S(1)}, f32[3,32,128]{2,1,0:T(8,128)S(1)}, u32[]{:S(2)}, u32[]{:S(2)}) collective-permute-start(f32[3,32,128]{2,1,0:T(8,128)S(1)} %get-tuple-element.22), channel_id=1, source_target_pairs={{0,6},{2,4},{4,2},{6,0},{1,7},{3,5},{5,3},{7,1},{8,14},{10,12},{12... | collective-permute-start | bytes 147464 | tf_op jit(solution)/shard_map/ppermute | solution.py:35
  10.0 0.5 %ends.1 = (f32[4,8,128]{2,1,0:T(8,128)S(1)}, f32[8,128]{1,0:T(8,128)S(1)}) custom-call(f32[3,32,32,128]{3,2,1,0:T(8,128)S(1)} %copy-done), custom_call_target="tpu_custom_call" | custom-call | tf_op jit(solution)/shard_map/ends/pallas_call | solution.py:378
  10.5 0.0 copy-start.1
  10.5 0.0 copy-start.2
  10.5 0.1 collective-permute-start.4
  10.6 1.2 %collective-permute-done.4.refs_4_.refs_1_ = f32[4,8,128]{2,1,0:T(8,128)S(1)} collective-permute-done((f32[4,8,128]{2,1,0:T(8,128)S(1)}, f32[4,8,128]{2,1,0:T(8,128)S(1)}, u32[]{:S(2)}, u32[]{:S(2)}) %collective-permute-start.4) | collective-permute-done | bytes 16416 | tf_op jit(solution)/shard_map/ppermute | solution.py:30
  11.7 1.3 %collective-permute-start.7 = (f32[8,128]{1,0:T(8,128)S(1)}, f32[8,128]{1,0:T(8,128)S(1)}, u32[]{:S(2)}, u32[]{:S(2)}) collective-permute-start(f32[8,128]{1,0:T(8,128)S(1)} %column.1.refs_4_), channel_id=1, source_target_pairs={{0,6},{2,4},{4,2},{6,0},{1,7},{3,5},{5,3},{7,1},{8,14},{10,12},{12... | collective-permute-start | bytes 12296 | tf_op jit(solution)/shard_map/ppermute | solution.py:30
  13.1 0.0 collective-permute-done.refs_0_
  13.1 0.8 %collective-permute-start.6 = (f32[8,128]{1,0:T(8,128)S(1)}, f32[8,128]{1,0:T(8,128)S(1)}, u32[]{:S(2)}, u32[]{:S(2)}) collective-permute-start(f32[8,128]{1,0:T(8,128)S(1)} %column.1.refs_4_), channel_id=1, source_target_pairs={{0,4},{2,6},{4,0},{6,2},{1,5},{3,7},{5,1},{7,3},{8,12},{10,14},{12... | collective-permute-start | bytes 12296 | tf_op jit(solution)/shard_map/ppermute | solution.py:30
  13.9 0.0 collective-permute-done.1.refs_1_
  13.9 2.2 %collective-permute-start.5 = (f32[8,128]{1,0:T(8,128)S(1)}, f32[8,128]{1,0:T(8,128)S(1)}, u32[]{:S(2)}, u32[]{:S(2)}) collective-permute-start(f32[8,128]{1,0:T(8,128)S(1)} %column.1.refs_4_), channel_id=1, source_target_pairs={{0,2},{2,0},{4,6},{6,4},{1,3},{3,1},{5,7},{7,5},{8,10},{10,8},{12,... | collective-permute-start | bytes 12296 | tf_op jit(solution)/shard_map/ppermute | solution.py:30
  16.1 0.0 collective-permute-done.2.refs_2_
  16.1 0.0 collective-permute-done.3.refs_3_
  16.1 1.6 %q.1 = (f32[33,8,128]{2,1,0:T(8,128)S(1)}, f32[33,8,128]{2,1,0:T(8,128)S(1)}, f32[33,8,128]{2,1,0:T(8,128)S(1)}, f32[33,8,128]{2,1,0:T(8,128)S(1)}) custom-call(f32[3,32,32,128]{3,2,1,0:T(8,128)S(1)} %copy-done, f32[3,32,128]{2,1,0:T(8,128)S(1)} %collective-permute-done.refs_0_, f32[3,32,128]{2,1,0:T(8,128)S(1)} %collective-permute-done.1.refs_1_, ...), custom_call_target="tpu_custom_call" | custom-call | tf_op jit(solution)/shard_map/q/pallas_call | solution.py:416
  17.7 0.0 collective-permute-done.7.refs_7_
  17.7 0.0 collective-permute-done.6.refs_6_
  17.8 1.6 %collective-permute-start.8 = (f32[33,8,128]{2,1,0:T(8,128)S(1)}, f32[33,8,128]{2,1,0:T(8,128)S(1)}, u32[]{:S(2)}, u32[]{:S(2)}) collective-permute-start(f32[33,8,128]{2,1,0:T(8,128)S(1)} %get-tuple-element.30), channel_id=1, source_target_pairs={{0,8},{8,0},{16,24},{24,16},{1,9},{9,1},{17,25},{25,17},{2,10},{10... | collective-permute-start | bytes 405512 | tf_op jit(solution)/shard_map/ppermute | solution.py:30
  19.3 0.5 %collective-permute-start.9 = (f32[33,8,128]{2,1,0:T(8,128)S(1)}, f32[33,8,128]{2,1,0:T(8,128)S(1)}, u32[]{:S(2)}, u32[]{:S(2)}) collective-permute-start(f32[33,8,128]{2,1,0:T(8,128)S(1)} %get-tuple-element.31), channel_id=1, source_target_pairs={{0,16},{8,24},{16,0},{24,8},{1,17},{9,25},{17,1},{25,9},{2,18},{10... | collective-permute-start | bytes 405512 | tf_op jit(solution)/shard_map/ppermute | solution.py:30
  19.8 1.5 %collective-permute-start.10 = (f32[33,8,128]{2,1,0:T(8,128)S(1)}, f32[33,8,128]{2,1,0:T(8,128)S(1)}, u32[]{:S(2)}, u32[]{:S(2)}) collective-permute-start(f32[33,8,128]{2,1,0:T(8,128)S(1)} %get-tuple-element.32), channel_id=1, source_target_pairs={{0,24},{8,16},{16,8},{24,0},{1,25},{9,17},{17,9},{25,1},{2,26},{10... | collective-permute-start | bytes 405512 | tf_op jit(solution)/shard_map/ppermute | solution.py:30
  21.3 2.2 %collective-permute-done.8.refs_1_ = f32[33,8,128]{2,1,0:T(8,128)S(1)} collective-permute-done((f32[33,8,128]{2,1,0:T(8,128)S(1)}, f32[33,8,128]{2,1,0:T(8,128)S(1)}, u32[]{:S(2)}, u32[]{:S(2)}) %collective-permute-start.8) | collective-permute-done | bytes 135200 | tf_op jit(solution)/shard_map/ppermute | solution.py:30
  23.5 3.3 %collective-permute-done.9.refs_2_ = f32[33,8,128]{2,1,0:T(8,128)S(1)} collective-permute-done((f32[33,8,128]{2,1,0:T(8,128)S(1)}, f32[33,8,128]{2,1,0:T(8,128)S(1)}, u32[]{:S(2)}, u32[]{:S(2)}) %collective-permute-start.9) | collective-permute-done | bytes 135200 | tf_op jit(solution)/shard_map/ppermute | solution.py:30
  26.8 6.5 %render.1.refs_0_ = f32[8,4,8,128]{3,2,1,0:T(8,128)S(1)} custom-call(f32[33,8,128]{2,1,0:T(8,128)S(1)} %get-tuple-element.29.refs_0_, f32[33,8,128]{2,1,0:T(8,128)S(1)} %collective-permute-done.8.refs_1_, f32[33,8,128]{2,1,0:T(8,128)S(1)} %collective-permute-done.9.refs_2_, f32[33,8,128]{2,1,0:T(8,128)S(1)} %collective-permute-done.10.refs_3_, ...), custom_call_target="tpu_custom_call" | custom-call | tf_op jit(solution)/shard_map/render/pallas_call | solution.py:441
  33.3 1.2 %collective-permute-start.13 = (f32[8,4,8,128]{3,2,1,0:T(8,128)S(1)}, f32[8,4,8,128]{3,2,1,0:T(8,128)S(1)}, u32[]{:S(2)}, u32[]{:S(2)}) collective-permute-start(f32[8,4,8,128]{3,2,1,0:T(8,128)S(1)} %render.1.refs_0_), channel_id=1, source_target_pairs={{0,24},{8,16},{16,8},{24,0},{1,25},{9,17},{17,9},{25,1},{2,26},{10... | collective-permute-start | bytes 393224 | tf_op jit(solution)/shard_map/ppermute | solution.py:30
  34.5 0.8 %collective-permute-start.12 = (f32[8,4,8,128]{3,2,1,0:T(8,128)S(1)}, f32[8,4,8,128]{3,2,1,0:T(8,128)S(1)}, u32[]{:S(2)}, u32[]{:S(2)}) collective-permute-start(f32[8,4,8,128]{3,2,1,0:T(8,128)S(1)} %render.1.refs_0_), channel_id=1, source_target_pairs={{0,16},{8,24},{16,0},{24,8},{1,17},{9,25},{17,1},{25,9},{2,18},{10... | collective-permute-start | bytes 393224 | tf_op jit(solution)/shard_map/ppermute | solution.py:30
  35.3 1.6 %collective-permute-start.11 = (f32[8,4,8,128]{3,2,1,0:T(8,128)S(1)}, f32[8,4,8,128]{3,2,1,0:T(8,128)S(1)}, u32[]{:S(2)}, u32[]{:S(2)}) collective-permute-start(f32[8,4,8,128]{3,2,1,0:T(8,128)S(1)} %render.1.refs_0_), channel_id=1, source_target_pairs={{0,8},{8,0},{16,24},{24,16},{1,9},{9,1},{17,25},{25,17},{2,10},{10... | collective-permute-start | bytes 393224 | tf_op jit(solution)/shard_map/ppermute | solution.py:30
  36.9 2.5 %collective-permute-done.13.refs_3_ = f32[8,4,8,128]{3,2,1,0:T(8,128)S(1)} collective-permute-done((f32[8,4,8,128]{3,2,1,0:T(8,128)S(1)}, f32[8,4,8,128]{3,2,1,0:T(8,128)S(1)}, u32[]{:S(2)}, u32[]{:S(2)}) %collective-permute-start.13) | collective-permute-done | bytes 131104 | tf_op jit(solution)/shard_map/ppermute | solution.py:30
  39.4 1.3 %collective-permute-done.12.refs_2_ = f32[8,4,8,128]{3,2,1,0:T(8,128)S(1)} collective-permute-done((f32[8,4,8,128]{3,2,1,0:T(8,128)S(1)}, f32[8,4,8,128]{3,2,1,0:T(8,128)S(1)}, u32[]{:S(2)}, u32[]{:S(2)}) %collective-permute-start.12) | collective-permute-done | bytes 131104 | tf_op jit(solution)/shard_map/ppermute | solution.py:30
  40.7 0.8 %assemble.1 = f32[8,4,32,128]{3,2,1,0:T(8,128)} custom-call(f32[8,4,8,128]{3,2,1,0:T(8,128)S(1)} %render.1.refs_0_, f32[8,4,8,128]{3,2,1,0:T(8,128)S(1)} %collective-permute-done.11.refs_1_, f32[8,4,8,128]{3,2,1,0:T(8,128)S(1)} %collective-permute-done.12.refs_2_, f32[8,4,8,128]{3,2,1,0:T(8,128)S(1)} %collective-permute-done.13.refs_3_), custom_call_target="tpu_custom_call" | custom-call | tf_op jit(solution)/shard_map/assemble/pallas_call | solution.py:460
  (9 shorter events, 0.0 us)
Async XLA Ops:
  0.0 10.0 %copy-start = (f32[3,32,32,128]{3,2,1,0:T(8,128)S(1)}, f32[3,32,32,128]{3,2,1,0:T(8,128)}, u32[]{:S(2)}) copy-start(f32[3,32,32,128]{3,2,1,0:T(8,128)} %v_hbm.3) | copy-start | bytes 4718596
  1.4 11.7 %collective-permute-start = (f32[3,32,128]{2,1,0:T(8,128)S(1)}, f32[3,32,128]{2,1,0:T(8,128)S(1)}, u32[]{:S(2)}, u32[]{:S(2)}) collective-permute-start(f32[3,32,128]{2,1,0:T(8,128)S(1)} %get-tuple-element.19), channel_id=1, source_target_pairs={{0,8},{8,0},{16,24},{24,16},{1,9},{9,1},{17,25},{25,17},{2,10},{10... | collective-permute-start | bytes 147464 | tf_op jit(solution)/shard_map/ppermute | solution.py:30
  4.4 9.5 %collective-permute-start.1 = (f32[3,32,128]{2,1,0:T(8,128)S(1)}, f32[3,32,128]{2,1,0:T(8,128)S(1)}, u32[]{:S(2)}, u32[]{:S(2)}) collective-permute-start(f32[3,32,128]{2,1,0:T(8,128)S(1)} %get-tuple-element.20), channel_id=1, source_target_pairs={{0,24},{8,16},{16,8},{24,0},{1,25},{9,17},{17,9},{25,1},{2,26},{10... | collective-permute-start | bytes 147464 | tf_op jit(solution)/shard_map/ppermute | solution.py:35
  5.9 10.2 %collective-permute-start.2 = (f32[3,32,128]{2,1,0:T(8,128)S(1)}, f32[3,32,128]{2,1,0:T(8,128)S(1)}, u32[]{:S(2)}, u32[]{:S(2)}) collective-permute-start(f32[3,32,128]{2,1,0:T(8,128)S(1)} %get-tuple-element.21), channel_id=1, source_target_pairs={{0,2},{2,0},{4,6},{6,4},{1,3},{3,1},{5,7},{7,5},{8,10},{10,8},{12,... | collective-permute-start | bytes 147464 | tf_op jit(solution)/shard_map/ppermute | solution.py:30
  7.5 8.6 %collective-permute-start.3 = (f32[3,32,128]{2,1,0:T(8,128)S(1)}, f32[3,32,128]{2,1,0:T(8,128)S(1)}, u32[]{:S(2)}, u32[]{:S(2)}) collective-permute-start(f32[3,32,128]{2,1,0:T(8,128)S(1)} %get-tuple-element.22), channel_id=1, source_target_pairs={{0,6},{2,4},{4,2},{6,0},{1,7},{3,5},{5,3},{7,1},{8,14},{10,12},{12... | collective-permute-start | bytes 147464 | tf_op jit(solution)/shard_map/ppermute | solution.py:35
  10.5 16.4 %copy-start.1 = (f32[8,4,128]{2,1,0:T(4,128)S(1)}, f32[8,4,128]{2,1,0:T(4,128)}, u32[]{:S(2)}) copy-start(f32[8,4,128]{2,1,0:T(4,128)} %param.5) | copy-start | bytes 49156
  10.5 16.4 %copy-start.2 = (s32[8]{0:T(128)S(1)}, s32[8]{0:T(128)}, u32[]{:S(2)}) copy-start(s32[8]{0:T(128)} %refs_4_.1) | copy-start | bytes 100
  10.5 1.2 %collective-permute-start.4 = (f32[4,8,128]{2,1,0:T(8,128)S(1)}, f32[4,8,128]{2,1,0:T(8,128)S(1)}, u32[]{:S(2)}, u32[]{:S(2)}) collective-permute-start(f32[4,8,128]{2,1,0:T(8,128)S(1)} %get-tuple-element.23), channel_id=1, source_target_pairs={{0,1},{1,0},{2,3},{3,2},{4,5},{5,4},{6,7},{7,6},{8,9},{9,8},{10,11... | collective-permute-start | bytes 49160 | tf_op jit(solution)/shard_map/ppermute | solution.py:30
  11.7 6.0 %collective-permute-start.7 = (f32[8,128]{1,0:T(8,128)S(1)}, f32[8,128]{1,0:T(8,128)S(1)}, u32[]{:S(2)}, u32[]{:S(2)}) collective-permute-start(f32[8,128]{1,0:T(8,128)S(1)} %column.1.refs_4_), channel_id=1, source_target_pairs={{0,6},{2,4},{4,2},{6,0},{1,7},{3,5},{5,3},{7,1},{8,14},{10,12},{12... | collective-permute-start | bytes 12296 | tf_op jit(solution)/shard_map/ppermute | solution.py:30
  13.1 4.6 %collective-permute-start.6 = (f32[8,128]{1,0:T(8,128)S(1)}, f32[8,128]{1,0:T(8,128)S(1)}, u32[]{:S(2)}, u32[]{:S(2)}) collective-permute-start(f32[8,128]{1,0:T(8,128)S(1)} %column.1.refs_4_), channel_id=1, source_target_pairs={{0,4},{2,6},{4,0},{6,2},{1,5},{3,7},{5,1},{7,3},{8,12},{10,14},{12... | collective-permute-start | bytes 12296 | tf_op jit(solution)/shard_map/ppermute | solution.py:30
  13.9 3.8 %collective-permute-start.5 = (f32[8,128]{1,0:T(8,128)S(1)}, f32[8,128]{1,0:T(8,128)S(1)}, u32[]{:S(2)}, u32[]{:S(2)}) collective-permute-start(f32[8,128]{1,0:T(8,128)S(1)} %column.1.refs_4_), channel_id=1, source_target_pairs={{0,2},{2,0},{4,6},{6,4},{1,3},{3,1},{5,7},{7,5},{8,10},{10,8},{12,... | collective-permute-start | bytes 12296 | tf_op jit(solution)/shard_map/ppermute | solution.py:30
  17.8 5.8 %collective-permute-start.8 = (f32[33,8,128]{2,1,0:T(8,128)S(1)}, f32[33,8,128]{2,1,0:T(8,128)S(1)}, u32[]{:S(2)}, u32[]{:S(2)}) collective-permute-start(f32[33,8,128]{2,1,0:T(8,128)S(1)} %get-tuple-element.30), channel_id=1, source_target_pairs={{0,8},{8,0},{16,24},{24,16},{1,9},{9,1},{17,25},{25,17},{2,10},{10... | collective-permute-start | bytes 405512 | tf_op jit(solution)/shard_map/ppermute | solution.py:30
  19.3 7.5 %collective-permute-start.9 = (f32[33,8,128]{2,1,0:T(8,128)S(1)}, f32[33,8,128]{2,1,0:T(8,128)S(1)}, u32[]{:S(2)}, u32[]{:S(2)}) collective-permute-start(f32[33,8,128]{2,1,0:T(8,128)S(1)} %get-tuple-element.31), channel_id=1, source_target_pairs={{0,16},{8,24},{16,0},{24,8},{1,17},{9,25},{17,1},{25,9},{2,18},{10... | collective-permute-start | bytes 405512 | tf_op jit(solution)/shard_map/ppermute | solution.py:30
  19.8 7.0 %collective-permute-start.10 = (f32[33,8,128]{2,1,0:T(8,128)S(1)}, f32[33,8,128]{2,1,0:T(8,128)S(1)}, u32[]{:S(2)}, u32[]{:S(2)}) collective-permute-start(f32[33,8,128]{2,1,0:T(8,128)S(1)} %get-tuple-element.32), channel_id=1, source_target_pairs={{0,24},{8,16},{16,8},{24,0},{1,25},{9,17},{17,9},{25,1},{2,26},{10... | collective-permute-start | bytes 405512 | tf_op jit(solution)/shard_map/ppermute | solution.py:30
  33.3 6.0 %collective-permute-start.13 = (f32[8,4,8,128]{3,2,1,0:T(8,128)S(1)}, f32[8,4,8,128]{3,2,1,0:T(8,128)S(1)}, u32[]{:S(2)}, u32[]{:S(2)}) collective-permute-start(f32[8,4,8,128]{3,2,1,0:T(8,128)S(1)} %render.1.refs_0_), channel_id=1, source_target_pairs={{0,24},{8,16},{16,8},{24,0},{1,25},{9,17},{17,9},{25,1},{2,26},{10... | collective-permute-start | bytes 393224 | tf_op jit(solution)/shard_map/ppermute | solution.py:30
  34.5 6.2 %collective-permute-start.12 = (f32[8,4,8,128]{3,2,1,0:T(8,128)S(1)}, f32[8,4,8,128]{3,2,1,0:T(8,128)S(1)}, u32[]{:S(2)}, u32[]{:S(2)}) collective-permute-start(f32[8,4,8,128]{3,2,1,0:T(8,128)S(1)} %render.1.refs_0_), channel_id=1, source_target_pairs={{0,16},{8,24},{16,0},{24,8},{1,17},{9,25},{17,1},{25,9},{2,18},{10... | collective-permute-start | bytes 393224 | tf_op jit(solution)/shard_map/ppermute | solution.py:30
  35.3 5.4 %collective-permute-start.11 = (f32[8,4,8,128]{3,2,1,0:T(8,128)S(1)}, f32[8,4,8,128]{3,2,1,0:T(8,128)S(1)}, u32[]{:S(2)}, u32[]{:S(2)}) collective-permute-start(f32[8,4,8,128]{3,2,1,0:T(8,128)S(1)} %render.1.refs_0_), channel_id=1, source_target_pairs={{0,8},{8,0},{16,24},{24,16},{1,9},{9,1},{17,25},{25,17},{2,10},{10... | collective-permute-start | bytes 393224 | tf_op jit(solution)/shard_map/ppermute | solution.py:30
